TPU v7x, 1024 devices: a whole 4x8x16 slice. The times are simulated.
1024 devices in a mesh: tm: 16 (over y, core), space: 16 (over z), dp: 4 (over x).
Axes of the slice: x: 4, y: 8, z: 16, core: 2. Of those that a mesh axis runs over, the one named last changes fastest.
Arguments:
- latents: bfloat16 [4, 4096, 2048], P('dp', 'tm'), may hold values from -6 to 6
- proj_input: bfloat16 [2048, 128], replicated, may hold values from -0.125 to 0.125
- proj_output: bfloat16 [2048, 128], replicated, may hold values from -0.125 to 0.125
- scan_input: bfloat16 [4, 4096, 4096], P('dp', 'tm', 'space'), may hold values from -6 to 6
- log_decay: float32 [4, 4096, 32], P('dp', 'tm', 'space'), may hold values from -2 to 0
- att_queries: bfloat16 [4, 4096, 4096], P('dp', 'tm', 'space'), may hold values from -67.88225 to 67.88225
- att_keys: bfloat16 [4, 4096, 4096], P('dp', 'tm', 'space'), may hold values from -3 to 3
- att_values: bfloat16 [4, 4096, 4096], P('dp', 'tm', 'space'), may hold values from -6 to 6
- scan_cotangent: bfloat16 [4, 4096, 4096], P('dp', 'tm', 'space'), may hold values from -0.59765625 to 0.59765625
- window_offsets: int32 [4, 32], P('dp', 'tm'), may hold values from 0 to 63
Outputs:
- layer_out: bfloat16 [4, 4096, 4096], P('dp', 'tm', 'space')
- input_grad: bfloat16 [4, 4096, 4096], P('dp', 'tm', 'space')
- proj_grad: float32 [2048, 256], P('space')
All inputs are finite; a program needn't handle non-finite values.
Results may differ from a plain program's by a relative error of at most 0.027.
Values may be sent and summed in bfloat16 or wider, within the bound.
No kernel may reach another device: no remote copies, remote signals or barrier semaphores. Data moves between devices by JAX's collectives and lax.ppermute only.
A program may use at most 32 MiB of HBM per device.

v0:
```python
import math

import jax
import jax.numpy as jnp
from jax import lax
from jax.sharding import PartitionSpec as P

W = 128
QB = 128


precise = lax.Precision.HIGHEST


def shifted(block, axis, distance):
    devices = range(lax.axis_size(axis))
    route = [(i - distance, i) for i in devices if i - distance in devices]
    return lax.ppermute(block, axis, route)


def block_decay(cum_decay):
    row_count = cum_decay.shape[1]
    position = jnp.arange(row_count)
    lower_mask = position[:, None] >= position[None, :]
    per_head_split = jnp.swapaxes(cum_decay, 1, 2)
    log_gap = per_head_split[:, :, :, None] - per_head_split[:, :, None, :]
    return jnp.exp(jnp.where(lower_mask, log_gap, -jnp.inf))


def on_device(
    latents,
    proj_input,
    proj_output,
    scan_input,
    log_decay,
    att_queries,
    att_keys,
    att_values,
    scan_cotangent,
    window_offsets,
):
    clip_count, row_count, model_width = latents.shape
    head_count = log_decay.shape[2]
    head_dim = scan_input.shape[2] // head_count
    state_count = proj_input.shape[1]
    state_scale = 1.0 / math.sqrt(state_count)
    b_rows = jnp.einsum(
        "crd,dn->crn", latents, proj_input, preferred_element_type=jnp.float32
    ).astype(jnp.bfloat16)
    c_rows = jnp.einsum(
        "crd,dn->crn", latents, proj_output, preferred_element_type=jnp.float32
    ).astype(jnp.bfloat16)
    cum_decay = jnp.cumsum(log_decay, axis=1)
    block_total = cum_decay[:, -1]
    head_rise = jnp.exp(cum_decay)
    tail_fall = jnp.exp(block_total[:, None] - cum_decay)
    decay_mat = block_decay(cum_decay)
    kernel = (
        jnp.einsum("ctn,csn->cts", c_rows, b_rows, preferred_element_type=jnp.float32) * state_scale
    )
    mixing = (kernel[:, None] * decay_mat).astype(jnp.bfloat16)
    scan_heads = scan_input.reshape(clip_count, row_count, head_count, head_dim)
    cotan_heads = scan_cotangent.reshape(clip_count, row_count, head_count, head_dim)
    scan_wide = scan_heads.astype(jnp.float32)
    cotan_wide = cotan_heads.astype(jnp.float32)
    b_wide = b_rows.astype(jnp.float32)
    c_wide = c_rows.astype(jnp.float32) * state_scale
    fresh = jnp.einsum(
        "cshp,csn->chpn", scan_wide * tail_fall[..., None], b_wide, precision=precise
    )
    back_fresh = jnp.einsum(
        "cthp,ctn->chpn", cotan_wide * head_rise[..., None], c_wide, precision=precise
    )
    carried = jnp.exp(block_total)

    def forward_step(counter, state):
        return shifted(
            (carried[..., None, None] * state + fresh).astype(jnp.bfloat16), "tm", 1
        ).astype(jnp.float32)

    def reverse_pass_step(counter, state):
        return shifted(
            (carried[..., None, None] * state + back_fresh).astype(jnp.bfloat16), "tm", -1
        ).astype(jnp.float32)

    state_in = lax.fori_loop(0, lax.axis_size("tm") - 1, forward_step, jnp.zeros_like(fresh))
    grad_in = lax.fori_loop(
        0, lax.axis_size("tm") - 1, reverse_pass_step, jnp.zeros_like(back_fresh)
    )
    tails = shifted((att_keys[:, row_count - W :], att_values[:, row_count - W :]), "tm", 1)
    inner = jnp.einsum("chts,cshp->cthp", mixing, scan_heads, preferred_element_type=jnp.float32)
    scan_out = inner + head_rise[..., None] * jnp.einsum(
        "ctn,chpn->cthp", c_wide, state_in, precision=precise
    )
    normed = scan_out * lax.rsqrt(jnp.mean(scan_out * scan_out, axis=-1, keepdims=True) + 1e-05)
    key_ext = jnp.concatenate([tails[0], att_keys], axis=1).reshape(
        clip_count, W + row_count, head_count, head_dim
    )
    value_ext = jnp.concatenate([tails[1], att_values], axis=1).reshape(
        clip_count, W + row_count, head_count, head_dim
    )
    query_heads = att_queries.reshape(clip_count, row_count, head_count, head_dim)
    start = lax.axis_index("tm") * row_count
    t_pos = start + jnp.arange(row_count)
    s_pos = start - W + jnp.arange(W + row_count)
    offset_each = jnp.repeat(window_offsets, QB, axis=1)
    seen = (
        (s_pos[None, None, :] <= t_pos[None, :, None])
        & (s_pos[None, None, :] >= t_pos[None, :, None] - W + 1 + offset_each[:, :, None])
        & (s_pos[None, None, :] >= 0)
    )
    scores = jnp.einsum(
        "cthp,cshp->chts", query_heads, key_ext, preferred_element_type=jnp.float32
    ) / math.sqrt(head_dim)
    scores = jnp.where(seen[:, None], scores, -jnp.inf)
    highest = jnp.max(scores, axis=-1, keepdims=True)
    expo = jnp.exp(scores - highest)
    probs = (expo / jnp.sum(expo, axis=-1, keepdims=True)).astype(jnp.bfloat16)
    attended = jnp.einsum("chts,cshp->cthp", probs, value_ext, preferred_element_type=jnp.float32)
    layer_out = (
        (normed + attended)
        .reshape(clip_count, row_count, head_count * head_dim)
        .astype(jnp.bfloat16)
    )
    grad_x = jnp.einsum("chts,cthp->cshp", mixing, cotan_heads, preferred_element_type=jnp.float32)
    grad_x = grad_x + tail_fall[..., None] * jnp.einsum(
        "chpn,csn->cshp", grad_in, b_wide, precision=precise
    )
    input_grad = grad_x.reshape(clip_count, row_count, head_count * head_dim).astype(jnp.bfloat16)
    product = jnp.einsum(
        "cthp,cshp->chts", cotan_heads, scan_heads, preferred_element_type=jnp.float32
    )
    weigh = (product * decay_mat * state_scale).astype(jnp.bfloat16)
    grad_b = jnp.einsum("chts,ctn->chsn", weigh, c_rows, preferred_element_type=jnp.float32)
    grad_b = grad_b + jnp.swapaxes(tail_fall, 1, 2)[..., None] * jnp.einsum(
        "cshp,chpn->chsn", scan_wide, grad_in, precision=precise
    )
    gradient_readout = jnp.einsum(
        "chts,csn->chtn", weigh, b_rows, preferred_element_type=jnp.float32
    )
    gradient_readout = gradient_readout + jnp.swapaxes(head_rise, 1, 2)[
        ..., None
    ] * state_scale * jnp.einsum("cthp,chpn->chtn", cotan_wide, state_in, precision=precise)
    both = jnp.concatenate([grad_b, gradient_readout], axis=-1).astype(jnp.bfloat16)
    share_rows = model_width // lax.axis_size("space")
    term = jnp.zeros((lax.axis_size("space") * share_rows, 2 * state_count), jnp.float32)
    for head in range(head_count):
        term = term + jnp.einsum(
            "crd,crn->dn", latents, both[:, head], preferred_element_type=jnp.float32
        )
    share = lax.psum_scatter(
        term.astype(jnp.bfloat16), "space", scatter_dimension=0, tiled=True
    ).astype(jnp.float32)
    summed = lax.psum(share, ("tm", "dp"))
    proj_grad = summed / math.sqrt(
        clip_count * lax.axis_size("dp") * row_count * lax.axis_size("tm")
    )
    return (layer_out, input_grad, proj_grad)


def solution(mesh):
    return jax.shard_map(
        on_device,
        mesh=mesh,
        in_specs=(
            P("dp", "tm", None),
            P(),
            P(),
            P("dp", "tm", "space"),
            P("dp", "tm", "space"),
            P("dp", "tm", "space"),
            P("dp", "tm", "space"),
            P("dp", "tm", "space"),
            P("dp", "tm", "space"),
            P("dp", "tm"),
        ),
        out_specs=(P("dp", "tm", "space"), P("dp", "tm", "space"), P("space", None)),
        check_vma=False,
    )
```

profile of v0, /device:TPU:1, one launch (start us, length us, event | category | flops | bytes accessed | tf_op | source)
XLA Modules:
  0.0 564.0 jit_solution(15033835768672801537)
XLA Ops:
  8.2 4.7 collective-permute-start.2
  14.0 1.9 collective-permute-start.3
  17.9 1.5 convolution_convert_fusion
  23.0 91.1 %while.22 = (s32[]{:T(128)}, f32[1,2,128,128]{3,2,1,0:T(8,128)S(1)}, f32[1,2]{1,0:T(1,128)S(1)}, f32[1,2,128,128]{3,2,1,0:T(8,128)S(1)}, s32[]{:T(128)}, /*index=5*/s32[]{:T(128)}) while((s32[]{:T(128)}, f32[1,2,128,128]{3,2,1,0:T(8,128)S(1)}, f32[1,2]{1,0:T(1,128)S(1)}, f32[1,2,128,128]{3,2,1,0:T(8,128)S(1)}, s32[]{:T(128)}, ...), condition=%wide.region_3.4_spmd.clone, body=%wide.region_2.3_spmd.clone.sunk | while | flops 163843 | bytes 786559 | solution.py:86
  23.1 3.6 collective-permute-start
  26.7 9.9 %collective-permute-done = bf16[1,2,128,128]{3,2,1,0:T(8,128)(2,1)S(1)} collective-permute-done((bf16[1,2,128,128]{3,2,1,0:T(8,128)(2,1)S(1)}, bf16[1,2,128,128]{3,2,1,0:T(8,128)(2,1)S(1)}, u32[]{:S(2)}, u32[]{:S(2)}) %collective-permute-start) | collective-permute-done | bytes 65568 | tf_op jit(solution)/shard_map/while/body/eval_jaxpr/ppermute | solution.py:18
  36.7 1.9 collective-permute-start
  38.6 1.3 collective-permute-done
  40.0 4.3 collective-permute-start
  44.3 1.3 collective-permute-done
  45.7 4.3 collective-permute-start
  50.0 1.3 collective-permute-done
  51.4 4.3 collective-permute-start
  55.7 1.3 collective-permute-done
  57.1 4.3 collective-permute-start
  61.4 1.3 collective-permute-done
  62.8 4.3 collective-permute-start
  67.1 1.3 collective-permute-done
  68.5 4.3 collective-permute-start
  72.8 1.3 collective-permute-done
  74.2 4.3 collective-permute-start
  78.5 1.3 collective-permute-done
  80.0 4.3 collective-permute-start
  84.2 1.3 collective-permute-done
  85.7 4.3 collective-permute-start
  89.9 1.3 collective-permute-done
  91.4 4.3 collective-permute-start
  97.1 4.3 collective-permute-start
  102.8 4.3 collective-permute-start
  108.5 4.3 collective-permute-start
  114.4 99.2 %while.23 = (s32[]{:T(128)}, f32[1,2,128,128]{3,2,1,0:T(8,128)S(1)}, f32[1,2]{1,0:T(1,128)S(1)}, f32[1,2,128,128]{3,2,1,0:T(8,128)S(1)}, s32[]{:T(128)}, /*index=5*/s32[]{:T(128)}) while((s32[]{:T(128)}, f32[1,2,128,128]{3,2,1,0:T(8,128)S(1)}, f32[1,2]{1,0:T(1,128)S(1)}, f32[1,2,128,128]{3,2,1,0:T(8,128)S(1)}, s32[]{:T(128)}, ...), condition=%wide.region_8.9_spmd.clone, body=%wide.region_7.8_spmd.clone.sunk | while | flops 163843 | bytes 786559 | solution.py:87
  114.5 1.9 collective-permute-start.1
  116.5 4.3 collective-permute-done.1
  120.9 1.9 collective-permute-start.1
  122.8 3.7 collective-permute-done.1
  126.6 1.9 collective-permute-start.1
  128.5 3.7 collective-permute-done.1
  132.3 1.9 collective-permute-start.1
  134.2 3.7 collective-permute-done.1
  138.0 1.9 collective-permute-start.1
  139.9 4.1 collective-permute-done.1
  144.1 1.9 collective-permute-start.1
  146.1 4.7 collective-permute-done.1
  150.9 1.9 collective-permute-start.1
  152.8 5.5 collective-permute-done.1
  158.4 1.9 collective-permute-start.1
  160.4 4.9 collective-permute-done.1
  165.4 1.9 collective-permute-start.1
  167.3 4.9 collective-permute-done.1
  172.3 1.9 collective-permute-start.1
  174.2 4.9 collective-permute-done.1
  179.2 1.9 collective-permute-start.1
  181.1 4.9 collective-permute-done.1
  186.1 1.9 collective-permute-start.1
  188.0 4.9 collective-permute-done.1
  193.0 1.9 collective-permute-start.1
  195.0 4.9 collective-permute-done.1
  199.9 1.9 collective-permute-start.1
  201.9 4.9 collective-permute-done.1
  206.9 1.9 collective-permute-start.1
  208.8 4.9 collective-permute-done.1
  215.0 1.3 copy.106
  223.7 77.9 %reduce-scatter.4.cloned.1.call-done = bf16[128,256]{1,0:T(8,128)(2,1)} async-done(((bf16[2048,256]{1,0:T(8,128)(2,1)}), bf16[128,256]{1,0:T(8,128)(2,1)}) %reduce-scatter.4.cloned.1.call-update) | async-done | bytes 65552
  302.6 253.9 %all-reduce.1 = f32[128,256]{0,1:T(8,128)S(1)} all-reduce(bf16[128,256]{0,1:T(8,128)(2,1)S(1)} %copy.107), channel_id=1, replica_groups=mesh['tm'=16,'space'=16,'dp'=4] {'tm','dp'}, use_global_device_ids=true, to_apply=%region_10.11 | all-reduce | flops 32768 | bytes 196608 | tf_op jit(solution)/shard_map/psum | solution.py:154
  (156 shorter events, 26.1 us)
Async XLA Ops:
  7.2 10.7 %copy-start = (bf16[1,256,2048]{2,1,0:T(8,128)(2,1)S(1)}, bf16[1,256,2048]{2,1,0:T(8,128)(2,1)}, u32[]{:S(2)}) copy-start(bf16[1,256,2048]{2,1,0:T(8,128)(2,1)} %param.14) | copy-start | bytes 3145732
  7.2 12.1 %copy-start.1 = (bf16[2048,128]{1,0:T(8,128)(2,1)S(1)}, bf16[2048,128]{1,0:T(8,128)(2,1)}, u32[]{:S(2)}) copy-start(bf16[2048,128]{1,0:T(8,128)(2,1)} %param.16) | copy-start | bytes 1572868
  7.2 12.6 %copy-start.2 = (bf16[1,256,256]{2,1,0:T(8,128)(2,1)S(1)}, bf16[1,256,256]{2,1,0:T(8,128)(2,1)}, u32[]{:S(2)}) copy-start(bf16[1,256,256]{2,1,0:T(8,128)(2,1)} %param.17) | copy-start | bytes 393220
  7.2 294.4 %reduce-scatter.4.cloned.1.call-start = ((), (), s32[]{:S(2)}) async-start(), calls=%async_computation.1 | async-start | bytes 1114112
  8.2 11.6 %copy-start.3 = (bf16[1,256,256]{2,1,0:T(8,128)(2,1)S(1)}, bf16[1,256,256]{2,1,0:T(8,128)(2,1)}, u32[]{:S(2)}) copy-start(bf16[1,256,256]{2,1,0:T(8,128)(2,1)} %param.22) | copy-start | bytes 393220
  8.2 211.7 %collective-permute-start.2 = (bf16[1,128,256]{2,1,0:T(8,128)(2,1)S(1)}, bf16[1,128,256]{2,1,0:T(8,128)(2,1)}, u32[]{:S(2)}, u32[]{:S(2)}) collective-permute-start(bf16[1,128,256]{2,1,0:T(8,128)(2,1)S(1)} %slice.24), channel_id=1, source_target_pairs={{0,64},{64,128},{128,192},{192,256},{256,320},{320,384},{384,448},... | collective-permute-start | bytes 196616 | tf_op jit(solution)/shard_map/ppermute | solution.py:18
  14.0 207.0 %collective-permute-start.3 = (bf16[1,128,256]{1,2,0:T(8,128)(2,1)S(1)}, bf16[1,128,256]{1,2,0:T(8,128)(2,1)}, u32[]{:S(2)}, u32[]{:S(2)}) collective-permute-start(bf16[1,128,256]{1,2,0:T(8,128)(2,1)S(1)} %slice.30), channel_id=1, source_target_pairs={{0,64},{64,128},{128,192},{192,256},{256,320},{320,384},{384,448},... | collective-permute-start | bytes 196616 | tf_op jit(solution)/shard_map/ppermute | solution.py:18
  15.9 5.0 copy-start.6
  20.6 0.6 copy-start.9
  22.4 91.7 %copy-start.8 = (f32[2,256]{1,0:T(2,128)S(1)}, f32[2,256]{1,0:T(2,128)}, u32[]{:S(2)}) copy-start(f32[2,256]{1,0:T(2,128)} %get-tuple-element.104) | copy-start | bytes 6148
  23.1 13.5 %collective-permute-start = (bf16[1,2,128,128]{3,2,1,0:T(8,128)(2,1)S(1)}, bf16[1,2,128,128]{3,2,1,0:T(8,128)(2,1)S(1)}, u32[]{:S(2)}, u32[]{:S(2)}) collective-permute-start(bf16[1,2,128,128]{3,2,1,0:T(8,128)(2,1)S(1)} %fusion.99), channel_id=1, source_target_pairs={{0,64},{64,128},{128,192},{192,256},{256,320},{320,384},{384,448},... | collective-permute-start | bytes 196616 | tf_op jit(solution)/shard_map/while/body/eval_jaxpr/ppermute | solution.py:18
  36.7 3.2 collective-permute-start
  40.0 5.6 collective-permute-start
  45.7 5.6 collective-permute-start
  51.4 5.6 collective-permute-start
  57.1 5.6 collective-permute-start
  62.8 5.6 collective-permute-start
  68.5 5.6 collective-permute-start
  74.2 5.6 collective-permute-start
  80.0 5.6 collective-permute-start
  85.7 5.6 collective-permute-start
  91.4 5.6 collective-permute-start
  97.1 5.6 collective-permute-start
  102.8 5.6 collective-permute-start
  108.5 5.6 collective-permute-start
  114.5 6.2 %collective-permute-start.1 = (bf16[1,2,128,128]{3,2,1,0:T(8,128)(2,1)S(1)}, bf16[1,2,128,128]{3,2,1,0:T(8,128)(2,1)S(1)}, u32[]{:S(2)}, u32[]{:S(2)}) collective-permute-start(bf16[1,2,128,128]{3,2,1,0:T(8,128)(2,1)S(1)} %fusion.100), channel_id=1, source_target_pairs={{64,0},{128,64},{192,128},{256,192},{320,256},{384,320},{448,384},... | collective-permute-start | bytes 196616 | tf_op jit(solution)/shard_map/while/body/eval_jaxpr/ppermute | solution.py:18
  120.9 5.6 collective-permute-start.1
  126.6 5.6 collective-permute-start.1
  132.3 5.6 collective-permute-start.1
  138.0 6.0 %collective-permute-start.1 = (bf16[1,2,128,128]{3,2,1,0:T(8,128)(2,1)S(1)}, bf16[1,2,128,128]{3,2,1,0:T(8,128)(2,1)S(1)}, u32[]{:S(2)}, u32[]{:S(2)}) collective-permute-start(bf16[1,2,128,128]{3,2,1,0:T(8,128)(2,1)S(1)} %fusion.100), channel_id=1, source_target_pairs={{64,0},{128,64},{192,128},{256,192},{320,256},{384,320},{448,384},... | collective-permute-start | bytes 196616 | tf_op jit(solution)/shard_map/while/body/eval_jaxpr/ppermute | solution.py:18
  144.1 6.7 %collective-permute-start.1 = (bf16[1,2,128,128]{3,2,1,0:T(8,128)(2,1)S(1)}, bf16[1,2,128,128]{3,2,1,0:T(8,128)(2,1)S(1)}, u32[]{:S(2)}, u32[]{:S(2)}) collective-permute-start(bf16[1,2,128,128]{3,2,1,0:T(8,128)(2,1)S(1)} %fusion.100), channel_id=1, source_target_pairs={{64,0},{128,64},{192,128},{256,192},{320,256},{384,320},{448,384},... | collective-permute-start | bytes 196616 | tf_op jit(solution)/shard_map/while/body/eval_jaxpr/ppermute | solution.py:18
  150.9 7.4 %collective-permute-start.1 = (bf16[1,2,128,128]{3,2,1,0:T(8,128)(2,1)S(1)}, bf16[1,2,128,128]{3,2,1,0:T(8,128)(2,1)S(1)}, u32[]{:S(2)}, u32[]{:S(2)}) collective-permute-start(bf16[1,2,128,128]{3,2,1,0:T(8,128)(2,1)S(1)} %fusion.100), channel_id=1, source_target_pairs={{64,0},{128,64},{192,128},{256,192},{320,256},{384,320},{448,384},... | collective-permute-start | bytes 196616 | tf_op jit(solution)/shard_map/while/body/eval_jaxpr/ppermute | solution.py:18
  158.4 6.8 %collective-permute-start.1 = (bf16[1,2,128,128]{3,2,1,0:T(8,128)(2,1)S(1)}, bf16[1,2,128,128]{3,2,1,0:T(8,128)(2,1)S(1)}, u32[]{:S(2)}, u32[]{:S(2)}) collective-permute-start(bf16[1,2,128,128]{3,2,1,0:T(8,128)(2,1)S(1)} %fusion.100), channel_id=1, source_target_pairs={{64,0},{128,64},{192,128},{256,192},{320,256},{384,320},{448,384},... | collective-permute-start | bytes 196616 | tf_op jit(solution)/shard_map/while/body/eval_jaxpr/ppermute | solution.py:18
  165.4 6.8 %collective-permute-start.1 = (bf16[1,2,128,128]{3,2,1,0:T(8,128)(2,1)S(1)}, bf16[1,2,128,128]{3,2,1,0:T(8,128)(2,1)S(1)}, u32[]{:S(2)}, u32[]{:S(2)}) collective-permute-start(bf16[1,2,128,128]{3,2,1,0:T(8,128)(2,1)S(1)} %fusion.100), channel_id=1, source_target_pairs={{64,0},{128,64},{192,128},{256,192},{320,256},{384,320},{448,384},... | collective-permute-start | bytes 196616 | tf_op jit(solution)/shard_map/while/body/eval_jaxpr/ppermute | solution.py:18
  172.3 6.8 %collective-permute-start.1 = (bf16[1,2,128,128]{3,2,1,0:T(8,128)(2,1)S(1)}, bf16[1,2,128,128]{3,2,1,0:T(8,128)(2,1)S(1)}, u32[]{:S(2)}, u32[]{:S(2)}) collective-permute-start(bf16[1,2,128,128]{3,2,1,0:T(8,128)(2,1)S(1)} %fusion.100), channel_id=1, source_target_pairs={{64,0},{128,64},{192,128},{256,192},{320,256},{384,320},{448,384},... | collective-permute-start | bytes 196616 | tf_op jit(solution)/shard_map/while/body/eval_jaxpr/ppermute | solution.py:18
  179.2 6.8 %collective-permute-start.1 = (bf16[1,2,128,128]{3,2,1,0:T(8,128)(2,1)S(1)}, bf16[1,2,128,128]{3,2,1,0:T(8,128)(2,1)S(1)}, u32[]{:S(2)}, u32[]{:S(2)}) collective-permute-start(bf16[1,2,128,128]{3,2,1,0:T(8,128)(2,1)S(1)} %fusion.100), channel_id=1, source_target_pairs={{64,0},{128,64},{192,128},{256,192},{320,256},{384,320},{448,384},... | collective-permute-start | bytes 196616 | tf_op jit(solution)/shard_map/while/body/eval_jaxpr/ppermute | solution.py:18
  186.1 6.8 %collective-permute-start.1 = (bf16[1,2,128,128]{3,2,1,0:T(8,128)(2,1)S(1)}, bf16[1,2,128,128]{3,2,1,0:T(8,128)(2,1)S(1)}, u32[]{:S(2)}, u32[]{:S(2)}) collective-permute-start(bf16[1,2,128,128]{3,2,1,0:T(8,128)(2,1)S(1)} %fusion.100), channel_id=1, source_target_pairs={{64,0},{128,64},{192,128},{256,192},{320,256},{384,320},{448,384},... | collective-permute-start | bytes 196616 | tf_op jit(solution)/shard_map/while/body/eval_jaxpr/ppermute | solution.py:18
  193.0 6.8 %collective-permute-start.1 = (bf16[1,2,128,128]{3,2,1,0:T(8,128)(2,1)S(1)}, bf16[1,2,128,128]{3,2,1,0:T(8,128)(2,1)S(1)}, u32[]{:S(2)}, u32[]{:S(2)}) collective-permute-start(bf16[1,2,128,128]{3,2,1,0:T(8,128)(2,1)S(1)} %fusion.100), channel_id=1, source_target_pairs={{64,0},{128,64},{192,128},{256,192},{320,256},{384,320},{448,384},... | collective-permute-start | bytes 196616 | tf_op jit(solution)/shard_map/while/body/eval_jaxpr/ppermute | solution.py:18
  199.9 6.8 %collective-permute-start.1 = (bf16[1,2,128,128]{3,2,1,0:T(8,128)(2,1)S(1)}, bf16[1,2,128,128]{3,2,1,0:T(8,128)(2,1)S(1)}, u32[]{:S(2)}, u32[]{:S(2)}) collective-permute-start(bf16[1,2,128,128]{3,2,1,0:T(8,128)(2,1)S(1)} %fusion.100), channel_id=1, source_target_pairs={{64,0},{128,64},{192,128},{256,192},{320,256},{384,320},{448,384},... | collective-permute-start | bytes 196616 | tf_op jit(solution)/shard_map/while/body/eval_jaxpr/ppermute | solution.py:18
  206.9 6.8 %collective-permute-start.1 = (bf16[1,2,128,128]{3,2,1,0:T(8,128)(2,1)S(1)}, bf16[1,2,128,128]{3,2,1,0:T(8,128)(2,1)S(1)}, u32[]{:S(2)}, u32[]{:S(2)}) collective-permute-start(bf16[1,2,128,128]{3,2,1,0:T(8,128)(2,1)S(1)} %fusion.100), channel_id=1, source_target_pairs={{64,0},{128,64},{192,128},{256,192},{320,256},{384,320},{448,384},... | collective-permute-start | bytes 196616 | tf_op jit(solution)/shard_map/while/body/eval_jaxpr/ppermute | solution.py:18
  214.9 2.0 copy-start.10
  214.9 3.2 copy-start.11
  216.3 2.4 copy-start.7
  216.3 2.8 copy-start.5
  216.3 3.6 copy-start.4
Sparse Core Ops, SparseCore 0:
  216.4 85.1 reduce-scatter.3
where the time goes:
time: 568 us; the launch traced here: 564 us
  blocking collectives  254 us (45%)
  waiting for transfers between devices  175 us (31%)
  starting transfers between devices  96.5 us (17%)
  between operations  14.5 us (3%)
  local copies, waits for them, and re-layouts  8.76 us (2%)
  matrix products  8.32 us (1%)
  other arithmetic  6.51 us (1%)
    psum x1, blocking collectives, on_device(): summed = lax.psum(share, ('tm', 'dp'))  254 us
    ppermute x32, waiting for transfers between devices, shifted(): return lax.ppermute(block, axis, route)  96.7 us
    ppermute x32, starting transfers between devices, shifted(): return lax.ppermute(block, axis, route)  96.4 us
    unnamed x2, waiting for transfers between devices  77.9 us
  transfers between devices with their start and end apart: 33, of which 31 were waited for; matrix products, arithmetic and copies ran while one was open for 4% of the time, Pallas kernels for 0%

commit v1 on v0

v1 whole, which is shorter than its diff:
```python
import functools
import math

import jax
import jax.numpy as jnp
from jax import lax
from jax.experimental import pallas as pl
from jax.experimental.pallas import tpu as pltpu
from jax.sharding import PartitionSpec as P

W = 128
QB = 128
F32 = jnp.float32
BF16 = jnp.bfloat16
VMEM = pl.BlockSpec(memory_space=pltpu.VMEM)
SMEM = pl.BlockSpec(memory_space=pltpu.SMEM)
NEG = -1e30
EXTRA = 16


def dot(a, b, left, right, precision=None):
    return lax.dot_general(
        a, b, (((left,), (right,)), ((), ())), preferred_element_type=F32, precision=precision
    )


def call(body, out, args, specs=None, flops=0, transcendentals=0, moved=0):
    return pl.pallas_call(
        body,
        out_shape=[jax.ShapeDtypeStruct(s, t) for s, t in out],
        in_specs=specs or [VMEM] * len(args),
        out_specs=[VMEM] * len(out),
        compiler_params=pltpu.CompilerParams(vmem_limit_bytes=40 * 2**20),
        cost_estimate=pl.CostEstimate(
            flops=flops, transcendentals=transcendentals, bytes_accessed=moved
        ),
    )(*args)


def three_parts(value):
    high = value.astype(BF16)
    rest = value - high.astype(F32)
    middle = rest.astype(BF16)
    return high, middle, (rest - middle.astype(F32)).astype(BF16)


def put_totals(send, at, totals):
    row = lax.broadcasted_iota(jnp.int32, (EXTRA, send.shape[1]), 0)
    extra = jnp.zeros((EXTRA, send.shape[1]), F32)
    for h, total in enumerate(totals):
        for part, value in enumerate(three_parts(total)):
            extra = jnp.where(row == 3 * h + part, value.astype(F32), extra)
    send[at : at + EXTRA, :] = extra.astype(BF16)


def pre_body(heads, place, lat, wb, wc, x, cot, ld, b_out, c_out, cumc_out, cumr_out, fresh_out,
             back_out, table_out, send, mine_out):
    rows = lat.shape[0]
    cols = x.shape[1]
    hd = cols // heads
    n = wb.shape[1]
    scale = 1.0 / math.sqrt(n)
    b = dot(lat[...], wb[...], 1, 0).astype(BF16)
    c = dot(lat[...], wc[...], 1, 0).astype(BF16)
    b_out[...] = b
    c_out[...] = c
    share = mine_out.shape[1]
    mine_out[...] = lat[:, pl.ds(pl.multiple_of(place[0] * share, share), share)]
    t = lax.broadcasted_iota(jnp.int32, (rows, rows), 0)
    s = lax.broadcasted_iota(jnp.int32, (rows, rows), 1)
    lower = (s <= t).astype(F32)
    cumc = dot(lower, ld[...], 1, 0, lax.Precision.HIGHEST)
    cumr = dot(ld[...], lower, 0, 1, lax.Precision.HIGHEST)
    cumc_out[...] = cumc
    cumr_out[...] = cumr
    total = cumc[rows - 1 : rows, :]
    tail = jnp.exp(total - cumc)
    rise = jnp.exp(cumc) * scale
    table_out[...] = jnp.zeros_like(table_out)
    totals = []
    for h in range(heads):
        at = slice(h * hd, (h + 1) * hd)
        xs = (x[:, at].astype(F32) * tail[:, h : h + 1]).astype(BF16)
        gs = (cot[:, at].astype(F32) * rise[:, h : h + 1]).astype(BF16)
        fresh = dot(xs, b, 0, 0)
        back = dot(gs, c, 0, 0)
        fresh_out[at, :] = fresh
        back_out[at, :] = back
        send[at, :] = fresh.astype(BF16)
        send[cols + h * hd : cols + (h + 1) * hd, :] = back.astype(BF16)
        totals.append(jnp.broadcast_to(total[:, h : h + 1], (1, n)))
        table_out[h : h + 1, :] = totals[h]
    put_totals(send, 2 * cols, totals)


def totals_of(got, at):
    total = got[at : at + 1, :].astype(F32)
    for part in (1, 2):
        total = total + got[at + part : at + part + 1, :].astype(F32)
    return total


def pair_body(place, got, fwd, bwd, table, send):
    cols, n = fwd.shape
    slots, hd, _ = send.shape
    hd = hd - EXTRA
    me = place[0]
    late = me % 2
    chip = me // 2
    own = jnp.where(late == 1, table[1:2, :], table[0:1, :])
    theirs = jnp.where(
        late == 1, totals_of(got, 2 * cols + 3), totals_of(got, 2 * cols)
    )
    at = pl.ds(pl.multiple_of(late * hd, hd), hd)
    to = pl.ds(pl.multiple_of(cols + late * hd, hd), hd)
    got_f, got_b = got[at, :].astype(F32), got[to, :].astype(F32)
    by_own, by_theirs = jnp.exp(own), jnp.exp(theirs)
    early = late == 0
    f = jnp.where(early, by_theirs, 1.0) * fwd[at, :] + jnp.where(early, 1.0, by_own) * got_f
    b = jnp.where(early, 1.0, by_theirs) * bwd[at, :] + jnp.where(early, by_own, 1.0) * got_b
    f, b = f.astype(BF16), b.astype(BF16)
    row = lax.broadcasted_iota(jnp.int32, (EXTRA, n), 0)
    extra = jnp.zeros((EXTRA, n), F32)
    for part, value in enumerate(three_parts(own + theirs)):
        extra = jnp.where(row == part, value.astype(F32), extra)
    extra = extra.astype(BF16)
    for slot in range(slots):
        ahead = slot // 2 > chip

        @pl.when(ahead)
        def _():
            send[slot, :hd, :] = f

        @pl.when(jnp.logical_not(ahead))
        def _():
            send[slot, :hd, :] = b

        send[slot, hd:, :] = extra


def attend_body(heads, qb, place, offsets, q, k, v, tail, out):
    rows = q.shape[0]
    hd = q.shape[1] // heads
    w = tail.shape[0]
    scale = 1.0 / math.sqrt(hd)
    i = lax.broadcasted_iota(jnp.int32, (qb, qb + w), 0)
    u = lax.broadcasted_iota(jnp.int32, (qb, qb + w), 1)
    for blk in range(rows // qb):
        off = offsets[0, blk]
        seen = (u <= i + w) & (u >= i + 1 + off)
        if blk == 0:
            seen = seen & ((u >= w) | (place[0] > 0))
        for h in range(heads):
            at = slice(h * hd, (h + 1) * hd)
            if blk == 0:
                keys = jnp.concatenate([tail[:, at], k[:qb, at]], axis=0)
                values = jnp.concatenate(
                    [tail[:, heads * hd + h * hd : heads * hd + (h + 1) * hd], v[:qb, at]], axis=0
                )
            else:
                keys = k[blk * qb - w : (blk + 1) * qb, at]
                values = v[blk * qb - w : (blk + 1) * qb, at]
            scores = dot(q[blk * qb : (blk + 1) * qb, at], keys, 1, 1) * scale
            scores = jnp.where(seen, scores, NEG)
            expo = jnp.exp(scores - jnp.max(scores, axis=-1, keepdims=True))
            probs = (expo / jnp.sum(expo, axis=-1, keepdims=True)).astype(BF16)
            out[blk * qb : (blk + 1) * qb, at] = dot(probs, values, 1, 0)


def local_body(heads, x, cot, b, c, cumc, cumr, inner_out, gx_out, both_out):
    rows = x.shape[0]
    hd = x.shape[1] // heads
    n = b.shape[1]
    scale = 1.0 / math.sqrt(n)
    t = lax.broadcasted_iota(jnp.int32, (rows, rows), 0)
    s = lax.broadcasted_iota(jnp.int32, (rows, rows), 1)
    kern = dot(c[...], b[...], 1, 1) * scale
    weigh = None
    for h in range(heads):
        at = slice(h * hd, (h + 1) * hd)
        gap = cumc[:, h : h + 1] - cumr[h : h + 1, :]
        decay = jnp.exp(jnp.where(s <= t, gap, NEG))
        mixing = (kern * decay).astype(BF16)
        inner_out[:, at] = dot(mixing, x[:, at], 1, 0)
        gx_out[:, at] = dot(mixing, cot[:, at], 0, 0)
        one = dot(cot[:, at], x[:, at], 1, 1) * decay
        weigh = one if weigh is None else weigh + one
    weigh = (weigh * scale).astype(BF16)
    both_out[:, :n] = dot(weigh, c[...], 0, 0)
    both_out[:, n:] = dot(weigh, b[...], 1, 0)


def grads_body(heads, place, got, pair, x, cot, cumc, both, out, enter_out, leave_out):
    rows = x.shape[0]
    cols = x.shape[1]
    hd = cols // heads
    slots, _, n = got.shape
    scale = 1.0 / math.sqrt(n)
    chip = place[0] // 2
    early = place[0] % 2 == 0
    gb = both[:, :n]
    gc = both[:, n:]
    for h in range(heads):
        at = slice(h * hd, (h + 1) * hd)
        decays = [jnp.exp(totals_of(got.at[2 * i + h], hd)) for i in range(slots // 2)]
        state = jnp.zeros((hd, n), F32)
        grad = jnp.zeros((hd, n), F32)
        for i in range(slots // 2):
            used = i < chip
            state = jnp.where(used, decays[i], 1.0) * state + jnp.where(used, 1.0, 0.0) * got[
                2 * i + h, :hd, :
            ].astype(F32)
        for i in reversed(range(slots // 2)):
            used = i > chip
            grad = jnp.where(used, decays[i], 1.0) * grad + jnp.where(used, 1.0, 0.0) * got[
                2 * i + h, :hd, :
            ].astype(F32)
        by_theirs = jnp.exp(totals_of(pair, 2 * cols + 3 * h))
        their_f = pair[at, :].astype(F32)
        their_b = pair[cols + h * hd : cols + (h + 1) * hd, :].astype(F32)
        state = jnp.where(early, 1.0, by_theirs) * state + jnp.where(early, 0.0, 1.0) * their_f
        grad = jnp.where(early, by_theirs, 1.0) * grad + jnp.where(early, 1.0, 0.0) * their_b
        state, grad = state.astype(BF16), grad.astype(BF16)
        enter_out[at, :] = state
        leave_out[at, :] = grad
        cum = cumc[:, h : h + 1]
        tail = jnp.exp(cumc[rows - 1 : rows, h : h + 1] - cum)
        rise = jnp.exp(cum) * scale
        gb = gb + tail * dot(x[:, at], grad, 1, 0)
        gc = gc + rise * dot(cot[:, at], state, 1, 0)
    piece = out.shape[1]
    gb, gc = gb.astype(BF16), gc.astype(BF16)
    for i in range(out.shape[0]):
        out[i, :, :n] = gb[i * piece : (i + 1) * piece, :]
        out[i, :, n:] = gc[i * piece : (i + 1) * piece, :]


def finish_body(heads, b, c, cumc, inner, gx, attended, enter, leave, layer_out, input_grad):
    rows = b.shape[0]
    hd = inner.shape[1] // heads
    n = b.shape[1]
    scale = 1.0 / math.sqrt(n)
    for h in range(heads):
        at = slice(h * hd, (h + 1) * hd)
        cum = cumc[:, h : h + 1]
        tail = jnp.exp(cumc[rows - 1 : rows, h : h + 1] - cum)
        rise = jnp.exp(cum) * scale
        y = inner[:, at] + rise * dot(c[...], enter[at, :], 1, 1)
        y = y * lax.rsqrt(jnp.mean(y * y, axis=-1, keepdims=True) + 1e-05)
        layer_out[:, at] = (y + attended[:, at]).astype(BF16)
        g = gx[:, at] + tail * dot(b[...], leave[at, :], 1, 1)
        input_grad[:, at] = g.astype(BF16)


def gather_body(scale, got, out):
    total = got[0].astype(F32)
    for i in range(1, got.shape[0]):
        total = total + got[i].astype(F32)
    total = (total * scale).astype(BF16)
    for i in range(out.shape[0]):
        out[i] = total


def project_body(mine, both, out):
    size, rows, cols = both.shape
    term = dot(mine[...], both[...].reshape(size * rows, cols), 0, 0)
    piece = out.shape[1]
    for i in range(out.shape[0]):
        out[i] = term[i * piece : (i + 1) * piece, :].astype(BF16)


def unpack_body(got, out):
    piece = got.shape[1]
    for i in range(got.shape[0]):
        out[i * piece : (i + 1) * piece, :] = got[i].astype(F32)


def shifted(block, axis, distance):
    devices = range(lax.axis_size(axis))
    route = [(i - distance, i) for i in devices if i - distance in devices]
    return lax.ppermute(block, axis, route)


def swapped(block, axis, distance):
    return lax.ppermute(block, axis, [(i, i ^ distance) for i in range(lax.axis_size(axis))])


def summed(pieces, axes, scale=1.0):
    got = lax.all_to_all(pieces, axes, 0, 0)
    copies = call(functools.partial(gather_body, scale), [(pieces.shape, BF16)], (got,))[0]
    return lax.all_to_all(copies, axes, 0, 0)


def on_device(latents, proj_input, proj_output, scan_input, log_decay, att_queries, att_keys,
              att_values, scan_cotangent, window_offsets):
    _, rows, width = latents.shape
    heads = log_decay.shape[2]
    cols = scan_input.shape[2]
    hd = cols // heads
    n = proj_input.shape[1]
    share = width // lax.axis_size("space")
    assert heads == 2
    tm = lax.axis_size("tm")
    me = lax.axis_index("tm")
    lat, x, ld = latents[0], scan_input[0], log_decay[0]
    q, k, v, cot = att_queries[0], att_keys[0], att_values[0], scan_cotangent[0]

    tails = shifted(jnp.concatenate([k[rows - W :], v[rows - W :]], axis=1), "tm", 1)
    state = ((cols, n), F32)
    wire = ((2 * cols + EXTRA, n), BF16)
    b, c, cumc, cumr, fwd, bwd, table, send, mine = call(
        functools.partial(pre_body, heads),
        [((rows, n), BF16), ((rows, n), BF16), ((rows, heads), F32), ((heads, rows), F32), state, state,
         ((24, n), F32), wire, ((rows, share), BF16)],
        (lax.axis_index("space")[None], lat, proj_input, proj_output, x, cot, ld),
        [SMEM] + [VMEM] * 6,
        flops=2 * rows * width * 2 * n + 4 * rows * cols * n,
    )
    attended = call(
        functools.partial(attend_body, heads, QB),
        [((rows, cols), F32)],
        (me[None], window_offsets, q, k, v, tails),
        [SMEM, SMEM] + [VMEM] * 4,
        flops=4 * rows * 2 * W * cols,
        transcendentals=rows * 2 * W * heads,
    )[0]
    inner, gx, both = call(
        functools.partial(local_body, heads),
        [((rows, cols), F32), ((rows, cols), F32), ((rows, 2 * n), F32)],
        (x, cot, b, c, cumc, cumr),
        flops=8 * rows * rows * cols,
        transcendentals=rows * rows * heads,
    )
    pair = swapped(send, "tm", 1)
    spread = call(
        pair_body,
        [((tm, hd + EXTRA, n), BF16)],
        (me[None], pair, fwd, bwd, table),
        [SMEM] + [VMEM] * 4,
    )[0]
    got = lax.all_to_all(spread, "tm", 0, 0)
    space = lax.axis_size("space")
    both, enter, leave = call(
        functools.partial(grads_body, heads),
        [((space, rows // space, 2 * n), BF16), ((cols, n), BF16), ((cols, n), BF16)],
        (me[None], got, pair, x, cot, cumc, both),
        [SMEM] + [VMEM] * 6,
        flops=4 * rows * cols * n,
    )
    layer_out, input_grad = call(
        functools.partial(finish_body, heads),
        [((rows, cols), BF16), ((rows, cols), BF16)],
        (b, c, cumc, inner, gx, attended, enter, leave),
        flops=4 * rows * cols * n,
    )
    both = summed(both, ("space",))
    others = tm * lax.axis_size("dp")
    term = call(
        project_body,
        [((others, share // others, 2 * n), BF16)],
        (mine, both),
        flops=2 * rows * share * 2 * n,
    )[0]
    term = summed(term, ("tm", "dp"), 1.0 / math.sqrt(rows * others))
    proj_grad = call(unpack_body, [((share, 2 * n), F32)], (term,))[0]
    return layer_out[None], input_grad[None], proj_grad


def solution(mesh):
    wide = P("dp", "tm", "space")
    return jax.shard_map(
        on_device,
        mesh=mesh,
        in_specs=(P("dp", "tm", None), P(), P(), wide, wide, wide, wide, wide, wide, P("dp", "tm")),
        out_specs=(wide, wide, P("space", None)),
        check_vma=False,
    )
```

time: 568 us -> 125 us (0.22)
  blocking collectives: 254 us -> 39.5 us
  waiting for transfers between devices: 175 us -> 30.6 us
  starting transfers between devices: 96.5 us -> 38.7 us
  between operations: 14.5 us -> 0.8 us
  Pallas kernels: 0 us -> 8.57 us
  matrix products: 8.32 us -> 0 us
  other arithmetic: 6.51 us -> 0.01 us
    psum x1 -> x0, blocking collectives: 254 us -> none  [on_device(): summed = lax.psum(share, ('tm', 'dp'))]
    ppermute x32 -> x1, waiting for transfers between devices: 96.7 us -> 0.01 us  [shifted(): return lax.ppermute(block, axis, route)]
    ppermute x32 -> x1, starting transfers between devices: 96.4 us -> 3.67 us  [shifted(): return lax.ppermute(block, axis, route)]
    unnamed x2 -> x0, waiting for transfers between devices: 77.9 us -> none
    all_to_all x0 -> x2, blocking collectives: none -> 39.5 us  [the longest x1 22.2 us: summed(): got = lax.all_to_all(pieces, axes, 0, 0)]
    all_to_all x0 -> x3, waiting for transfers between devices: none -> 29.6 us  [the longest x1 17.8 us: on_device(): got = lax.all_to_all(spread, 'tm', 0, 0)]
    all_to_all x0 -> x3, starting transfers between devices: none -> 19 us  [the longest x1 9.77 us: summed(): got = lax.all_to_all(pieces, axes, 0, 0)]
    ppermute x0 -> x1, starting transfers between devices: none -> 16.1 us  [swapped(): lax.ppermute(block, axis, [(i, i ^ distance) for i in range(lax.axis_size...]
  transfers between devices with their start and end apart: 33 -> 5, of which waited for: 31 -> 4; matrix products, arithmetic and copies ran while one was open for 4% -> 0% of each run, Pallas kernels for 0% -> 3%
where the time goes in v1:
time: 125 us; the launch traced here: 124 us
  blocking collectives  39.5 us (32%)
  starting transfers between devices  38.7 us (31%)
  waiting for transfers between devices  30.6 us (24%)
  Pallas kernels  8.57 us (7%)
  local copies, waits for them, and re-layouts  5.78 us (5%)
    all_to_all x1, blocking collectives, summed(): got = lax.all_to_all(pieces, axes, 0, 0)  22.2 us
    all_to_all x1, waiting for transfers between devices, on_device(): got = lax.all_to_all(spread, 'tm', 0, 0)  17.8 us
    all_to_all x1, blocking collectives, summed(): return lax.all_to_all(copies, axes, 0, 0)  17.3 us
    ppermute x1, starting transfers between devices, swapped(): lax.ppermute(block, axis, [(i, i ^ distance) for i in range(lax.axis_size...  16.1 us
    all_to_all x1, starting transfers between devices, summed(): got = lax.all_to_all(pieces, axes, 0, 0)  9.77 us
    pallas_call x10, Pallas kernels, call(): pl.pallas_call(body, out_shape=[jax.ShapeDtypeStruct(s, t) for s, t in ou...  8.57 us
    all_to_all x1, waiting for transfers between devices, summed(): return lax.all_to_all(copies, axes, 0, 0)  6.25 us
    unnamed x21, local copies, waits for them, and re-layouts  5.77 us
  transfers between devices with their start and end apart: 5, of which 4 were waited for; matrix products, arithmetic and copies ran while one was open for 0% of the time, Pallas kernels for 3%

profile of v1, /device:TPU:1, one launch (start us, length us, event | category | flops | bytes accessed | tf_op | source)
XLA Modules:
  0.0 124.0 jit_solution(2890883985173042099)
XLA Ops:
  0.6 0.0 copy-start
  0.6 0.8 copy.13
  1.5 0.1 copy-done
  1.6 0.0 copy-start.1
  1.6 0.9 copy-done.1
  2.5 0.0 copy-start.3
  2.5 1.2 copy-done.3
  3.7 0.0 copy-start.4
  3.7 1.0 copy-done.4
  4.7 0.0 copy-start.5
  4.7 1.0 copy-done.5
  5.8 1.5 %shard_map.121 = (bf16[256,128]{1,0:T(8,128)(2,1)S(1)}, bf16[256,128]{1,0:T(8,128)(2,1)S(1)}, f32[256,2]{1,0:T(8,128)S(1)}, f32[2,256]{1,0:T(2,128)S(1)}, f32[25...) custom-call(s32[1]{0:T(128)} %bitcast.place, ...), custom_call_target="tpu_custom_call" | custom-call | flops 301989888 | tf_op jit(solution)/shard_map/pallas_call | solution.py:28
  7.3 16.1 %collective-permute-start.1 = (bf16[528,128]{1,0:T(8,128)(2,1)S(1)}, bf16[528,128]{1,0:T(8,128)(2,1)S(1)}, u32[]{:S(2)}, u32[]{:S(2)}) collective-permute-start(bf16[528,128]{1,0:T(8,128)(2,1)S(1)} %get-tuple-element.26), channel_id=1, source_target_pairs={{0,64},{64,0},{128,192},{192,128},{256,320},{320,256},{384,448},{4... | collective-permute-start | bytes 405512 | tf_op jit(solution)/shard_map/ppermute | solution.py:285
  23.3 1.0 collective-permute-done.1.got.pair
  24.3 1.0 shard_map.124
  25.3 0.0 copy-start.2
  25.3 3.9 %all-to-all-start = ((bf16[16,144,128]{2,1,0:T(8,128)(2,1)}), bf16[16,144,128]{2,1,0:T(8,128)(2,1)S(1)}, u32[]{:S(2)}, u32[]{:S(2)}) async-start(bf16[16,144,128]{2,1,0:T(8,128)(2,1)} %shard_map.124), calls=%async_computation | async-start | bytes 1179648 | tf_op jit(solution)/shard_map/all_to_all | solution.py:341
  29.2 0.0 copy-done.2
  29.2 0.8 shard_map.122
  30.0 17.8 %all-to-all-done.got = bf16[16,144,128]{2,1,0:T(8,128)(2,1)S(1)} async-done(((bf16[16,144,128]{2,1,0:T(8,128)(2,1)}), bf16[16,144,128]{2,1,0:T(8,128)(2,1)S(1)}, u32[]{:S(2)}, u32[]{:S(2)}) %all-to-all-start) | async-done | bytes 589856 | tf_op jit(solution)/shard_map/all_to_all | solution.py:341
  47.8 0.5 shard_map.125
  48.4 22.2 %all_to_all.25.got = bf16[16,16,256]{2,1,0:T(8,128)(2,1)S(1)} all-to-all(bf16[16,16,256]{2,1,0:T(8,128)(2,1)S(1)} %get-tuple-element.36), channel_id=1, replica_groups=mesh['tm'=16,'space'=16,'dp'=4] {'space'}, dimensions={0} | all-to-all | bytes 262144 | tf_op jit(solution)/shard_map/all_to_all | solution.py:289
  70.6 17.3 %all_to_all.26.both = bf16[16,16,256]{2,1,0:T(8,128)(2,1)S(1)} all-to-all(bf16[16,16,256]{2,1,0:T(8,128)(2,1)S(1)} %shard_map.127), channel_id=1, replica_groups=mesh['tm'=16,'space'=16,'dp'=4] {'space'}, dimensions={0} | all-to-all | bytes 262144 | tf_op jit(solution)/shard_map/all_to_all | solution.py:291
  87.9 0.0 copy-start.7
  87.9 0.8 shard_map.128
  88.7 0.0 copy-start.6
  88.7 9.8 %all-to-all-start.3 = ((bf16[64,2,256]{2,1,0:T(2,128)(2,1)}), bf16[64,2,256]{2,1,0:T(2,128)(2,1)S(1)}, u32[]{:S(2)}, u32[]{:S(2)}) async-start(bf16[64,2,256]{2,1,0:T(2,128)(2,1)} %shard_map.128), calls=%async_computation.3 | async-start | bytes 131072 | tf_op jit(solution)/shard_map/all_to_all | solution.py:289
  98.5 0.0 copy-done.7
  98.5 0.0 copy-done.6
  98.6 0.0 copy-start.8
  98.6 3.7 %collective-permute-start = (bf16[128,512]{1,0:T(8,128)(2,1)S(1)}, bf16[128,512]{1,0:T(8,128)(2,1)S(1)}, u32[]{:S(2)}, u32[]{:S(2)}) collective-permute-start(bf16[128,512]{1,0:T(8,128)(2,1)S(1)} %pad_maximum_fusion), channel_id=1, source_target_pairs={{0,64},{64,128},{128,192},{192,256},{256,320},{320,384},{384,448},... | collective-permute-start | bytes 393224 | tf_op jit(solution)/shard_map/ppermute | solution.py:281
  102.3 5.5 %all-to-all-done.3.got = bf16[64,2,256]{2,1,0:T(2,128)(2,1)S(1)} async-done(((bf16[64,2,256]{2,1,0:T(2,128)(2,1)}), bf16[64,2,256]{2,1,0:T(2,128)(2,1)S(1)}, u32[]{:S(2)}, u32[]{:S(2)}) %all-to-all-start.3) | async-done | bytes 65568 | tf_op jit(solution)/shard_map/all_to_all | solution.py:289
  107.8 0.7 shard_map.129
  108.5 5.3 %all-to-all-start.4 = ((bf16[64,2,256]{2,1,0:T(2,128)(2,1)}), bf16[64,2,256]{2,1,0:T(2,128)(2,1)S(1)}, u32[]{:S(2)}, u32[]{:S(2)}) async-start(bf16[64,2,256]{2,1,0:T(2,128)(2,1)} %shard_map.129), calls=%async_computation.4 | async-start | bytes 131072 | tf_op jit(solution)/shard_map/all_to_all | solution.py:291
  113.9 0.0 collective-permute-done.tail
  113.9 0.0 copy-start.9
  113.9 0.0 copy-done.8
  113.9 0.6 copy-done.9
  114.5 1.4 %shard_map.123.attended = f32[256,256]{1,0:T(8,128)S(1)} custom-call(s32[1]{0:T(128)} %bitcast.5.place, s32[1,2]{1,0:T(1,128)S(1)} %copy-done.9, bf16[256,256]{1,0:T(8,128)(2,1)S(1)} %bitcast.25, bf16[256,256]{1,0:T(8,128)(2,1)S(1)} %bitcast.23, bf16[256,256]{1,0:T(8,128)(2,1)S(1)} %bitcast.24, bf16[128,512]{1,0:T(8,128)(2,1)S(1)} %collective-permute-done.tail), custom_call_target="tpu_custom_call" | custom-call | flops 67108864 | tf_op jit(solution)/shard_map/pallas_call | solution.py:28
  116.0 1.0 shard_map.126
  117.0 6.3 %all-to-all-done.4.got = bf16[64,2,256]{2,1,0:T(2,128)(2,1)S(1)} async-done(((bf16[64,2,256]{2,1,0:T(2,128)(2,1)}), bf16[64,2,256]{2,1,0:T(2,128)(2,1)S(1)}, u32[]{:S(2)}, u32[]{:S(2)}) %all-to-all-start.4) | async-done | bytes 65568 | tf_op jit(solution)/shard_map/all_to_all | solution.py:291
  123.3 0.7 shard_map.130
  (3 shorter events, 0.0 us)
Async XLA Ops:
  0.6 0.9 copy-start
  1.6 0.9 copy-start.1
  2.5 1.2 copy-start.3
  3.7 1.0 copy-start.4
  4.7 1.0 copy-start.5
  7.3 17.0 %collective-permute-start.1 = (bf16[528,128]{1,0:T(8,128)(2,1)S(1)}, bf16[528,128]{1,0:T(8,128)(2,1)S(1)}, u32[]{:S(2)}, u32[]{:S(2)}) collective-permute-start(bf16[528,128]{1,0:T(8,128)(2,1)S(1)} %get-tuple-element.26), channel_id=1, source_target_pairs={{0,64},{64,0},{128,192},{192,128},{256,320},{320,256},{384,448},{4... | collective-permute-start | bytes 405512 | tf_op jit(solution)/shard_map/ppermute | solution.py:285
  25.3 3.9 %copy-start.2 = (bf16[1,256,256]{2,1,0:T(8,128)(2,1)S(1)}, bf16[1,256,256]{2,1,0:T(8,128)(2,1)}, u32[]{:S(2)}) copy-start(bf16[1,256,256]{2,1,0:T(8,128)(2,1)} %param.18) | copy-start | bytes 393220
  25.3 22.5 %all-to-all-start = ((bf16[16,144,128]{2,1,0:T(8,128)(2,1)}), bf16[16,144,128]{2,1,0:T(8,128)(2,1)S(1)}, u32[]{:S(2)}, u32[]{:S(2)}) async-start(bf16[16,144,128]{2,1,0:T(8,128)(2,1)} %shard_map.124), calls=%async_computation | async-start | bytes 1179648 | tf_op jit(solution)/shard_map/all_to_all | solution.py:341
  87.9 10.6 %copy-start.7 = (bf16[1,256,256]{2,1,0:T(8,128)(2,1)S(1)}, bf16[1,256,256]{2,1,0:T(8,128)(2,1)}, u32[]{:S(2)}) copy-start(bf16[1,256,256]{2,1,0:T(8,128)(2,1)} %param.17) | copy-start | bytes 393220
  88.7 9.8 %copy-start.6 = (bf16[1,256,256]{2,1,0:T(8,128)(2,1)S(1)}, bf16[1,256,256]{2,1,0:T(8,128)(2,1)}, u32[]{:S(2)}) copy-start(bf16[1,256,256]{2,1,0:T(8,128)(2,1)} %param.16) | copy-start | bytes 393220
  88.7 19.1 %all-to-all-start.3 = ((bf16[64,2,256]{2,1,0:T(2,128)(2,1)}), bf16[64,2,256]{2,1,0:T(2,128)(2,1)S(1)}, u32[]{:S(2)}, u32[]{:S(2)}) async-start(bf16[64,2,256]{2,1,0:T(2,128)(2,1)} %shard_map.128), calls=%async_computation.3 | async-start | bytes 131072 | tf_op jit(solution)/shard_map/all_to_all | solution.py:289
  98.6 15.3 %copy-start.8 = (bf16[1,256,256]{2,1,0:T(8,128)(2,1)S(1)}, bf16[1,256,256]{2,1,0:T(8,128)(2,1)}, u32[]{:S(2)}) copy-start(bf16[1,256,256]{2,1,0:T(8,128)(2,1)} %param.15) | copy-start | bytes 393220
  98.6 15.3 %collective-permute-start = (bf16[128,512]{1,0:T(8,128)(2,1)S(1)}, bf16[128,512]{1,0:T(8,128)(2,1)S(1)}, u32[]{:S(2)}, u32[]{:S(2)}) collective-permute-start(bf16[128,512]{1,0:T(8,128)(2,1)S(1)} %pad_maximum_fusion), channel_id=1, source_target_pairs={{0,64},{64,128},{128,192},{192,256},{256,320},{320,384},{384,448},... | collective-permute-start | bytes 393224 | tf_op jit(solution)/shard_map/ppermute | solution.py:281
  108.5 14.7 %all-to-all-start.4 = ((bf16[64,2,256]{2,1,0:T(2,128)(2,1)}), bf16[64,2,256]{2,1,0:T(2,128)(2,1)S(1)}, u32[]{:S(2)}, u32[]{:S(2)}) async-start(bf16[64,2,256]{2,1,0:T(2,128)(2,1)} %shard_map.129), calls=%async_computation.4 | async-start | bytes 131072 | tf_op jit(solution)/shard_map/all_to_all | solution.py:291
  113.9 0.7 copy-start.9

commit v2 on v1

--- a/solution.py
+++ b/solution.py
@@ -13,6 +13,7 @@
 F32 = jnp.float32
 BF16 = jnp.bfloat16
 VMEM = pl.BlockSpec(memory_space=pltpu.VMEM)
+HBM = pl.BlockSpec(memory_space=pltpu.HBM)
 SMEM = pl.BlockSpec(memory_space=pltpu.SMEM)
 NEG = -1e30
 EXTRA = 16
@@ -24,12 +25,13 @@
     )
 
 
-def call(body, out, args, specs=None, flops=0, transcendentals=0, moved=0):
+def call(body, out, args, specs=None, scratch=(), flops=0, transcendentals=0, moved=0):
     return pl.pallas_call(
         body,
         out_shape=[jax.ShapeDtypeStruct(s, t) for s, t in out],
         in_specs=specs or [VMEM] * len(args),
         out_specs=[VMEM] * len(out),
+        scratch_shapes=scratch,
         compiler_params=pltpu.CompilerParams(vmem_limit_bytes=40 * 2**20),
         cost_estimate=pl.CostEstimate(
             flops=flops, transcendentals=transcendentals, bytes_accessed=moved
@@ -53,24 +55,23 @@
     send[at : at + EXTRA, :] = extra.astype(BF16)
 
 
-def pre_body(heads, place, lat, wb, wc, x, cot, ld, b_out, c_out, cumc_out, cumr_out, fresh_out,
-             back_out, table_out, send, mine_out):
+def pre_body(heads, place, lat_in, wb_in, wc_in, x_in, cot_in, ld_in, b_out, c_out, cumc_out, cumr_out,
+             fresh_out, back_out, table_out, send, mine_out, lat, wb, wc, x, cot, ld, sems):
+    pairs = ((ld_in, ld), (lat_in, lat), (wb_in, wb), (wc_in, wc), (x_in, x), (cot_in, cot))
+    copies = [pltpu.make_async_copy(src, dst, sems.at[i]) for i, (src, dst) in enumerate(pairs)]
+    for copy in copies:
+        copy.start()
     rows = lat.shape[0]
     cols = x.shape[1]
     hd = cols // heads
     n = wb.shape[1]
     scale = 1.0 / math.sqrt(n)
-    b = dot(lat[...], wb[...], 1, 0).astype(BF16)
-    c = dot(lat[...], wc[...], 1, 0).astype(BF16)
-    b_out[...] = b
-    c_out[...] = c
-    share = mine_out.shape[1]
-    mine_out[...] = lat[:, pl.ds(pl.multiple_of(place[0] * share, share), share)]
     t = lax.broadcasted_iota(jnp.int32, (rows, rows), 0)
     s = lax.broadcasted_iota(jnp.int32, (rows, rows), 1)
     lower = (s <= t).astype(F32)
-    cumc = dot(lower, ld[...], 1, 0, lax.Precision.HIGHEST)
-    cumr = dot(ld[...], lower, 0, 1, lax.Precision.HIGHEST)
+    copies[0].wait()
+    cumc = dot(lower, ld[...], 1, 1, lax.Precision.HIGHEST)
+    cumr = dot(ld[...], lower, 1, 1, lax.Precision.HIGHEST)
     cumc_out[...] = cumc
     cumr_out[...] = cumr
     total = cumc[rows - 1 : rows, :]
@@ -78,6 +79,21 @@
     rise = jnp.exp(cumc) * scale
     table_out[...] = jnp.zeros_like(table_out)
     totals = []
+    for h in range(heads):
+        totals.append(jnp.broadcast_to(total[:, h : h + 1], (1, n)))
+        table_out[h : h + 1, :] = totals[h]
+    put_totals(send, 2 * cols, totals)
+    copies[1].wait()
+    share = mine_out.shape[1]
+    mine_out[...] = lat[:, pl.ds(pl.multiple_of(place[0] * share, share), share)]
+    copies[2].wait()
+    b = dot(lat[...], wb[...], 1, 0).astype(BF16)
+    b_out[...] = b
+    copies[3].wait()
+    c = dot(lat[...], wc[...], 1, 0).astype(BF16)
+    c_out[...] = c
+    copies[4].wait()
+    copies[5].wait()
     for h in range(heads):
         at = slice(h * hd, (h + 1) * hd)
         xs = (x[:, at].astype(F32) * tail[:, h : h + 1]).astype(BF16)
@@ -88,9 +104,6 @@
         back_out[at, :] = back
         send[at, :] = fresh.astype(BF16)
         send[cols + h * hd : cols + (h + 1) * hd, :] = back.astype(BF16)
-        totals.append(jnp.broadcast_to(total[:, h : h + 1], (1, n)))
-        table_out[h : h + 1, :] = totals[h]
-    put_totals(send, 2 * cols, totals)
 
 
 def totals_of(got, at):
@@ -118,27 +131,17 @@
     early = late == 0
     f = jnp.where(early, by_theirs, 1.0) * fwd[at, :] + jnp.where(early, 1.0, by_own) * got_f
     b = jnp.where(early, 1.0, by_theirs) * bwd[at, :] + jnp.where(early, by_own, 1.0) * got_b
-    f, b = f.astype(BF16), b.astype(BF16)
     row = lax.broadcasted_iota(jnp.int32, (EXTRA, n), 0)
     extra = jnp.zeros((EXTRA, n), F32)
     for part, value in enumerate(three_parts(own + theirs)):
         extra = jnp.where(row == part, value.astype(F32), extra)
     extra = extra.astype(BF16)
     for slot in range(slots):
-        ahead = slot // 2 > chip
-
-        @pl.when(ahead)
-        def _():
-            send[slot, :hd, :] = f
-
-        @pl.when(jnp.logical_not(ahead))
-        def _():
-            send[slot, :hd, :] = b
-
+        send[slot, :hd, :] = jnp.where(slot // 2 > chip, f, b).astype(BF16)
         send[slot, hd:, :] = extra
 
 
-def attend_body(heads, qb, place, offsets, q, k, v, tail, out):
+def attend(heads, qb, place, offsets, q, k, v, tail, out):
     rows = q.shape[0]
     hd = q.shape[1] // heads
     w = tail.shape[0]
@@ -167,7 +170,9 @@
             out[blk * qb : (blk + 1) * qb, at] = dot(probs, values, 1, 0)
 
 
-def local_body(heads, x, cot, b, c, cumc, cumr, inner_out, gx_out, both_out):
+def middle_body(heads, qb, place, offsets, q, k, v, tail, x, cot, b, c, cumc, cumr, attended_out,
+                inner_out, gx_out, both_out):
+    attend(heads, qb, place, offsets, q, k, v, tail, attended_out)
     rows = x.shape[0]
     hd = x.shape[1] // heads
     n = b.shape[1]
@@ -302,9 +307,13 @@
     assert heads == 2
     tm = lax.axis_size("tm")
     me = lax.axis_index("tm")
-    lat, x, ld = latents[0], scan_input[0], log_decay[0]
+    lat, x, ld = latents[0], scan_input[0], log_decay[0].T
     q, k, v, cot = att_queries[0], att_keys[0], att_values[0], scan_cotangent[0]
 
+    inputs = [
+        pltpu.with_memory_space_constraint(a, pltpu.HBM)
+        for a in (lat, proj_input, proj_output, x, cot, ld)
+    ]
     tails = shifted(jnp.concatenate([k[rows - W :], v[rows - W :]], axis=1), "tm", 1)
     state = ((cols, n), F32)
     wire = ((2 * cols + EXTRA, n), BF16)
@@ -312,24 +321,18 @@
         functools.partial(pre_body, heads),
         [((rows, n), BF16), ((rows, n), BF16), ((rows, heads), F32), ((heads, rows), F32), state, state,
          ((24, n), F32), wire, ((rows, share), BF16)],
-        (lax.axis_index("space")[None], lat, proj_input, proj_output, x, cot, ld),
-        [SMEM] + [VMEM] * 6,
+        (lax.axis_index("space")[None], *inputs),
+        [SMEM] + [HBM] * 6,
+        [pltpu.VMEM(a.shape, a.dtype) for a in inputs] + [pltpu.SemaphoreType.DMA((6,))],
         flops=2 * rows * width * 2 * n + 4 * rows * cols * n,
     )
-    attended = call(
-        functools.partial(attend_body, heads, QB),
-        [((rows, cols), F32)],
-        (me[None], window_offsets, q, k, v, tails),
-        [SMEM, SMEM] + [VMEM] * 4,
-        flops=4 * rows * 2 * W * cols,
-        transcendentals=rows * 2 * W * heads,
-    )[0]
-    inner, gx, both = call(
-        functools.partial(local_body, heads),
-        [((rows, cols), F32), ((rows, cols), F32), ((rows, 2 * n), F32)],
-        (x, cot, b, c, cumc, cumr),
-        flops=8 * rows * rows * cols,
-        transcendentals=rows * rows * heads,
+    attended, inner, gx, both = call(
+        functools.partial(middle_body, heads, QB),
+        [((rows, cols), F32), ((rows, cols), F32), ((rows, cols), F32), ((rows, 2 * n), F32)],
+        (me[None], window_offsets, q, k, v, tails, x, cot, b, c, cumc, cumr),
+        [SMEM, SMEM] + [VMEM] * 10,
+        flops=8 * rows * rows * cols + 4 * rows * 2 * W * cols,
+        transcendentals=rows * rows * heads + rows * 2 * W * heads,
     )
     pair = swapped(send, "tm", 1)
     spread = call(

time: 125 us -> 122 us (0.976)
  blocking collectives: 39.5 us -> 60.6 us
  starting transfers between devices: 38.7 us -> 28.9 us
  waiting for transfers between devices: 30.6 us -> 21.4 us
  local copies, waits for them, and re-layouts: 5.78 us -> 0.68 us
    all_to_all x1 -> x2, blocking collectives: 22.2 us -> 43.8 us  [summed(): got = lax.all_to_all(pieces, axes, 0, 0)]
    all_to_all x1, waiting for transfers between devices: 17.8 us -> 1.27 us  [on_device(): got = lax.all_to_all(spread, 'tm', 0, 0)]
    ppermute x1, waiting for transfers between devices: 0.01 us -> 10.8 us  [shifted(): return lax.ppermute(block, axis, route)]
    all_to_all x1 -> x0, starting transfers between devices: 9.77 us -> none  [summed(): got = lax.all_to_all(pieces, axes, 0, 0)]
    all_to_all x1 -> x0, waiting for transfers between devices: 5.53 us -> none  [summed(): got = lax.all_to_all(pieces, axes, 0, 0)]
    unnamed x21 -> x12, local copies, waits for them, and re-layouts: 5.77 us -> 0.67 us
    all_to_all x1, waiting for transfers between devices: 6.25 us -> 8.35 us  [summed(): return lax.all_to_all(copies, axes, 0, 0)]
    pallas_call x10 -> x9, Pallas kernels: 8.57 us -> 8.95 us  [call(): pl.pallas_call(body, out_shape=[jax.ShapeDtypeStruct(s, t) for s, t in ou...]
  transfers between devices with their start and end apart: 5 -> 4, of which waited for: 4 -> 4; matrix products, arithmetic and copies ran while one was open for 0% -> 0% of each run, Pallas kernels for 3% -> 3%
where the time goes in v2:
time: 122 us; the launch traced here: 121 us
  blocking collectives  60.6 us (50%)
  starting transfers between devices  28.9 us (24%)
  waiting for transfers between devices  21.4 us (18%)
  Pallas kernels  8.95 us (7%)
    all_to_all x2, blocking collectives, summed(): got = lax.all_to_all(pieces, axes, 0, 0)  43.8 us
    all_to_all x1, blocking collectives, summed(): return lax.all_to_all(copies, axes, 0, 0)  16.7 us
    ppermute x1, starting transfers between devices, swapped(): lax.ppermute(block, axis, [(i, i ^ distance) for i in range(lax.axis_size...  16.1 us
    ppermute x1, waiting for transfers between devices, shifted(): return lax.ppermute(block, axis, route)  10.8 us
    pallas_call x9, Pallas kernels, call(): pl.pallas_call(body, out_shape=[jax.ShapeDtypeStruct(s, t) for s, t in ou...  8.95 us
    all_to_all x1, waiting for transfers between devices, summed(): return lax.all_to_all(copies, axes, 0, 0)  8.35 us
    all_to_all x1, starting transfers between devices, summed(): return lax.all_to_all(copies, axes, 0, 0)  5.32 us
    all_to_all x1, starting transfers between devices, on_device(): got = lax.all_to_all(spread, 'tm', 0, 0)  3.86 us
  transfers between devices with their start and end apart: 4, of which 4 were waited for; matrix products, arithmetic and copies ran while one was open for 0% of the time, Pallas kernels for 3%

profile of v2, /device:TPU:1, one launch (start us, length us, event | category | flops | bytes accessed | tf_op | source)
XLA Modules:
  0.0 121.3 jit_solution(7255880354081895864)
XLA Ops:
  0.6 2.7 %shard_map.121 = (bf16[256,128]{1,0:T(8,128)(2,1)S(1)}, bf16[256,128]{1,0:T(8,128)(2,1)S(1)}, f32[256,2]{1,0:T(8,128)S(1)}, f32[2,256]{1,0:T(2,128)S(1)}, f32[25...) custom-call(s32[1]{0:T(128)} %bitcast.place, ...), custom_call_target="tpu_custom_call" | custom-call | flops 301989888 | tf_op jit(solution)/shard_map/pallas_call | solution.py:29
  3.4 16.1 %collective-permute-start.1 = (bf16[528,128]{1,0:T(8,128)(2,1)S(1)}, bf16[528,128]{1,0:T(8,128)(2,1)S(1)}, u32[]{:S(2)}, u32[]{:S(2)}) collective-permute-start(bf16[528,128]{1,0:T(8,128)(2,1)S(1)} %get-tuple-element.28), channel_id=1, source_target_pairs={{0,64},{64,0},{128,192},{192,128},{256,320},{320,256},{384,448},{4... | collective-permute-start | bytes 405512 | tf_op jit(solution)/shard_map/ppermute | solution.py:290
  19.4 1.0 collective-permute-done.1.got.pair
  20.4 0.9 shard_map.123
  21.3 0.0 copy-start.2
  21.3 0.0 copy-start.3
  21.3 3.9 %all-to-all-start = ((bf16[16,144,128]{2,1,0:T(8,128)(2,1)}), bf16[16,144,128]{2,1,0:T(8,128)(2,1)S(1)}, u32[]{:S(2)}, u32[]{:S(2)}) async-start(bf16[16,144,128]{2,1,0:T(8,128)(2,1)} %shard_map.123), calls=%async_computation | async-start | bytes 1179648 | tf_op jit(solution)/shard_map/all_to_all | solution.py:344
  25.1 0.0 copy-done.2
  25.2 0.0 copy-done.3
  25.2 0.0 copy-start.4
  25.2 0.0 copy-start
  25.2 0.0 copy-start.1
  25.2 3.7 %collective-permute-start = (bf16[128,512]{1,0:T(8,128)(2,1)S(1)}, bf16[128,512]{1,0:T(8,128)(2,1)S(1)}, u32[]{:S(2)}, u32[]{:S(2)}) collective-permute-start(bf16[128,512]{1,0:T(8,128)(2,1)S(1)} %pad_maximum_fusion), channel_id=1, source_target_pairs={{0,64},{64,128},{128,192},{192,256},{256,320},{320,384},{384,448},... | collective-permute-start | bytes 393224 | tf_op jit(solution)/shard_map/ppermute | solution.py:286
  28.9 10.8 %collective-permute-done.tail = bf16[128,512]{1,0:T(8,128)(2,1)S(1)} collective-permute-done((bf16[128,512]{1,0:T(8,128)(2,1)S(1)}, bf16[128,512]{1,0:T(8,128)(2,1)S(1)}, u32[]{:S(2)}, u32[]{:S(2)}) %collective-permute-start) | collective-permute-done | bytes 131104 | tf_op jit(solution)/shard_map/ppermute | solution.py:286
  39.8 0.0 copy-start.5
  39.8 0.0 copy-done.4
  39.8 0.0 copy-done
  39.8 0.0 copy-done.1
  39.8 0.6 copy-done.5
  40.4 2.1 %shard_map.122 = (f32[256,256]{1,0:T(8,128)S(1)}, f32[256,256]{1,0:T(8,128)S(1)}, f32[256,256]{1,0:T(8,128)S(1)}, f32[256,256]{1,0:T(8,128)S(1)}) custom-call(s32[1]{0:T(128)} %bitcast.6.place, s32[1,2]{1,0:T(1,128)S(1)} %copy-done.5, bf16[256,256]{1,0:T(8,128)(2,1)S(1)} %bitcast.25, bf16[256,256]{1,0:T(8,128)(2,1)S(1)} %bitcast.23, ...), custom_call_target="tpu_custom_call" | custom-call | flops 201326592 | tf_op jit(solution)/shard_map/pallas_call | solution.py:29
  42.5 1.3 %all-to-all-done.got = bf16[16,144,128]{2,1,0:T(8,128)(2,1)S(1)} async-done(((bf16[16,144,128]{2,1,0:T(8,128)(2,1)}), bf16[16,144,128]{2,1,0:T(8,128)(2,1)S(1)}, u32[]{:S(2)}, u32[]{:S(2)}) %all-to-all-start) | async-done | bytes 589856 | tf_op jit(solution)/shard_map/all_to_all | solution.py:344
  43.8 0.5 shard_map.124
  44.4 22.8 %all_to_all.25.got = bf16[16,16,256]{2,1,0:T(8,128)(2,1)S(1)} all-to-all(bf16[16,16,256]{2,1,0:T(8,128)(2,1)S(1)} %get-tuple-element.38), channel_id=1, replica_groups=mesh['tm'=16,'space'=16,'dp'=4] {'space'}, dimensions={0} | all-to-all | bytes 262144 | tf_op jit(solution)/shard_map/all_to_all | solution.py:294
  67.2 16.7 %all_to_all.26.both = bf16[16,16,256]{2,1,0:T(8,128)(2,1)S(1)} all-to-all(bf16[16,16,256]{2,1,0:T(8,128)(2,1)S(1)} %shard_map.126), channel_id=1, replica_groups=mesh['tm'=16,'space'=16,'dp'=4] {'space'}, dimensions={0} | all-to-all | bytes 262144 | tf_op jit(solution)/shard_map/all_to_all | solution.py:296
  83.9 0.2 shard_map.127
  84.1 21.0 %all_to_all.27.got = bf16[64,2,256]{2,1,0:T(2,128)(2,1)S(1)} all-to-all(bf16[64,2,256]{2,1,0:T(2,128)(2,1)S(1)} %shard_map.127), channel_id=1, replica_groups=mesh['tm'=16,'space'=16,'dp'=4] {'tm','dp'}, dimensions={0} | all-to-all | bytes 131072 | tf_op jit(solution)/shard_map/all_to_all | solution.py:294
  105.2 0.7 shard_map.128
  105.9 5.3 %all-to-all-start.4 = ((bf16[64,2,256]{2,1,0:T(2,128)(2,1)}), bf16[64,2,256]{2,1,0:T(2,128)(2,1)S(1)}, u32[]{:S(2)}, u32[]{:S(2)}) async-start(bf16[64,2,256]{2,1,0:T(2,128)(2,1)} %shard_map.128), calls=%async_computation.4 | async-start | bytes 131072 | tf_op jit(solution)/shard_map/all_to_all | solution.py:296
  111.2 1.0 shard_map.125
  112.2 8.3 %all-to-all-done.4.got = bf16[64,2,256]{2,1,0:T(2,128)(2,1)S(1)} async-done(((bf16[64,2,256]{2,1,0:T(2,128)(2,1)}), bf16[64,2,256]{2,1,0:T(2,128)(2,1)S(1)}, u32[]{:S(2)}, u32[]{:S(2)}) %all-to-all-start.4) | async-done | bytes 65568 | tf_op jit(solution)/shard_map/all_to_all | solution.py:296
  120.6 0.7 shard_map.129
  (3 shorter events, 0.0 us)
Async XLA Ops:
  3.4 17.0 %collective-permute-start.1 = (bf16[528,128]{1,0:T(8,128)(2,1)S(1)}, bf16[528,128]{1,0:T(8,128)(2,1)S(1)}, u32[]{:S(2)}, u32[]{:S(2)}) collective-permute-start(bf16[528,128]{1,0:T(8,128)(2,1)S(1)} %get-tuple-element.28), channel_id=1, source_target_pairs={{0,64},{64,0},{128,192},{192,128},{256,320},{320,256},{384,448},{4... | collective-permute-start | bytes 405512 | tf_op jit(solution)/shard_map/ppermute | solution.py:290
  21.3 3.9 %copy-start.2 = (bf16[1,256,256]{2,1,0:T(8,128)(2,1)S(1)}, bf16[1,256,256]{2,1,0:T(8,128)(2,1)}, u32[]{:S(2)}) copy-start(bf16[1,256,256]{2,1,0:T(8,128)(2,1)} %param.16) | copy-start | bytes 393220
  21.3 3.9 %copy-start.3 = (bf16[1,256,256]{2,1,0:T(8,128)(2,1)S(1)}, bf16[1,256,256]{2,1,0:T(8,128)(2,1)}, u32[]{:S(2)}) copy-start(bf16[1,256,256]{2,1,0:T(8,128)(2,1)} %param.17) | copy-start | bytes 393220
  21.3 22.5 %all-to-all-start = ((bf16[16,144,128]{2,1,0:T(8,128)(2,1)}), bf16[16,144,128]{2,1,0:T(8,128)(2,1)S(1)}, u32[]{:S(2)}, u32[]{:S(2)}) async-start(bf16[16,144,128]{2,1,0:T(8,128)(2,1)} %shard_map.123), calls=%async_computation | async-start | bytes 1179648 | tf_op jit(solution)/shard_map/all_to_all | solution.py:344
  25.2 14.6 %copy-start.4 = (bf16[1,256,256]{2,1,0:T(8,128)(2,1)S(1)}, bf16[1,256,256]{2,1,0:T(8,128)(2,1)}, u32[]{:S(2)}) copy-start(bf16[1,256,256]{2,1,0:T(8,128)(2,1)} %param.15) | copy-start | bytes 393220
  25.2 14.6 %copy-start = (bf16[1,256,256]{2,1,0:T(8,128)(2,1)S(1)}, bf16[1,256,256]{2,1,0:T(8,128)(2,1)}, u32[]{:S(2)}) copy-start(bf16[1,256,256]{2,1,0:T(8,128)(2,1)} %param.13) | copy-start | bytes 393220
  25.2 14.6 %copy-start.1 = (bf16[1,256,256]{2,1,0:T(8,128)(2,1)S(1)}, bf16[1,256,256]{2,1,0:T(8,128)(2,1)}, u32[]{:S(2)}) copy-start(bf16[1,256,256]{2,1,0:T(8,128)(2,1)} %param.18) | copy-start | bytes 393220
  25.2 14.5 %collective-permute-start = (bf16[128,512]{1,0:T(8,128)(2,1)S(1)}, bf16[128,512]{1,0:T(8,128)(2,1)S(1)}, u32[]{:S(2)}, u32[]{:S(2)}) collective-permute-start(bf16[128,512]{1,0:T(8,128)(2,1)S(1)} %pad_maximum_fusion), channel_id=1, source_target_pairs={{0,64},{64,128},{128,192},{192,256},{256,320},{320,384},{384,448},... | collective-permute-start | bytes 393224 | tf_op jit(solution)/shard_map/ppermute | solution.py:286
  39.8 0.7 copy-start.5
  105.9 14.7 %all-to-all-start.4 = ((bf16[64,2,256]{2,1,0:T(2,128)(2,1)}), bf16[64,2,256]{2,1,0:T(2,128)(2,1)S(1)}, u32[]{:S(2)}, u32[]{:S(2)}) async-start(bf16[64,2,256]{2,1,0:T(2,128)(2,1)} %shard_map.128), calls=%async_computation.4 | async-start | bytes 131072 | tf_op jit(solution)/shard_map/all_to_all | solution.py:296

commit v3 on v2

--- a/solution.py
+++ b/solution.py
@@ -137,11 +137,45 @@
         extra = jnp.where(row == part, value.astype(F32), extra)
     extra = extra.astype(BF16)
     for slot in range(slots):
-        send[slot, :hd, :] = jnp.where(slot // 2 > chip, f, b).astype(BF16)
+        send[slot, :hd, :] = jnp.where(slot > chip, f, b).astype(BF16)
         send[slot, hd:, :] = extra
 
 
-def attend(heads, qb, place, offsets, q, k, v, tail, out):
+def scan_body(place, got, pair, fwd, bwd, table, keep, send):
+    cols, n = fwd.shape
+    slots, hd, _ = got.shape
+    hd = hd - EXTRA
+    late = place[0] % 2
+    chip = place[0] // 2
+    early = late == 0
+    decays = [jnp.exp(totals_of(got.at[i], hd)) for i in range(slots)]
+    state = jnp.zeros((hd, n), F32)
+    grad = jnp.zeros((hd, n), F32)
+    for i in range(slots):
+        used = i < chip
+        state = jnp.where(used, decays[i], 1.0) * state
+        state = state + jnp.where(used, 1.0, 0.0) * got[i, :hd, :].astype(F32)
+    for i in reversed(range(slots)):
+        used = i > chip
+        grad = jnp.where(used, decays[i], 1.0) * grad
+        grad = grad + jnp.where(used, 1.0, 0.0) * got[i, :hd, :].astype(F32)
+    by_own = jnp.exp(jnp.where(early, table[0:1, :], table[1:2, :]))
+    by_theirs = jnp.exp(
+        jnp.where(early, totals_of(pair, 2 * cols), totals_of(pair, 2 * cols + 3))
+    )
+    at = pl.ds(pl.multiple_of(late * hd, hd), hd)
+    to = pl.ds(pl.multiple_of(cols + late * hd, hd), hd)
+    after = jnp.where(early, fwd[at, :], pair[at, :].astype(F32))
+    after = after + jnp.where(early, by_own, by_theirs) * state
+    before = jnp.where(early, pair[to, :].astype(F32), bwd[at, :])
+    before = before + jnp.where(early, by_theirs, by_own) * grad
+    keep[:hd, :] = jnp.where(early, state, after).astype(BF16)
+    keep[hd:, :] = jnp.where(early, before, grad).astype(BF16)
+    send[:hd, :] = jnp.where(early, after, state).astype(BF16)
+    send[hd:, :] = jnp.where(early, grad, before).astype(BF16)
+
+
+def attend_body(heads, qb, place, offsets, q, k, v, tail, out):
     rows = q.shape[0]
     hd = q.shape[1] // heads
     w = tail.shape[0]
@@ -170,9 +204,7 @@
             out[blk * qb : (blk + 1) * qb, at] = dot(probs, values, 1, 0)
 
 
-def middle_body(heads, qb, place, offsets, q, k, v, tail, x, cot, b, c, cumc, cumr, attended_out,
-                inner_out, gx_out, both_out):
-    attend(heads, qb, place, offsets, q, k, v, tail, attended_out)
+def local_body(heads, x, cot, b, c, cumc, cumr, inner_out, gx_out, both_out):
     rows = x.shape[0]
     hd = x.shape[1] // heads
     n = b.shape[1]
@@ -195,37 +227,19 @@
     both_out[:, n:] = dot(weigh, b[...], 1, 0)
 
 
-def grads_body(heads, place, got, pair, x, cot, cumc, both, out, enter_out, leave_out):
+def grads_body(heads, place, keep, got, x, cot, cumc, both, out, enter_out, leave_out):
     rows = x.shape[0]
     cols = x.shape[1]
     hd = cols // heads
-    slots, _, n = got.shape
+    n = keep.shape[1]
     scale = 1.0 / math.sqrt(n)
-    chip = place[0] // 2
-    early = place[0] % 2 == 0
     gb = both[:, :n]
     gc = both[:, n:]
     for h in range(heads):
         at = slice(h * hd, (h + 1) * hd)
-        decays = [jnp.exp(totals_of(got.at[2 * i + h], hd)) for i in range(slots // 2)]
-        state = jnp.zeros((hd, n), F32)
-        grad = jnp.zeros((hd, n), F32)
-        for i in range(slots // 2):
-            used = i < chip
-            state = jnp.where(used, decays[i], 1.0) * state + jnp.where(used, 1.0, 0.0) * got[
-                2 * i + h, :hd, :
-            ].astype(F32)
-        for i in reversed(range(slots // 2)):
-            used = i > chip
-            grad = jnp.where(used, decays[i], 1.0) * grad + jnp.where(used, 1.0, 0.0) * got[
-                2 * i + h, :hd, :
-            ].astype(F32)
-        by_theirs = jnp.exp(totals_of(pair, 2 * cols + 3 * h))
-        their_f = pair[at, :].astype(F32)
-        their_b = pair[cols + h * hd : cols + (h + 1) * hd, :].astype(F32)
-        state = jnp.where(early, 1.0, by_theirs) * state + jnp.where(early, 0.0, 1.0) * their_f
-        grad = jnp.where(early, by_theirs, 1.0) * grad + jnp.where(early, 1.0, 0.0) * their_b
-        state, grad = state.astype(BF16), grad.astype(BF16)
+        mine = place[0] % 2 == h
+        state = jnp.where(mine, keep[:hd, :].astype(F32), got[:hd, :].astype(F32)).astype(BF16)
+        grad = jnp.where(mine, keep[hd:, :].astype(F32), got[hd:, :].astype(F32)).astype(BF16)
         enter_out[at, :] = state
         leave_out[at, :] = grad
         cum = cumc[:, h : h + 1]
@@ -257,7 +271,8 @@
         input_grad[:, at] = g.astype(BF16)
 
 
-def gather_body(scale, got, out):
+def gather_body(scale, got, *rest):
+    out = rest[-1]
     total = got[0].astype(F32)
     for i in range(1, got.shape[0]):
         total = total + got[i].astype(F32)
@@ -290,9 +305,14 @@
     return lax.ppermute(block, axis, [(i, i ^ distance) for i in range(lax.axis_size(axis))])
 
 
-def summed(pieces, axes, scale=1.0):
+def summed(pieces, axes, scale=1.0, beside=()):
     got = lax.all_to_all(pieces, axes, 0, 0)
-    copies = call(functools.partial(gather_body, scale), [(pieces.shape, BF16)], (got,))[0]
+    copies = call(
+        functools.partial(gather_body, scale),
+        [(pieces.shape, BF16)],
+        (got, *(pltpu.with_memory_space_constraint(a, pltpu.HBM) for a in beside)),
+        [VMEM] + [HBM] * len(beside),
+    )[0]
     return lax.all_to_all(copies, axes, 0, 0)
 
 
@@ -326,27 +346,42 @@
         [pltpu.VMEM(a.shape, a.dtype) for a in inputs] + [pltpu.SemaphoreType.DMA((6,))],
         flops=2 * rows * width * 2 * n + 4 * rows * cols * n,
     )
-    attended, inner, gx, both = call(
-        functools.partial(middle_body, heads, QB),
-        [((rows, cols), F32), ((rows, cols), F32), ((rows, cols), F32), ((rows, 2 * n), F32)],
-        (me[None], window_offsets, q, k, v, tails, x, cot, b, c, cumc, cumr),
-        [SMEM, SMEM] + [VMEM] * 10,
-        flops=8 * rows * rows * cols + 4 * rows * 2 * W * cols,
-        transcendentals=rows * rows * heads + rows * 2 * W * heads,
+    attended = call(
+        functools.partial(attend_body, heads, QB),
+        [((rows, cols), F32)],
+        (me[None], window_offsets, q, k, v, tails),
+        [SMEM, SMEM] + [VMEM] * 4,
+        flops=4 * rows * 2 * W * cols,
+        transcendentals=rows * 2 * W * heads,
+    )[0]
+    inner, gx, both = call(
+        functools.partial(local_body, heads),
+        [((rows, cols), F32), ((rows, cols), F32), ((rows, 2 * n), F32)],
+        (x, cot, b, c, cumc, cumr),
+        flops=8 * rows * rows * cols,
+        transcendentals=rows * rows * heads,
     )
     pair = swapped(send, "tm", 1)
     spread = call(
         pair_body,
-        [((tm, hd + EXTRA, n), BF16)],
+        [((tm // 2, hd + EXTRA, n), BF16)],
         (me[None], pair, fwd, bwd, table),
         [SMEM] + [VMEM] * 4,
     )[0]
-    got = lax.all_to_all(spread, "tm", 0, 0)
+    same_core = [list(range(core, tm, 2)) for core in range(2)]
+    got = lax.all_to_all(spread, "tm", 0, 0, axis_index_groups=same_core)
+    keep, send = call(
+        scan_body,
+        [((2 * hd, n), BF16), ((2 * hd, n), BF16)],
+        (me[None], got, pair, fwd, bwd, table),
+        [SMEM] + [VMEM] * 5,
+    )
+    got = swapped(send, "tm", 1)
     space = lax.axis_size("space")
     both, enter, leave = call(
         functools.partial(grads_body, heads),
         [((space, rows // space, 2 * n), BF16), ((cols, n), BF16), ((cols, n), BF16)],
-        (me[None], got, pair, x, cot, cumc, both),
+        (me[None], keep, got, x, cot, cumc, both),
         [SMEM] + [VMEM] * 6,
         flops=4 * rows * cols * n,
     )
@@ -356,7 +391,7 @@
         (b, c, cumc, inner, gx, attended, enter, leave),
         flops=4 * rows * cols * n,
     )
-    both = summed(both, ("space",))
+    both = summed(both, ("space",), beside=(layer_out,))
     others = tm * lax.axis_size("dp")
     term = call(
         project_body,

time: 122 us -> 116 us (0.951)
  waiting for transfers between devices: 21.4 us -> 7.13 us
  blocking collectives: 60.6 us -> 67.3 us
  starting transfers between devices: 28.9 us -> 32 us
    all_to_all x2 -> x1, blocking collectives: 43.8 us -> 18.5 us  [summed(): got = lax.all_to_all(pieces, axes, 0, 0)]
    all_to_all x1 -> x2, blocking collectives: 16.7 us -> 33.8 us  [summed(): return lax.all_to_all(copies, axes, 0, 0)]
    all_to_all x0 -> x1, blocking collectives: none -> 15 us  [on_device(): got = lax.all_to_all(spread, 'tm', 0, 0, axis_index_groups=same_core)]
    ppermute x1, waiting for transfers between devices: 10.8 us -> 1.93 us  [shifted(): return lax.ppermute(block, axis, route)]
    all_to_all x2 -> x1, waiting for transfers between devices: 9.62 us -> 4.18 us  [summed(): got = lax.all_to_all(pieces, axes, 0, 0)]
    ppermute x1 -> x2, starting transfers between devices: 16.1 us -> 18.8 us  [swapped(): lax.ppermute(block, axis, [(i, i ^ distance) for i in range(lax.axis_size...]
    all_to_all x2 -> x1, starting transfers between devices: 9.18 us -> 10.3 us  [summed(): got = lax.all_to_all(pieces, axes, 0, 0)]
    pallas_call x9 -> x11, Pallas kernels: 8.95 us -> 8.15 us  [call(): pl.pallas_call(body, out_shape=[jax.ShapeDtypeStruct(s, t) for s, t in ou...]
where the time goes in v3:
time: 116 us
  blocking collectives  67.3 us (58%)
  starting transfers between devices  32 us (28%)
  Pallas kernels  8.15 us (7%)
  waiting for transfers between devices  7.13 us (6%)
    all_to_all x2, blocking collectives, summed(): return lax.all_to_all(copies, axes, 0, 0)  33.8 us
    ppermute x2, starting transfers between devices, swapped(): lax.ppermute(block, axis, [(i, i ^ distance) for i in range(lax.axis_size...  18.8 us
    all_to_all x1, blocking collectives, summed(): got = lax.all_to_all(pieces, axes, 0, 0)  18.5 us
    all_to_all x1, blocking collectives, on_device(): got = lax.all_to_all(spread, 'tm', 0, 0, axis_index_groups=same_core)  15 us
    all_to_all x1, starting transfers between devices, summed(): got = lax.all_to_all(pieces, axes, 0, 0)  10.3 us
    pallas_call x11, Pallas kernels, call(): pl.pallas_call(body, out_shape=[jax.ShapeDtypeStruct(s, t) for s, t in ou...  8.15 us
    all_to_all x1, waiting for transfers between devices, summed(): got = lax.all_to_all(pieces, axes, 0, 0)  4.18 us
    ppermute x1, starting transfers between devices, shifted(): return lax.ppermute(block, axis, route)  2.84 us
  transfers between devices with their start and end apart: 4, of which 4 were waited for; matrix products, arithmetic and copies ran while one was open for 0% of the time, Pallas kernels for 3%

profile of v3, /device:TPU:1, one launch (start us, length us, event | category | flops | bytes accessed | tf_op | source)
XLA Modules:
  0.0 116.0 jit_solution(15959538823143706984)
XLA Ops:
  0.6 2.7 %shard_map.121 = (bf16[256,128]{1,0:T(8,128)(2,1)S(1)}, bf16[256,128]{1,0:T(8,128)(2,1)S(1)}, f32[256,2]{1,0:T(8,128)S(1)}, f32[2,256]{1,0:T(2,128)S(1)}, f32[25...) custom-call(s32[1]{0:T(128)} %bitcast.place, ...), custom_call_target="tpu_custom_call" | custom-call | flops 301989888 | tf_op jit(solution)/shard_map/pallas_call | solution.py:29
  3.4 16.1 %collective-permute-start.1 = (bf16[528,128]{1,0:T(8,128)(2,1)S(1)}, bf16[528,128]{1,0:T(8,128)(2,1)S(1)}, u32[]{:S(2)}, u32[]{:S(2)}) collective-permute-start(bf16[528,128]{1,0:T(8,128)(2,1)S(1)} %get-tuple-element.28), channel_id=1, source_target_pairs={{0,64},{64,0},{128,192},{192,128},{256,320},{320,256},{384,448},{4... | collective-permute-start | bytes 405512 | tf_op jit(solution)/shard_map/ppermute | solution.py:305
  19.4 1.0 collective-permute-done.1.got.pair
  20.4 0.1 shard_map.124
  20.5 15.0 %all_to_all.25.got = bf16[8,144,128]{2,1,0:T(8,128)(2,1)S(1)} all-to-all(bf16[8,144,128]{2,1,0:T(8,128)(2,1)S(1)} %shard_map.124), channel_id=1, replica_groups={{0,128,256,384,512,640,768,896},{64,192,320,448,576,704,832,960},{1,129..., dimensions={0} | all-to-all | bytes 589824 | tf_op jit(solution)/shard_map/all_to_all | solution.py:372
  35.5 0.0 copy-start
  35.5 0.0 copy-start.1
  35.5 0.2 shard_map.125
  35.7 2.8 %collective-permute-start.2 = (bf16[256,128]{1,0:T(8,128)(2,1)S(1)}, bf16[256,128]{1,0:T(8,128)(2,1)S(1)}, u32[]{:S(2)}, u32[]{:S(2)}) collective-permute-start(bf16[256,128]{1,0:T(8,128)(2,1)S(1)} %get-tuple-element.33), channel_id=1, source_target_pairs={{0,64},{64,0},{128,192},{192,128},{256,320},{320,256},{384,448},{4... | collective-permute-start | bytes 196616 | tf_op jit(solution)/shard_map/ppermute | solution.py:305
  38.5 0.0 copy-done
  38.5 0.0 copy-done.1
  38.5 0.8 shard_map.122
  39.3 0.1 collective-permute-done.2.got
  39.4 0.9 shard_map.126
  40.3 0.0 copy-start.2
  40.3 0.0 copy-start.3
  40.3 10.3 %all-to-all-start.1 = ((bf16[16,16,256]{2,1,0:T(8,128)(2,1)}), bf16[16,16,256]{2,1,0:T(8,128)(2,1)S(1)}, u32[]{:S(2)}, u32[]{:S(2)}) async-start(bf16[16,16,256]{2,1,0:T(8,128)(2,1)} %get-tuple-element.40), calls=%async_computation.1 | async-start | bytes 262144 | tf_op jit(solution)/shard_map/all_to_all | solution.py:309
  50.6 0.0 copy-done.2
  50.6 0.0 copy-done.3
  50.6 0.0 copy-start.4
  50.7 2.8 %collective-permute-start = (bf16[128,512]{1,0:T(8,128)(2,1)S(1)}, bf16[128,512]{1,0:T(8,128)(2,1)S(1)}, u32[]{:S(2)}, u32[]{:S(2)}) collective-permute-start(bf16[128,512]{1,0:T(8,128)(2,1)S(1)} %pad_maximum_fusion), channel_id=1, source_target_pairs={{0,64},{64,128},{128,192},{192,256},{256,320},{320,384},{384,448},... | collective-permute-start | bytes 393224 | tf_op jit(solution)/shard_map/ppermute | solution.py:301
  53.5 1.9 %collective-permute-done.tail = bf16[128,512]{1,0:T(8,128)(2,1)S(1)} collective-permute-done((bf16[128,512]{1,0:T(8,128)(2,1)S(1)}, bf16[128,512]{1,0:T(8,128)(2,1)S(1)}, u32[]{:S(2)}, u32[]{:S(2)}) %collective-permute-start) | collective-permute-done | bytes 131104 | tf_op jit(solution)/shard_map/ppermute | solution.py:301
  55.4 0.0 copy-start.5
  55.4 0.0 copy-done.4
  55.4 0.7 copy-done.5
  56.1 1.4 %shard_map.123.attended = f32[256,256]{1,0:T(8,128)S(1)} custom-call(s32[1]{0:T(128)} %bitcast.6.place, s32[1,2]{1,0:T(1,128)S(1)} %copy-done.5, bf16[256,256]{1,0:T(8,128)(2,1)S(1)} %bitcast.25, bf16[256,256]{1,0:T(8,128)(2,1)S(1)} %bitcast.23, bf16[256,256]{1,0:T(8,128)(2,1)S(1)} %bitcast.24, bf16[128,512]{1,0:T(8,128)(2,1)S(1)} %collective-permute-done.tail), custom_call_target="tpu_custom_call" | custom-call | flops 67108864 | tf_op jit(solution)/shard_map/pallas_call | solution.py:29
  57.5 1.0 shard_map.127
  58.6 4.2 %all-to-all-done.1.got = bf16[16,16,256]{2,1,0:T(8,128)(2,1)S(1)} async-done(((bf16[16,16,256]{2,1,0:T(8,128)(2,1)}), bf16[16,16,256]{2,1,0:T(8,128)(2,1)S(1)}, u32[]{:S(2)}, u32[]{:S(2)}) %all-to-all-start.1) | async-done | bytes 131104 | tf_op jit(solution)/shard_map/all_to_all | solution.py:309
  62.8 19.9 %all_to_all.26.both = bf16[16,16,256]{2,1,0:T(8,128)(2,1)S(1)} all-to-all(bf16[16,16,256]{2,1,0:T(8,128)(2,1)S(1)} %shard_map.128), channel_id=1, replica_groups=mesh['tm'=16,'space'=16,'dp'=4] {'space'}, dimensions={0} | all-to-all | bytes 262144 | tf_op jit(solution)/shard_map/all_to_all | solution.py:316
  82.7 0.2 shard_map.129
  82.9 18.5 %all_to_all.27.got = bf16[64,2,256]{2,1,0:T(2,128)(2,1)S(1)} all-to-all(bf16[64,2,256]{2,1,0:T(2,128)(2,1)S(1)} %shard_map.129), channel_id=1, replica_groups=mesh['tm'=16,'space'=16,'dp'=4] {'tm','dp'}, dimensions={0} | all-to-all | bytes 131072 | tf_op jit(solution)/shard_map/all_to_all | solution.py:309
  101.3 0.1 shard_map.130
  101.4 13.9 %all_to_all.28.got = bf16[64,2,256]{2,1,0:T(2,128)(2,1)S(1)} all-to-all(bf16[64,2,256]{2,1,0:T(2,128)(2,1)S(1)} %shard_map.130), channel_id=1, replica_groups=mesh['tm'=16,'space'=16,'dp'=4] {'tm','dp'}, dimensions={0} | all-to-all | bytes 131072 | tf_op jit(solution)/shard_map/all_to_all | solution.py:316
  115.3 0.7 shard_map.131
  (3 shorter events, 0.0 us)
Async XLA Ops:
  3.4 17.0 %collective-permute-start.1 = (bf16[528,128]{1,0:T(8,128)(2,1)S(1)}, bf16[528,128]{1,0:T(8,128)(2,1)S(1)}, u32[]{:S(2)}, u32[]{:S(2)}) collective-permute-start(bf16[528,128]{1,0:T(8,128)(2,1)S(1)} %get-tuple-element.28), channel_id=1, source_target_pairs={{0,64},{64,0},{128,192},{192,128},{256,320},{320,256},{384,448},{4... | collective-permute-start | bytes 405512 | tf_op jit(solution)/shard_map/ppermute | solution.py:305
  35.5 3.0 %copy-start = (bf16[1,256,256]{2,1,0:T(8,128)(2,1)S(1)}, bf16[1,256,256]{2,1,0:T(8,128)(2,1)}, u32[]{:S(2)}) copy-start(bf16[1,256,256]{2,1,0:T(8,128)(2,1)} %param.13) | copy-start | bytes 393220
  35.5 3.0 %copy-start.1 = (bf16[1,256,256]{2,1,0:T(8,128)(2,1)S(1)}, bf16[1,256,256]{2,1,0:T(8,128)(2,1)}, u32[]{:S(2)}) copy-start(bf16[1,256,256]{2,1,0:T(8,128)(2,1)} %param.18) | copy-start | bytes 393220
  35.7 3.7 %collective-permute-start.2 = (bf16[256,128]{1,0:T(8,128)(2,1)S(1)}, bf16[256,128]{1,0:T(8,128)(2,1)S(1)}, u32[]{:S(2)}, u32[]{:S(2)}) collective-permute-start(bf16[256,128]{1,0:T(8,128)(2,1)S(1)} %get-tuple-element.33), channel_id=1, source_target_pairs={{0,64},{64,0},{128,192},{192,128},{256,320},{320,256},{384,448},{4... | collective-permute-start | bytes 196616 | tf_op jit(solution)/shard_map/ppermute | solution.py:305
  40.3 10.3 %copy-start.2 = (bf16[1,256,256]{2,1,0:T(8,128)(2,1)S(1)}, bf16[1,256,256]{2,1,0:T(8,128)(2,1)}, u32[]{:S(2)}) copy-start(bf16[1,256,256]{2,1,0:T(8,128)(2,1)} %param.16) | copy-start | bytes 393220
  40.3 10.3 %copy-start.3 = (bf16[1,256,256]{2,1,0:T(8,128)(2,1)S(1)}, bf16[1,256,256]{2,1,0:T(8,128)(2,1)}, u32[]{:S(2)}) copy-start(bf16[1,256,256]{2,1,0:T(8,128)(2,1)} %param.17) | copy-start | bytes 393220
  40.3 22.5 %all-to-all-start.1 = ((bf16[16,16,256]{2,1,0:T(8,128)(2,1)}), bf16[16,16,256]{2,1,0:T(8,128)(2,1)S(1)}, u32[]{:S(2)}, u32[]{:S(2)}) async-start(bf16[16,16,256]{2,1,0:T(8,128)(2,1)} %get-tuple-element.40), calls=%async_computation.1 | async-start | bytes 262144 | tf_op jit(solution)/shard_map/all_to_all | solution.py:309
  50.6 4.8 %copy-start.4 = (bf16[1,256,256]{2,1,0:T(8,128)(2,1)S(1)}, bf16[1,256,256]{2,1,0:T(8,128)(2,1)}, u32[]{:S(2)}) copy-start(bf16[1,256,256]{2,1,0:T(8,128)(2,1)} %param.15) | copy-start | bytes 393220
  50.7 4.8 %collective-permute-start = (bf16[128,512]{1,0:T(8,128)(2,1)S(1)}, bf16[128,512]{1,0:T(8,128)(2,1)S(1)}, u32[]{:S(2)}, u32[]{:S(2)}) collective-permute-start(bf16[128,512]{1,0:T(8,128)(2,1)S(1)} %pad_maximum_fusion), channel_id=1, source_target_pairs={{0,64},{64,128},{128,192},{192,256},{256,320},{320,384},{384,448},... | collective-permute-start | bytes 393224 | tf_op jit(solution)/shard_map/ppermute | solution.py:301
  55.4 0.7 copy-start.5

commit v4 on v3

--- a/solution.py
+++ b/solution.py
@@ -17,6 +17,7 @@
 SMEM = pl.BlockSpec(memory_space=pltpu.SMEM)
 NEG = -1e30
 EXTRA = 16
+CHUNKS = 4
 
 
 def dot(a, b, left, right, precision=None):
@@ -56,15 +57,23 @@
 
 
 def pre_body(heads, place, lat_in, wb_in, wc_in, x_in, cot_in, ld_in, b_out, c_out, cumc_out, cumr_out,
-             fresh_out, back_out, table_out, send, mine_out, lat, wb, wc, x, cot, ld, sems):
-    pairs = ((ld_in, ld), (lat_in, lat), (wb_in, wb), (wc_in, wc), (x_in, x), (cot_in, cot))
+             fresh_out, back_out, table_out, send, mine_out, lat, w, x, cot, ld, sems):
+    n = wb_in.shape[1]
+    chunks = CHUNKS
+    deep = lat.shape[1] // chunks
+    pairs = [(ld_in, ld)]
+    for i in range(chunks):
+        part = slice(i * deep, (i + 1) * deep)
+        pairs.append((wb_in.at[part, :], w.at[part, :n]))
+        pairs.append((wc_in.at[part, :], w.at[part, n:]))
+        pairs.append((lat_in.at[:, part], lat.at[:, part]))
+    pairs += [(x_in, x), (cot_in, cot)]
     copies = [pltpu.make_async_copy(src, dst, sems.at[i]) for i, (src, dst) in enumerate(pairs)]
     for copy in copies:
         copy.start()
     rows = lat.shape[0]
     cols = x.shape[1]
     hd = cols // heads
-    n = wb.shape[1]
     scale = 1.0 / math.sqrt(n)
     t = lax.broadcasted_iota(jnp.int32, (rows, rows), 0)
     s = lax.broadcasted_iota(jnp.int32, (rows, rows), 1)
@@ -83,17 +92,21 @@
         totals.append(jnp.broadcast_to(total[:, h : h + 1], (1, n)))
         table_out[h : h + 1, :] = totals[h]
     put_totals(send, 2 * cols, totals)
-    copies[1].wait()
+    projected = None
+    for i in range(chunks):
+        for copy in copies[1 + 3 * i : 4 + 3 * i]:
+            copy.wait()
+        part = slice(i * deep, (i + 1) * deep)
+        one = dot(lat[:, part], w[part, :], 1, 0)
+        projected = one if projected is None else projected + one
+    b = projected[:, :n].astype(BF16)
+    c = projected[:, n:].astype(BF16)
+    b_out[...] = b
+    c_out[...] = c
+    for copy in copies[-2:]:
+        copy.wait()
     share = mine_out.shape[1]
     mine_out[...] = lat[:, pl.ds(pl.multiple_of(place[0] * share, share), share)]
-    copies[2].wait()
-    b = dot(lat[...], wb[...], 1, 0).astype(BF16)
-    b_out[...] = b
-    copies[3].wait()
-    c = dot(lat[...], wc[...], 1, 0).astype(BF16)
-    c_out[...] = c
-    copies[4].wait()
-    copies[5].wait()
     for h in range(heads):
         at = slice(h * hd, (h + 1) * hd)
         xs = (x[:, at].astype(F32) * tail[:, h : h + 1]).astype(BF16)
@@ -113,7 +126,7 @@
     return total
 
 
-def pair_body(place, got, fwd, bwd, table, send):
+def pair_body(place, got, fwd, bwd, table, _, send):
     cols, n = fwd.shape
     slots, hd, _ = send.shape
     hd = hd - EXTRA
@@ -175,36 +188,42 @@
     send[hd:, :] = jnp.where(early, grad, before).astype(BF16)
 
 
-def attend_body(heads, qb, place, offsets, q, k, v, tail, out):
+def attend_body(heads, qb, place, offsets_in, q, k, v, tail, out, offsets, sem):
+    copy = pltpu.make_async_copy(offsets_in, offsets, sem)
+    copy.start()
     rows = q.shape[0]
     hd = q.shape[1] // heads
     w = tail.shape[0]
     scale = 1.0 / math.sqrt(hd)
     i = lax.broadcasted_iota(jnp.int32, (qb, qb + w), 0)
     u = lax.broadcasted_iota(jnp.int32, (qb, qb + w), 1)
-    for blk in range(rows // qb):
-        off = offsets[0, blk]
-        seen = (u <= i + w) & (u >= i + 1 + off)
+
+    def window(own, blk, at, behind):
+        if blk == 0:
+            return jnp.concatenate([tail[:, behind], own[:qb, at]], axis=0)
+        return own[blk * qb - w : (blk + 1) * qb, at]
+
+    places = [(blk, h) for blk in range(rows // qb) for h in range(heads)]
+    scores = []
+    for blk, h in places:
+        at = slice(h * hd, (h + 1) * hd)
+        keys = window(k, blk, at, at)
+        scores.append(dot(q[blk * qb : (blk + 1) * qb, at], keys, 1, 1) * scale)
+    copy.wait()
+    for (blk, h), score in zip(places, scores):
+        at = slice(h * hd, (h + 1) * hd)
+        seen = (u <= i + w) & (u >= i + 1 + offsets[0, blk])
         if blk == 0:
             seen = seen & ((u >= w) | (place[0] > 0))
-        for h in range(heads):
-            at = slice(h * hd, (h + 1) * hd)
-            if blk == 0:
-                keys = jnp.concatenate([tail[:, at], k[:qb, at]], axis=0)
-                values = jnp.concatenate(
-                    [tail[:, heads * hd + h * hd : heads * hd + (h + 1) * hd], v[:qb, at]], axis=0
-                )
-            else:
-                keys = k[blk * qb - w : (blk + 1) * qb, at]
-                values = v[blk * qb - w : (blk + 1) * qb, at]
-            scores = dot(q[blk * qb : (blk + 1) * qb, at], keys, 1, 1) * scale
-            scores = jnp.where(seen, scores, NEG)
-            expo = jnp.exp(scores - jnp.max(scores, axis=-1, keepdims=True))
-            probs = (expo / jnp.sum(expo, axis=-1, keepdims=True)).astype(BF16)
-            out[blk * qb : (blk + 1) * qb, at] = dot(probs, values, 1, 0)
-
-
-def local_body(heads, x, cot, b, c, cumc, cumr, inner_out, gx_out, both_out):
+        score = jnp.where(seen, score, NEG)
+        expo = jnp.exp(score - jnp.max(score, axis=-1, keepdims=True))
+        probs = (expo / jnp.sum(expo, axis=-1, keepdims=True)).astype(BF16)
+        values = window(v, blk, at, slice((heads + h) * hd, (heads + h + 1) * hd))
+        out[blk * qb : (blk + 1) * qb, at] = dot(probs, values, 1, 0)
+
+
+def local_body(heads, x, cot, b, c, cumc, cumr, inner_out, gx_out, both_out, token):
+    token[...] = jnp.zeros_like(token)
     rows = x.shape[0]
     hd = x.shape[1] // heads
     n = b.shape[1]
@@ -305,15 +324,28 @@
     return lax.ppermute(block, axis, [(i, i ^ distance) for i in range(lax.axis_size(axis))])
 
 
-def summed(pieces, axes, scale=1.0, beside=()):
-    got = lax.all_to_all(pieces, axes, 0, 0)
-    copies = call(
+def gathered(scale, got, copies, beside=()):
+    return call(
         functools.partial(gather_body, scale),
-        [(pieces.shape, BF16)],
+        [((copies, *got.shape[1:]), BF16)],
         (got, *(pltpu.with_memory_space_constraint(a, pltpu.HBM) for a in beside)),
         [VMEM] + [HBM] * len(beside),
     )[0]
-    return lax.all_to_all(copies, axes, 0, 0)
+
+
+def summed(pieces, axes, scale=1.0):
+    got = lax.all_to_all(pieces, axes, 0, 0)
+    return lax.all_to_all(gathered(scale, got, pieces.shape[0]), axes, 0, 0)
+
+
+def summed_in_groups(pieces, axis, beside):
+    near = pieces.shape[0]
+    far = lax.axis_size(axis) // near
+    inside = [[near * g + i for i in range(near)] for g in range(far)]
+    across = [[i + near * g for g in range(far)] for i in range(near)]
+    got = lax.all_to_all(pieces, axis, 0, 0, axis_index_groups=inside)
+    got = lax.all_to_all(gathered(1.0, got, far), axis, 0, 0, axis_index_groups=across)
+    return lax.all_to_all(gathered(1.0, got, near, beside), axis, 0, 0, axis_index_groups=inside)
 
 
 def on_device(latents, proj_input, proj_output, scan_input, log_decay, att_queries, att_keys,
@@ -343,20 +375,28 @@
          ((24, n), F32), wire, ((rows, share), BF16)],
         (lax.axis_index("space")[None], *inputs),
         [SMEM] + [HBM] * 6,
-        [pltpu.VMEM(a.shape, a.dtype) for a in inputs] + [pltpu.SemaphoreType.DMA((6,))],
+        [
+            pltpu.VMEM((rows, width), BF16),
+            pltpu.VMEM((width, 2 * n), BF16),
+            pltpu.VMEM((rows, cols), BF16),
+            pltpu.VMEM((rows, cols), BF16),
+            pltpu.VMEM((heads, rows), F32),
+            pltpu.SemaphoreType.DMA((3 * CHUNKS + 3,)),
+        ],
         flops=2 * rows * width * 2 * n + 4 * rows * cols * n,
     )
     attended = call(
         functools.partial(attend_body, heads, QB),
         [((rows, cols), F32)],
-        (me[None], window_offsets, q, k, v, tails),
-        [SMEM, SMEM] + [VMEM] * 4,
+        (me[None], pltpu.with_memory_space_constraint(window_offsets, pltpu.HBM), q, k, v, tails),
+        [SMEM, HBM] + [VMEM] * 4,
+        [pltpu.SMEM(window_offsets.shape, jnp.int32), pltpu.SemaphoreType.DMA],
         flops=4 * rows * 2 * W * cols,
         transcendentals=rows * 2 * W * heads,
     )[0]
-    inner, gx, both = call(
+    inner, gx, both, token = call(
         functools.partial(local_body, heads),
-        [((rows, cols), F32), ((rows, cols), F32), ((rows, 2 * n), F32)],
+        [((rows, cols), F32), ((rows, cols), F32), ((rows, 2 * n), F32), ((8, n), F32)],
         (x, cot, b, c, cumc, cumr),
         flops=8 * rows * rows * cols,
         transcendentals=rows * rows * heads,
@@ -365,8 +405,8 @@
     spread = call(
         pair_body,
         [((tm // 2, hd + EXTRA, n), BF16)],
-        (me[None], pair, fwd, bwd, table),
-        [SMEM] + [VMEM] * 4,
+        (me[None], pair, fwd, bwd, table, token),
+        [SMEM] + [VMEM] * 5,
     )[0]
     same_core = [list(range(core, tm, 2)) for core in range(2)]
     got = lax.all_to_all(spread, "tm", 0, 0, axis_index_groups=same_core)
@@ -377,10 +417,10 @@
         [SMEM] + [VMEM] * 5,
     )
     got = swapped(send, "tm", 1)
-    space = lax.axis_size("space")
+    near = math.gcd(lax.axis_size("space"), 4)
     both, enter, leave = call(
         functools.partial(grads_body, heads),
-        [((space, rows // space, 2 * n), BF16), ((cols, n), BF16), ((cols, n), BF16)],
+        [((near, rows // near, 2 * n), BF16), ((cols, n), BF16), ((cols, n), BF16)],
         (me[None], keep, got, x, cot, cumc, both),
         [SMEM] + [VMEM] * 6,
         flops=4 * rows * cols * n,
@@ -391,7 +431,7 @@
         (b, c, cumc, inner, gx, attended, enter, leave),
         flops=4 * rows * cols * n,
     )
-    both = summed(both, ("space",), beside=(layer_out,))
+    both = summed_in_groups(both, "space", (layer_out,))
     others = tm * lax.axis_size("dp")
     term = call(
         project_body,

time: 116 us -> 114 us (0.983)
  blocking collectives: 67.3 us -> 63.3 us
  starting transfers between devices: 32 us -> 35.2 us
    all_to_all x2 -> x3, blocking collectives: 33.8 us -> 29.2 us  [the longest x1 13.9 us: summed(): return lax.all_to_all(gathered(scale, got, pieces.shape[0]), axes, 0, 0)]
    ppermute x1, starting transfers between devices: 2.84 us -> 4.57 us  [shifted(): return lax.ppermute(block, axis, route)]
    all_to_all x1, starting transfers between devices: 10.3 us -> 11.8 us  [summed_in_groups(): lax.all_to_all(gathered(1.0, got, far), axis, 0, 0, axis_index_groups=acr...]
    pallas_call x11 -> x12, Pallas kernels: 8.15 us -> 7.99 us  [call(): pl.pallas_call(body, out_shape=[jax.ShapeDtypeStruct(s, t) for s, t in ou...]
where the time goes in v4:
time: 114 us
  blocking collectives  63.3 us (56%)
  starting transfers between devices  35.2 us (31%)
  Pallas kernels  7.99 us (7%)
  waiting for transfers between devices  6.42 us (6%)
    all_to_all x1, blocking collectives, summed(): got = lax.all_to_all(pieces, axes, 0, 0)  19.1 us
    ppermute x2, starting transfers between devices, swapped(): lax.ppermute(block, axis, [(i, i ^ distance) for i in range(lax.axis_size...  18.8 us
    all_to_all x1, blocking collectives, on_device(): got = lax.all_to_all(spread, 'tm', 0, 0, axis_index_groups=same_core)  15 us
    all_to_all x1, blocking collectives, summed(): return lax.all_to_all(gathered(scale, got, pieces.shape[0]), axes, 0, 0)  13.9 us
    all_to_all x1, starting transfers between devices, summed_in_groups(): lax.all_to_all(gathered(1.0, got, far), axis, 0, 0, axis_index_groups=acr...  11.8 us
    all_to_all x1, blocking collectives, summed_in_groups(): lax.all_to_all(gathered(1.0, got, near, beside), axis, 0, 0, axis_index_g...  8.06 us
    pallas_call x12, Pallas kernels, call(): pl.pallas_call(body, out_shape=[jax.ShapeDtypeStruct(s, t) for s, t in ou...  7.99 us
    all_to_all x1, blocking collectives, summed_in_groups(): got = lax.all_to_all(pieces, axis, 0, 0, axis_index_groups=inside)  7.27 us
  transfers between devices with their start and end apart: 4, of which 4 were waited for; matrix products, arithmetic and copies ran while one was open for 0% of the time, Pallas kernels for 3%

profile of v4, /device:TPU:1, one launch (start us, length us, event | category | flops | bytes accessed | tf_op | source)
XLA Modules:
  0.0 113.8 jit_solution(12366365622761029982)
XLA Ops:
  0.6 0.0 copy-start
  0.6 0.0 copy-start.1
  0.7 2.9 %shard_map.121 = (bf16[256,128]{1,0:T(8,128)(2,1)S(1)}, bf16[256,128]{1,0:T(8,128)(2,1)S(1)}, f32[256,2]{1,0:T(8,128)S(1)}, f32[2,256]{1,0:T(2,128)S(1)}, f32[25...) custom-call(s32[1]{0:T(128)} %bitcast.place, ...), custom_call_target="tpu_custom_call" | custom-call | flops 301989888 | tf_op jit(solution)/shard_map/pallas_call | solution.py:30
  3.6 16.1 %collective-permute-start.1 = (bf16[528,128]{1,0:T(8,128)(2,1)S(1)}, bf16[528,128]{1,0:T(8,128)(2,1)S(1)}, u32[]{:S(2)}, u32[]{:S(2)}) collective-permute-start(bf16[528,128]{1,0:T(8,128)(2,1)S(1)} %get-tuple-element.29), channel_id=1, source_target_pairs={{0,64},{64,0},{128,192},{192,128},{256,320},{320,256},{384,448},{4... | collective-permute-start | bytes 405512 | tf_op jit(solution)/shard_map/ppermute | solution.py:324
  19.6 0.0 copy-done
  19.6 0.0 copy-done.1
  19.7 0.8 shard_map.122
  20.5 0.1 collective-permute-done.1.got.pair
  20.6 0.1 shard_map.124
  20.7 15.0 %all_to_all.30.got = bf16[8,144,128]{2,1,0:T(8,128)(2,1)S(1)} all-to-all(bf16[8,144,128]{2,1,0:T(8,128)(2,1)S(1)} %shard_map.124), channel_id=1, replica_groups={{0,128,256,384,512,640,768,896},{64,192,320,448,576,704,832,960},{1,129..., dimensions={0} | all-to-all | bytes 589824 | tf_op jit(solution)/shard_map/all_to_all | solution.py:412
  35.7 0.2 shard_map.125
  35.9 2.8 %collective-permute-start.2 = (bf16[256,128]{1,0:T(8,128)(2,1)S(1)}, bf16[256,128]{1,0:T(8,128)(2,1)S(1)}, u32[]{:S(2)}, u32[]{:S(2)}) collective-permute-start(bf16[256,128]{1,0:T(8,128)(2,1)S(1)} %get-tuple-element.35), channel_id=1, source_target_pairs={{0,64},{64,0},{128,192},{192,128},{256,320},{320,256},{384,448},{4... | collective-permute-start | bytes 196616 | tf_op jit(solution)/shard_map/ppermute | solution.py:324
  38.7 0.9 collective-permute-done.2.got
  39.6 0.2 shard_map.126
  39.8 7.3 %all_to_all.31.got = bf16[4,64,256]{2,1,0:T(8,128)(2,1)S(1)} all-to-all(bf16[4,64,256]{2,1,0:T(8,128)(2,1)S(1)} %get-tuple-element.42), channel_id=1, replica_groups={{0,4,8,12},{16,20,24,28},{32,36,40,44},{48,52,56,60},{1,5,9,13},{17,21,..., dimensions={0} | all-to-all | bytes 262144 | tf_op jit(solution)/shard_map/all_to_all | solution.py:346
  47.1 0.7 shard_map.128
  47.7 0.0 copy-start.2
  47.8 0.0 copy-start.3
  47.8 11.8 %all-to-all-start.2 = ((bf16[4,64,256]{2,1,0:T(8,128)(2,1)}), bf16[4,64,256]{2,1,0:T(8,128)(2,1)S(1)}, u32[]{:S(2)}, u32[]{:S(2)}) async-start(bf16[4,64,256]{2,1,0:T(8,128)(2,1)} %shard_map.128), calls=%async_computation.2 | async-start | bytes 262144 | tf_op jit(solution)/shard_map/all_to_all | solution.py:347
  59.5 0.0 copy-done.2
  59.5 0.0 copy-done.3
  59.5 0.0 copy-start.4
  59.6 4.6 %collective-permute-start = (bf16[128,512]{1,0:T(8,128)(2,1)S(1)}, bf16[128,512]{1,0:T(8,128)(2,1)S(1)}, u32[]{:S(2)}, u32[]{:S(2)}) collective-permute-start(bf16[128,512]{1,0:T(8,128)(2,1)S(1)} %pad_maximum_fusion), channel_id=1, source_target_pairs={{0,64},{64,128},{128,192},{192,256},{256,320},{320,384},{384,448},... | collective-permute-start | bytes 393224 | tf_op jit(solution)/shard_map/ppermute | solution.py:320
  64.2 1.9 %collective-permute-done.tail = bf16[128,512]{1,0:T(8,128)(2,1)S(1)} collective-permute-done((bf16[128,512]{1,0:T(8,128)(2,1)S(1)}, bf16[128,512]{1,0:T(8,128)(2,1)S(1)}, u32[]{:S(2)}, u32[]{:S(2)}) %collective-permute-start) | collective-permute-done | bytes 131104 | tf_op jit(solution)/shard_map/ppermute | solution.py:320
  66.1 0.0 copy-done.4
  66.1 1.1 shard_map.123.attended
  67.2 1.0 shard_map.127
  68.2 3.5 %all-to-all-done.2.got = bf16[4,64,256]{2,1,0:T(8,128)(2,1)S(1)} async-done(((bf16[4,64,256]{2,1,0:T(8,128)(2,1)}), bf16[4,64,256]{2,1,0:T(8,128)(2,1)S(1)}, u32[]{:S(2)}, u32[]{:S(2)}) %all-to-all-start.2) | async-done | bytes 131104 | tf_op jit(solution)/shard_map/all_to_all | solution.py:347
  71.7 8.1 %all_to_all.32.both = bf16[4,64,256]{2,1,0:T(8,128)(2,1)S(1)} all-to-all(bf16[4,64,256]{2,1,0:T(8,128)(2,1)S(1)} %shard_map.129), channel_id=1, replica_groups={{0,4,8,12},{16,20,24,28},{32,36,40,44},{48,52,56,60},{1,5,9,13},{17,21,..., dimensions={0} | all-to-all | bytes 262144 | tf_op jit(solution)/shard_map/all_to_all | solution.py:348
  79.8 0.2 shard_map.130
  80.0 19.1 %all_to_all.33.got = bf16[64,2,256]{2,1,0:T(2,128)(2,1)S(1)} all-to-all(bf16[64,2,256]{2,1,0:T(2,128)(2,1)S(1)} %shard_map.130), channel_id=1, replica_groups=mesh['tm'=16,'space'=16,'dp'=4] {'tm','dp'}, dimensions={0} | all-to-all | bytes 131072 | tf_op jit(solution)/shard_map/all_to_all | solution.py:337
  99.1 0.1 shard_map.131
  99.2 13.9 %all_to_all.34.got = bf16[64,2,256]{2,1,0:T(2,128)(2,1)S(1)} all-to-all(bf16[64,2,256]{2,1,0:T(2,128)(2,1)S(1)} %shard_map.131), channel_id=1, replica_groups=mesh['tm'=16,'space'=16,'dp'=4] {'tm','dp'}, dimensions={0} | all-to-all | bytes 131072 | tf_op jit(solution)/shard_map/all_to_all | solution.py:338
  113.0 0.7 shard_map.132
  (3 shorter events, 0.0 us)
Async XLA Ops:
  0.6 19.0 %copy-start = (bf16[1,256,256]{2,1,0:T(8,128)(2,1)S(1)}, bf16[1,256,256]{2,1,0:T(8,128)(2,1)}, u32[]{:S(2)}) copy-start(bf16[1,256,256]{2,1,0:T(8,128)(2,1)} %param.13) | copy-start | bytes 393220
  0.6 19.0 %copy-start.1 = (bf16[1,256,256]{2,1,0:T(8,128)(2,1)S(1)}, bf16[1,256,256]{2,1,0:T(8,128)(2,1)}, u32[]{:S(2)}) copy-start(bf16[1,256,256]{2,1,0:T(8,128)(2,1)} %param.18) | copy-start | bytes 393220
  3.6 17.0 %collective-permute-start.1 = (bf16[528,128]{1,0:T(8,128)(2,1)S(1)}, bf16[528,128]{1,0:T(8,128)(2,1)S(1)}, u32[]{:S(2)}, u32[]{:S(2)}) collective-permute-start(bf16[528,128]{1,0:T(8,128)(2,1)S(1)} %get-tuple-element.29), channel_id=1, source_target_pairs={{0,64},{64,0},{128,192},{192,128},{256,320},{320,256},{384,448},{4... | collective-permute-start | bytes 405512 | tf_op jit(solution)/shard_map/ppermute | solution.py:324
  35.9 3.7 %collective-permute-start.2 = (bf16[256,128]{1,0:T(8,128)(2,1)S(1)}, bf16[256,128]{1,0:T(8,128)(2,1)S(1)}, u32[]{:S(2)}, u32[]{:S(2)}) collective-permute-start(bf16[256,128]{1,0:T(8,128)(2,1)S(1)} %get-tuple-element.35), channel_id=1, source_target_pairs={{0,64},{64,0},{128,192},{192,128},{256,320},{320,256},{384,448},{4... | collective-permute-start | bytes 196616 | tf_op jit(solution)/shard_map/ppermute | solution.py:324
  47.7 11.8 %copy-start.2 = (bf16[1,256,256]{2,1,0:T(8,128)(2,1)S(1)}, bf16[1,256,256]{2,1,0:T(8,128)(2,1)}, u32[]{:S(2)}) copy-start(bf16[1,256,256]{2,1,0:T(8,128)(2,1)} %param.16) | copy-start | bytes 393220
  47.8 11.8 %copy-start.3 = (bf16[1,256,256]{2,1,0:T(8,128)(2,1)S(1)}, bf16[1,256,256]{2,1,0:T(8,128)(2,1)}, u32[]{:S(2)}) copy-start(bf16[1,256,256]{2,1,0:T(8,128)(2,1)} %param.17) | copy-start | bytes 393220
  47.8 23.9 %all-to-all-start.2 = ((bf16[4,64,256]{2,1,0:T(8,128)(2,1)}), bf16[4,64,256]{2,1,0:T(8,128)(2,1)S(1)}, u32[]{:S(2)}, u32[]{:S(2)}) async-start(bf16[4,64,256]{2,1,0:T(8,128)(2,1)} %shard_map.128), calls=%async_computation.2 | async-start | bytes 262144 | tf_op jit(solution)/shard_map/all_to_all | solution.py:347
  59.5 6.5 %copy-start.4 = (bf16[1,256,256]{2,1,0:T(8,128)(2,1)S(1)}, bf16[1,256,256]{2,1,0:T(8,128)(2,1)}, u32[]{:S(2)}) copy-start(bf16[1,256,256]{2,1,0:T(8,128)(2,1)} %param.15) | copy-start | bytes 393220
  59.6 6.5 %collective-permute-start = (bf16[128,512]{1,0:T(8,128)(2,1)S(1)}, bf16[128,512]{1,0:T(8,128)(2,1)S(1)}, u32[]{:S(2)}, u32[]{:S(2)}) collective-permute-start(bf16[128,512]{1,0:T(8,128)(2,1)S(1)} %pad_maximum_fusion), channel_id=1, source_target_pairs={{0,64},{64,128},{128,192},{192,256},{256,320},{320,384},{384,448},... | collective-permute-start | bytes 393224 | tf_op jit(solution)/shard_map/ppermute | solution.py:320

commit v5 on v4

--- a/solution.py
+++ b/solution.py
@@ -17,7 +17,7 @@
 SMEM = pl.BlockSpec(memory_space=pltpu.SMEM)
 NEG = -1e30
 EXTRA = 16
-CHUNKS = 4
+CHUNKS = 2
 
 
 def dot(a, b, left, right, precision=None):
@@ -61,13 +61,12 @@
     n = wb_in.shape[1]
     chunks = CHUNKS
     deep = lat.shape[1] // chunks
-    pairs = [(ld_in, ld)]
+    pairs = [(ld_in, ld), (x_in, x), (cot_in, cot)]
     for i in range(chunks):
         part = slice(i * deep, (i + 1) * deep)
         pairs.append((wb_in.at[part, :], w.at[part, :n]))
         pairs.append((wc_in.at[part, :], w.at[part, n:]))
         pairs.append((lat_in.at[:, part], lat.at[:, part]))
-    pairs += [(x_in, x), (cot_in, cot)]
     copies = [pltpu.make_async_copy(src, dst, sems.at[i]) for i, (src, dst) in enumerate(pairs)]
     for copy in copies:
         copy.start()
@@ -75,48 +74,50 @@
     cols = x.shape[1]
     hd = cols // heads
     scale = 1.0 / math.sqrt(n)
-    t = lax.broadcasted_iota(jnp.int32, (rows, rows), 0)
-    s = lax.broadcasted_iota(jnp.int32, (rows, rows), 1)
-    lower = (s <= t).astype(F32)
+    down = lax.broadcasted_iota(jnp.int32, (rows, rows), 0)
+    along = lax.broadcasted_iota(jnp.int32, (rows, rows), 1)
     copies[0].wait()
-    cumc = dot(lower, ld[...], 1, 1, lax.Precision.HIGHEST)
-    cumr = dot(ld[...], lower, 1, 1, lax.Precision.HIGHEST)
+    cumr = dot(ld[...], (down <= along).astype(F32), 1, 0, lax.Precision.HIGHEST)
+    cumc = dot((along <= down).astype(F32), ld[...], 1, 1, lax.Precision.HIGHEST)
     cumc_out[...] = cumc
     cumr_out[...] = cumr
-    total = cumc[rows - 1 : rows, :]
-    tail = jnp.exp(total - cumc)
-    rise = jnp.exp(cumc) * scale
+    tail = jnp.exp(cumr[:, rows - 1 : rows] - cumr)
+    rise = jnp.exp(cumr) * scale
     table_out[...] = jnp.zeros_like(table_out)
     totals = []
     for h in range(heads):
-        totals.append(jnp.broadcast_to(total[:, h : h + 1], (1, n)))
+        totals.append(jnp.broadcast_to(cumc[rows - 1 : rows, h : h + 1], (1, n)))
         table_out[h : h + 1, :] = totals[h]
     put_totals(send, 2 * cols, totals)
+    copies[1].wait()
+    copies[2].wait()
+    decayed = []
+    for h in range(heads):
+        at = slice(h * hd, (h + 1) * hd)
+        xs = (x[:, at].astype(F32).T * tail[h : h + 1, :]).astype(BF16)
+        gs = (cot[:, at].astype(F32).T * rise[h : h + 1, :]).astype(BF16)
+        decayed.append((xs, gs))
     projected = None
     for i in range(chunks):
-        for copy in copies[1 + 3 * i : 4 + 3 * i]:
+        for copy in copies[3 + 3 * i : 6 + 3 * i]:
             copy.wait()
         part = slice(i * deep, (i + 1) * deep)
         one = dot(lat[:, part], w[part, :], 1, 0)
         projected = one if projected is None else projected + one
     b = projected[:, :n].astype(BF16)
     c = projected[:, n:].astype(BF16)
-    b_out[...] = b
-    c_out[...] = c
-    for copy in copies[-2:]:
-        copy.wait()
-    share = mine_out.shape[1]
-    mine_out[...] = lat[:, pl.ds(pl.multiple_of(place[0] * share, share), share)]
-    for h in range(heads):
-        at = slice(h * hd, (h + 1) * hd)
-        xs = (x[:, at].astype(F32) * tail[:, h : h + 1]).astype(BF16)
-        gs = (cot[:, at].astype(F32) * rise[:, h : h + 1]).astype(BF16)
-        fresh = dot(xs, b, 0, 0)
-        back = dot(gs, c, 0, 0)
+    for h, (xs, gs) in enumerate(decayed):
+        at = slice(h * hd, (h + 1) * hd)
+        fresh = dot(xs, b, 1, 0)
+        back = dot(gs, c, 1, 0)
         fresh_out[at, :] = fresh
         back_out[at, :] = back
         send[at, :] = fresh.astype(BF16)
         send[cols + h * hd : cols + (h + 1) * hd, :] = back.astype(BF16)
+    b_out[...] = b
+    c_out[...] = c
+    share = mine_out.shape[1]
+    mine_out[...] = lat[:, pl.ds(pl.multiple_of(place[0] * share, share), share)]
 
 
 def totals_of(got, at):
@@ -328,14 +329,14 @@
     return call(
         functools.partial(gather_body, scale),
         [((copies, *got.shape[1:]), BF16)],
-        (got, *(pltpu.with_memory_space_constraint(a, pltpu.HBM) for a in beside)),
-        [VMEM] + [HBM] * len(beside),
+        (got, *beside),
+        [VMEM] + [HBM if a.size > 2**14 else VMEM for a in beside],
     )[0]
 
 
-def summed(pieces, axes, scale=1.0):
+def summed(pieces, axes, scale, beside):
     got = lax.all_to_all(pieces, axes, 0, 0)
-    return lax.all_to_all(gathered(scale, got, pieces.shape[0]), axes, 0, 0)
+    return lax.all_to_all(gathered(scale, got, pieces.shape[0], beside), axes, 0, 0)
 
 
 def summed_in_groups(pieces, axis, beside):
@@ -431,7 +432,7 @@
         (b, c, cumc, inner, gx, attended, enter, leave),
         flops=4 * rows * cols * n,
     )
-    both = summed_in_groups(both, "space", (layer_out,))
+    both = summed_in_groups(both, "space", (tails[:16, :n],))
     others = tm * lax.axis_size("dp")
     term = call(
         project_body,
@@ -439,7 +440,8 @@
         (mine, both),
         flops=2 * rows * share * 2 * n,
     )[0]
-    term = summed(term, ("tm", "dp"), 1.0 / math.sqrt(rows * others))
+    done = pltpu.with_memory_space_constraint(layer_out, pltpu.HBM)
+    term = summed(term, ("tm", "dp"), 1.0 / math.sqrt(rows * others), (done,))
     proj_grad = call(unpack_body, [((share, 2 * n), F32)], (term,))[0]
     return layer_out[None], input_grad[None], proj_grad
 

time: 114 us -> 115 us (level)
  blocking collectives: 63.3 us -> 44.2 us
  starting transfers between devices: 35.2 us -> 45.2 us
  waiting for transfers between devices: 6.42 us -> 15.8 us
    all_to_all x2 -> x1, blocking collectives: 33 us -> 13.9 us  [summed(): lax.all_to_all(gathered(scale, got, pieces.shape[0], beside), axes, 0, 0)]
    all_to_all x0 -> x1, starting transfers between devices: none -> 10.2 us  [summed(): got = lax.all_to_all(pieces, axes, 0, 0)]
    all_to_all x0 -> x1, waiting for transfers between devices: none -> 7.15 us  [summed(): got = lax.all_to_all(pieces, axes, 0, 0)]
    all_to_all x1, waiting for transfers between devices: 3.48 us -> 5.74 us  [summed_in_groups(): lax.all_to_all(gathered(1.0, got, far), axis, 0, 0, axis_index_groups=acr...]
  transfers between devices with their start and end apart: 4 -> 5, of which waited for: 4 -> 5; matrix products, arithmetic and copies ran while one was open for 0% -> 0% of each run, Pallas kernels for 3% -> 3%
where the time goes in v5:
time: 115 us; the launch traced here: 114 us
  starting transfers between devices  45.2 us (39%)
  blocking collectives  44.2 us (38%)
  waiting for transfers between devices  15.8 us (14%)
  Pallas kernels  8.37 us (7%)
    ppermute x2, starting transfers between devices, swapped(): lax.ppermute(block, axis, [(i, i ^ distance) for i in range(lax.axis_size...  18.8 us
    all_to_all x1, blocking collectives, on_device(): got = lax.all_to_all(spread, 'tm', 0, 0, axis_index_groups=same_core)  15 us
    all_to_all x1, blocking collectives, summed(): lax.all_to_all(gathered(scale, got, pieces.shape[0], beside), axes, 0, 0)  13.9 us
    all_to_all x1, starting transfers between devices, summed_in_groups(): lax.all_to_all(gathered(1.0, got, far), axis, 0, 0, axis_index_groups=acr...  11.8 us
    all_to_all x1, starting transfers between devices, summed(): got = lax.all_to_all(pieces, axes, 0, 0)  10.2 us
    pallas_call x12, Pallas kernels, call(): pl.pallas_call(body, out_shape=[jax.ShapeDtypeStruct(s, t) for s, t in ou...  8.37 us
    all_to_all x1, blocking collectives, summed_in_groups(): lax.all_to_all(gathered(1.0, got, near, beside), axis, 0, 0, axis_index_g...  8.06 us
    all_to_all x1, blocking collectives, summed_in_groups(): got = lax.all_to_all(pieces, axis, 0, 0, axis_index_groups=inside)  7.27 us
  transfers between devices with their start and end apart: 5, of which 5 were waited for; matrix products, arithmetic and copies ran while one was open for 0% of the time, Pallas kernels for 3%

profile of v5, /device:TPU:1, one launch (start us, length us, event | category | flops | bytes accessed | tf_op | source)
XLA Modules:
  0.0 114.5 jit_solution(14798679100558549039)
XLA Ops:
  0.6 0.0 copy-start
  0.6 0.0 copy-start.1
  0.7 2.6 %shard_map.121 = (bf16[256,128]{1,0:T(8,128)(2,1)S(1)}, bf16[256,128]{1,0:T(8,128)(2,1)S(1)}, f32[256,2]{1,0:T(8,128)S(1)}, f32[2,256]{1,0:T(2,128)S(1)}, f32[25...) custom-call(s32[1]{0:T(128)} %bitcast.place, ...), custom_call_target="tpu_custom_call" | custom-call | flops 301989888 | tf_op jit(solution)/shard_map/pallas_call | solution.py:30
  3.3 16.1 %collective-permute-start.1 = (bf16[528,128]{1,0:T(8,128)(2,1)S(1)}, bf16[528,128]{1,0:T(8,128)(2,1)S(1)}, u32[]{:S(2)}, u32[]{:S(2)}) collective-permute-start(bf16[528,128]{1,0:T(8,128)(2,1)S(1)} %get-tuple-element.29), channel_id=1, source_target_pairs={{0,64},{64,0},{128,192},{192,128},{256,320},{320,256},{384,448},{4... | collective-permute-start | bytes 405512 | tf_op jit(solution)/shard_map/ppermute | solution.py:325
  19.4 0.0 copy-done
  19.4 0.0 copy-done.1
  19.4 0.8 shard_map.122
  20.2 0.1 collective-permute-done.1.got.pair
  20.3 0.1 shard_map.124
  20.4 15.0 %all_to_all.30.got = bf16[8,144,128]{2,1,0:T(8,128)(2,1)S(1)} all-to-all(bf16[8,144,128]{2,1,0:T(8,128)(2,1)S(1)} %shard_map.124), channel_id=1, replica_groups={{0,128,256,384,512,640,768,896},{64,192,320,448,576,704,832,960},{1,129..., dimensions={0} | all-to-all | bytes 589824 | tf_op jit(solution)/shard_map/all_to_all | solution.py:413
  35.4 0.2 shard_map.125
  35.6 2.8 %collective-permute-start.2 = (bf16[256,128]{1,0:T(8,128)(2,1)S(1)}, bf16[256,128]{1,0:T(8,128)(2,1)S(1)}, u32[]{:S(2)}, u32[]{:S(2)}) collective-permute-start(bf16[256,128]{1,0:T(8,128)(2,1)S(1)} %get-tuple-element.35), channel_id=1, source_target_pairs={{0,64},{64,0},{128,192},{192,128},{256,320},{320,256},{384,448},{4... | collective-permute-start | bytes 196616 | tf_op jit(solution)/shard_map/ppermute | solution.py:325
  38.4 0.9 collective-permute-done.2.got
  39.3 0.2 shard_map.126
  39.5 7.3 %all_to_all.31.got = bf16[4,64,256]{2,1,0:T(8,128)(2,1)S(1)} all-to-all(bf16[4,64,256]{2,1,0:T(8,128)(2,1)S(1)} %get-tuple-element.42), channel_id=1, replica_groups={{0,4,8,12},{16,20,24,28},{32,36,40,44},{48,52,56,60},{1,5,9,13},{17,21,..., dimensions={0} | all-to-all | bytes 262144 | tf_op jit(solution)/shard_map/all_to_all | solution.py:347
  46.8 0.7 shard_map.128
  47.5 0.0 copy-start.2
  47.5 0.0 copy-start.3
  47.5 11.8 %all-to-all-start.2 = ((bf16[4,64,256]{2,1,0:T(8,128)(2,1)}), bf16[4,64,256]{2,1,0:T(8,128)(2,1)S(1)}, u32[]{:S(2)}, u32[]{:S(2)}) async-start(bf16[4,64,256]{2,1,0:T(8,128)(2,1)} %shard_map.128), calls=%async_computation.2 | async-start | bytes 262144 | tf_op jit(solution)/shard_map/all_to_all | solution.py:348
  59.3 0.0 copy-done.2
  59.3 0.0 copy-done.3
  59.3 4.4 %collective-permute-start = (bf16[128,512]{1,0:T(8,128)(2,1)S(1)}, bf16[128,512]{1,0:T(8,128)(2,1)S(1)}, u32[]{:S(2)}, u32[]{:S(2)}) collective-permute-start(bf16[128,512]{1,0:T(8,128)(2,1)S(1)} %pad_maximum_fusion), channel_id=1, source_target_pairs={{0,64},{64,128},{128,192},{192,256},{256,320},{320,384},{384,448},... | collective-permute-start | bytes 393224 | tf_op jit(solution)/shard_map/ppermute | solution.py:321
  63.8 1.9 %collective-permute-done.tail = bf16[128,512]{1,0:T(8,128)(2,1)S(1)} collective-permute-done((bf16[128,512]{1,0:T(8,128)(2,1)S(1)}, bf16[128,512]{1,0:T(8,128)(2,1)S(1)}, u32[]{:S(2)}, u32[]{:S(2)}) %collective-permute-start) | collective-permute-done | bytes 131104 | tf_op jit(solution)/shard_map/ppermute | solution.py:321
  65.7 5.7 %all-to-all-done.2.got = bf16[4,64,256]{2,1,0:T(8,128)(2,1)S(1)} async-done(((bf16[4,64,256]{2,1,0:T(8,128)(2,1)}), bf16[4,64,256]{2,1,0:T(8,128)(2,1)S(1)}, u32[]{:S(2)}, u32[]{:S(2)}) %all-to-all-start.2) | async-done | bytes 131104 | tf_op jit(solution)/shard_map/all_to_all | solution.py:348
  71.4 8.1 %all_to_all.32.both = bf16[4,64,256]{2,1,0:T(8,128)(2,1)S(1)} all-to-all(bf16[4,64,256]{2,1,0:T(8,128)(2,1)S(1)} %shard_map.129), channel_id=1, replica_groups={{0,4,8,12},{16,20,24,28},{32,36,40,44},{48,52,56,60},{1,5,9,13},{17,21,..., dimensions={0} | all-to-all | bytes 262144 | tf_op jit(solution)/shard_map/all_to_all | solution.py:349
  79.5 0.8 shard_map.130
  80.3 0.0 copy-start.4
  80.3 10.2 %all-to-all-start.4 = ((bf16[64,2,256]{2,1,0:T(2,128)(2,1)}), bf16[64,2,256]{2,1,0:T(2,128)(2,1)S(1)}, u32[]{:S(2)}, u32[]{:S(2)}) async-start(bf16[64,2,256]{2,1,0:T(2,128)(2,1)} %shard_map.130), calls=%async_computation.4 | async-start | bytes 131072 | tf_op jit(solution)/shard_map/all_to_all | solution.py:338
  90.5 0.0 copy-done.4
  90.5 1.1 shard_map.123.attended
  91.6 1.0 shard_map.127
  92.6 7.2 %all-to-all-done.4.got = bf16[64,2,256]{2,1,0:T(2,128)(2,1)S(1)} async-done(((bf16[64,2,256]{2,1,0:T(2,128)(2,1)}), bf16[64,2,256]{2,1,0:T(2,128)(2,1)S(1)}, u32[]{:S(2)}, u32[]{:S(2)}) %all-to-all-start.4) | async-done | bytes 65568 | tf_op jit(solution)/shard_map/all_to_all | solution.py:338
  99.8 0.1 shard_map.131
  99.9 13.9 %all_to_all.33.got = bf16[64,2,256]{2,1,0:T(2,128)(2,1)S(1)} all-to-all(bf16[64,2,256]{2,1,0:T(2,128)(2,1)S(1)} %shard_map.131), channel_id=1, replica_groups=mesh['tm'=16,'space'=16,'dp'=4] {'tm','dp'}, dimensions={0} | all-to-all | bytes 131072 | tf_op jit(solution)/shard_map/all_to_all | solution.py:339
  113.8 0.7 shard_map.132
  (4 shorter events, 0.0 us)
Async XLA Ops:
  0.6 18.7 %copy-start = (bf16[1,256,256]{2,1,0:T(8,128)(2,1)S(1)}, bf16[1,256,256]{2,1,0:T(8,128)(2,1)}, u32[]{:S(2)}) copy-start(bf16[1,256,256]{2,1,0:T(8,128)(2,1)} %param.13) | copy-start | bytes 393220
  0.6 18.7 %copy-start.1 = (bf16[1,256,256]{2,1,0:T(8,128)(2,1)S(1)}, bf16[1,256,256]{2,1,0:T(8,128)(2,1)}, u32[]{:S(2)}) copy-start(bf16[1,256,256]{2,1,0:T(8,128)(2,1)} %param.18) | copy-start | bytes 393220
  3.3 17.0 %collective-permute-start.1 = (bf16[528,128]{1,0:T(8,128)(2,1)S(1)}, bf16[528,128]{1,0:T(8,128)(2,1)S(1)}, u32[]{:S(2)}, u32[]{:S(2)}) collective-permute-start(bf16[528,128]{1,0:T(8,128)(2,1)S(1)} %get-tuple-element.29), channel_id=1, source_target_pairs={{0,64},{64,0},{128,192},{192,128},{256,320},{320,256},{384,448},{4... | collective-permute-start | bytes 405512 | tf_op jit(solution)/shard_map/ppermute | solution.py:325
  35.6 3.7 %collective-permute-start.2 = (bf16[256,128]{1,0:T(8,128)(2,1)S(1)}, bf16[256,128]{1,0:T(8,128)(2,1)S(1)}, u32[]{:S(2)}, u32[]{:S(2)}) collective-permute-start(bf16[256,128]{1,0:T(8,128)(2,1)S(1)} %get-tuple-element.35), channel_id=1, source_target_pairs={{0,64},{64,0},{128,192},{192,128},{256,320},{320,256},{384,448},{4... | collective-permute-start | bytes 196616 | tf_op jit(solution)/shard_map/ppermute | solution.py:325
  47.5 11.8 %copy-start.2 = (bf16[1,256,256]{2,1,0:T(8,128)(2,1)S(1)}, bf16[1,256,256]{2,1,0:T(8,128)(2,1)}, u32[]{:S(2)}) copy-start(bf16[1,256,256]{2,1,0:T(8,128)(2,1)} %param.16) | copy-start | bytes 393220
  47.5 11.8 %copy-start.3 = (bf16[1,256,256]{2,1,0:T(8,128)(2,1)S(1)}, bf16[1,256,256]{2,1,0:T(8,128)(2,1)}, u32[]{:S(2)}) copy-start(bf16[1,256,256]{2,1,0:T(8,128)(2,1)} %param.17) | copy-start | bytes 393220
  47.5 23.9 %all-to-all-start.2 = ((bf16[4,64,256]{2,1,0:T(8,128)(2,1)}), bf16[4,64,256]{2,1,0:T(8,128)(2,1)S(1)}, u32[]{:S(2)}, u32[]{:S(2)}) async-start(bf16[4,64,256]{2,1,0:T(8,128)(2,1)} %shard_map.128), calls=%async_computation.2 | async-start | bytes 262144 | tf_op jit(solution)/shard_map/all_to_all | solution.py:348
  59.3 6.4 %collective-permute-start = (bf16[128,512]{1,0:T(8,128)(2,1)S(1)}, bf16[128,512]{1,0:T(8,128)(2,1)S(1)}, u32[]{:S(2)}, u32[]{:S(2)}) collective-permute-start(bf16[128,512]{1,0:T(8,128)(2,1)S(1)} %pad_maximum_fusion), channel_id=1, source_target_pairs={{0,64},{64,128},{128,192},{192,256},{256,320},{320,384},{384,448},... | collective-permute-start | bytes 393224 | tf_op jit(solution)/shard_map/ppermute | solution.py:321
  80.3 10.2 %copy-start.4 = (bf16[1,256,256]{2,1,0:T(8,128)(2,1)S(1)}, bf16[1,256,256]{2,1,0:T(8,128)(2,1)}, u32[]{:S(2)}) copy-start(bf16[1,256,256]{2,1,0:T(8,128)(2,1)} %param.15) | copy-start | bytes 393220
  80.3 19.4 %all-to-all-start.4 = ((bf16[64,2,256]{2,1,0:T(2,128)(2,1)}), bf16[64,2,256]{2,1,0:T(2,128)(2,1)S(1)}, u32[]{:S(2)}, u32[]{:S(2)}) async-start(bf16[64,2,256]{2,1,0:T(2,128)(2,1)} %shard_map.130), calls=%async_computation.4 | async-start | bytes 131072 | tf_op jit(solution)/shard_map/all_to_all | solution.py:338

commit v6 on v5

--- a/solution.py
+++ b/solution.py
@@ -16,7 +16,7 @@
 HBM = pl.BlockSpec(memory_space=pltpu.HBM)
 SMEM = pl.BlockSpec(memory_space=pltpu.SMEM)
 NEG = -1e30
-EXTRA = 16
+EXTRA = 8
 CHUNKS = 2
 
 
@@ -189,7 +189,7 @@
     send[hd:, :] = jnp.where(early, grad, before).astype(BF16)
 
 
-def attend_body(heads, qb, place, offsets_in, q, k, v, tail, out, offsets, sem):
+def attend_body(heads, qb, place, offsets_in, q, k, v, tail, normed, out, offsets, sem):
     copy = pltpu.make_async_copy(offsets_in, offsets, sem)
     copy.start()
     rows = q.shape[0]
@@ -220,7 +220,8 @@
         expo = jnp.exp(score - jnp.max(score, axis=-1, keepdims=True))
         probs = (expo / jnp.sum(expo, axis=-1, keepdims=True)).astype(BF16)
         values = window(v, blk, at, slice((heads + h) * hd, (heads + h + 1) * hd))
-        out[blk * qb : (blk + 1) * qb, at] = dot(probs, values, 1, 0)
+        own = slice(blk * qb, (blk + 1) * qb)
+        out[own, at] = (normed[own, at] + dot(probs, values, 1, 0)).astype(BF16)
 
 
 def local_body(heads, x, cot, b, c, cumc, cumr, inner_out, gx_out, both_out, token):
@@ -274,7 +275,7 @@
         out[i, :, n:] = gc[i * piece : (i + 1) * piece, :]
 
 
-def finish_body(heads, b, c, cumc, inner, gx, attended, enter, leave, layer_out, input_grad):
+def finish_body(heads, b, c, cumc, inner, gx, enter, leave, normed_out, input_grad):
     rows = b.shape[0]
     hd = inner.shape[1] // heads
     n = b.shape[1]
@@ -286,7 +287,7 @@
         rise = jnp.exp(cum) * scale
         y = inner[:, at] + rise * dot(c[...], enter[at, :], 1, 1)
         y = y * lax.rsqrt(jnp.mean(y * y, axis=-1, keepdims=True) + 1e-05)
-        layer_out[:, at] = (y + attended[:, at]).astype(BF16)
+        normed_out[:, at] = y
         g = gx[:, at] + tail * dot(b[...], leave[at, :], 1, 1)
         input_grad[:, at] = g.astype(BF16)
 
@@ -330,13 +331,13 @@
         functools.partial(gather_body, scale),
         [((copies, *got.shape[1:]), BF16)],
         (got, *beside),
-        [VMEM] + [HBM if a.size > 2**14 else VMEM for a in beside],
+        [VMEM] + [HBM] * len(beside),
     )[0]
 
 
-def summed(pieces, axes, scale, beside):
+def summed(pieces, axes, scale):
     got = lax.all_to_all(pieces, axes, 0, 0)
-    return lax.all_to_all(gathered(scale, got, pieces.shape[0], beside), axes, 0, 0)
+    return lax.all_to_all(gathered(scale, got, pieces.shape[0]), axes, 0, 0)
 
 
 def summed_in_groups(pieces, axis, beside):
@@ -386,15 +387,6 @@
         ],
         flops=2 * rows * width * 2 * n + 4 * rows * cols * n,
     )
-    attended = call(
-        functools.partial(attend_body, heads, QB),
-        [((rows, cols), F32)],
-        (me[None], pltpu.with_memory_space_constraint(window_offsets, pltpu.HBM), q, k, v, tails),
-        [SMEM, HBM] + [VMEM] * 4,
-        [pltpu.SMEM(window_offsets.shape, jnp.int32), pltpu.SemaphoreType.DMA],
-        flops=4 * rows * 2 * W * cols,
-        transcendentals=rows * 2 * W * heads,
-    )[0]
     inner, gx, both, token = call(
         functools.partial(local_body, heads),
         [((rows, cols), F32), ((rows, cols), F32), ((rows, 2 * n), F32), ((8, n), F32)],
@@ -426,13 +418,23 @@
         [SMEM] + [VMEM] * 6,
         flops=4 * rows * cols * n,
     )
-    layer_out, input_grad = call(
+    normed, input_grad = call(
         functools.partial(finish_body, heads),
-        [((rows, cols), BF16), ((rows, cols), BF16)],
-        (b, c, cumc, inner, gx, attended, enter, leave),
+        [((rows, cols), F32), ((rows, cols), BF16)],
+        (b, c, cumc, inner, gx, enter, leave),
         flops=4 * rows * cols * n,
     )
-    both = summed_in_groups(both, "space", (tails[:16, :n],))
+    layer_out = call(
+        functools.partial(attend_body, heads, QB),
+        [((rows, cols), BF16)],
+        (me[None], pltpu.with_memory_space_constraint(window_offsets, pltpu.HBM), q, k, v, tails, normed),
+        [SMEM, HBM] + [VMEM] * 5,
+        [pltpu.SMEM(window_offsets.shape, jnp.int32), pltpu.SemaphoreType.DMA],
+        flops=4 * rows * 2 * W * cols,
+        transcendentals=rows * 2 * W * heads,
+    )[0]
+    done = pltpu.with_memory_space_constraint(layer_out, pltpu.HBM)
+    both = summed_in_groups(both, "space", (done,))
     others = tm * lax.axis_size("dp")
     term = call(
         project_body,
@@ -440,8 +442,7 @@
         (mine, both),
         flops=2 * rows * share * 2 * n,
     )[0]
-    done = pltpu.with_memory_space_constraint(layer_out, pltpu.HBM)
-    term = summed(term, ("tm", "dp"), 1.0 / math.sqrt(rows * others), (done,))
+    term = summed(term, ("tm", "dp"), 1.0 / math.sqrt(rows * others))
     proj_grad = call(unpack_body, [((share, 2 * n), F32)], (term,))[0]
     return layer_out[None], input_grad[None], proj_grad
 

time: 115 us -> 114 us (level)
  blocking collectives: 44.2 us -> 63.3 us
  starting transfers between devices: 45.2 us -> 34.7 us
  waiting for transfers between devices: 15.8 us -> 5.85 us
    all_to_all x1 -> x2, blocking collectives: 13.9 us -> 33 us  [the longest x1 19.1 us: summed(): got = lax.all_to_all(pieces, axes, 0, 0)]
    all_to_all x1 -> x0, starting transfers between devices: 10.2 us -> none  [summed(): got = lax.all_to_all(pieces, axes, 0, 0)]
    all_to_all x1 -> x0, waiting for transfers between devices: 7.15 us -> none  [summed(): got = lax.all_to_all(pieces, axes, 0, 0)]
    all_to_all x1, waiting for transfers between devices: 5.74 us -> 3.94 us  [summed_in_groups(): lax.all_to_all(gathered(1.0, got, far), axis, 0, 0, axis_index_groups=acr...]
  transfers between devices with their start and end apart: 5 -> 4, of which waited for: 5 -> 4; matrix products, arithmetic and copies ran while one was open for 0% -> 0% of each run, Pallas kernels for 3% -> 3%
where the time goes in v6:
time: 114 us; the launch traced here: 113 us
  blocking collectives  63.3 us (56%)
  starting transfers between devices  34.7 us (30%)
  Pallas kernels  8.43 us (7%)
  waiting for transfers between devices  5.85 us (5%)
    all_to_all x1, blocking collectives, summed(): got = lax.all_to_all(pieces, axes, 0, 0)  19.1 us
    ppermute x2, starting transfers between devices, swapped(): lax.ppermute(block, axis, [(i, i ^ distance) for i in range(lax.axis_size...  18.5 us
    all_to_all x1, blocking collectives, on_device(): got = lax.all_to_all(spread, 'tm', 0, 0, axis_index_groups=same_core)  15.1 us
    all_to_all x1, blocking collectives, summed(): return lax.all_to_all(gathered(scale, got, pieces.shape[0]), axes, 0, 0)  13.9 us
    all_to_all x1, starting transfers between devices, summed_in_groups(): lax.all_to_all(gathered(1.0, got, far), axis, 0, 0, axis_index_groups=acr...  11.7 us
    pallas_call x12, Pallas kernels, call(): pl.pallas_call(body, out_shape=[jax.ShapeDtypeStruct(s, t) for s, t in ou...  8.43 us
    all_to_all x1, blocking collectives, summed_in_groups(): lax.all_to_all(gathered(1.0, got, near, beside), axis, 0, 0, axis_index_g...  8.06 us
    all_to_all x1, blocking collectives, summed_in_groups(): got = lax.all_to_all(pieces, axis, 0, 0, axis_index_groups=inside)  7.27 us
  transfers between devices with their start and end apart: 4, of which 4 were waited for; matrix products, arithmetic and copies ran while one was open for 0% of the time, Pallas kernels for 3%

profile of v6, /device:TPU:1, one launch (start us, length us, event | category | flops | bytes accessed | tf_op | source)
XLA Modules:
  0.0 113.1 jit_solution(13427805236784420579)
XLA Ops:
  0.6 0.0 copy-start
  0.6 0.0 copy-start.1
  0.7 2.6 %shard_map.121 = (bf16[256,128]{1,0:T(8,128)(2,1)S(1)}, bf16[256,128]{1,0:T(8,128)(2,1)S(1)}, f32[256,2]{1,0:T(8,128)S(1)}, f32[2,256]{1,0:T(2,128)S(1)}, f32[25...) custom-call(s32[1]{0:T(128)} %bitcast.6.place, ...), custom_call_target="tpu_custom_call" | custom-call | flops 301989888 | tf_op jit(solution)/shard_map/pallas_call | solution.py:30
  3.3 16.1 %collective-permute-start.1 = (bf16[520,128]{1,0:T(8,128)(2,1)S(1)}, bf16[520,128]{1,0:T(8,128)(2,1)S(1)}, u32[]{:S(2)}, u32[]{:S(2)}) collective-permute-start(bf16[520,128]{1,0:T(8,128)(2,1)S(1)} %get-tuple-element.29), channel_id=1, source_target_pairs={{0,64},{64,0},{128,192},{192,128},{256,320},{320,256},{384,448},{4... | collective-permute-start | bytes 399368 | tf_op jit(solution)/shard_map/ppermute | solution.py:326
  19.4 0.0 copy-done
  19.4 0.0 copy-done.1
  19.4 0.8 shard_map.122
  20.2 0.1 collective-permute-done.1.got.pair
  20.3 0.1 shard_map.123
  20.4 15.1 %all_to_all.30.got = bf16[8,136,128]{2,1,0:T(8,128)(2,1)S(1)} all-to-all(bf16[8,136,128]{2,1,0:T(8,128)(2,1)S(1)} %shard_map.123), channel_id=1, replica_groups={{0,128,256,384,512,640,768,896},{64,192,320,448,576,704,832,960},{1,129..., dimensions={0} | all-to-all | bytes 557056 | tf_op jit(solution)/shard_map/all_to_all | solution.py:405
  35.5 0.2 shard_map.124
  35.6 2.4 %collective-permute-start.2 = (bf16[256,128]{1,0:T(8,128)(2,1)S(1)}, bf16[256,128]{1,0:T(8,128)(2,1)S(1)}, u32[]{:S(2)}, u32[]{:S(2)}) collective-permute-start(bf16[256,128]{1,0:T(8,128)(2,1)S(1)} %get-tuple-element.35), channel_id=1, source_target_pairs={{0,64},{64,0},{128,192},{192,128},{256,320},{320,256},{384,448},{4... | collective-permute-start | bytes 196616 | tf_op jit(solution)/shard_map/ppermute | solution.py:326
  38.1 0.9 collective-permute-done.2.got
  39.0 0.2 shard_map.125
  39.2 7.3 %all_to_all.31.got = bf16[4,64,256]{2,1,0:T(8,128)(2,1)S(1)} all-to-all(bf16[4,64,256]{2,1,0:T(8,128)(2,1)S(1)} %get-tuple-element.42), channel_id=1, replica_groups={{0,4,8,12},{16,20,24,28},{32,36,40,44},{48,52,56,60},{1,5,9,13},{17,21,..., dimensions={0} | all-to-all | bytes 262144 | tf_op jit(solution)/shard_map/all_to_all | solution.py:348
  46.5 0.7 shard_map.128
  47.2 0.0 copy-start.2
  47.2 0.0 copy-start.3
  47.2 11.7 %all-to-all-start.2 = ((bf16[4,64,256]{2,1,0:T(8,128)(2,1)}), bf16[4,64,256]{2,1,0:T(8,128)(2,1)S(1)}, u32[]{:S(2)}, u32[]{:S(2)}) async-start(bf16[4,64,256]{2,1,0:T(8,128)(2,1)} %shard_map.128), calls=%async_computation.2 | async-start | bytes 262144 | tf_op jit(solution)/shard_map/all_to_all | solution.py:349
  58.9 0.0 copy-done.2
  58.9 0.0 copy-done.3
  59.0 4.4 %collective-permute-start = (bf16[128,512]{1,0:T(8,128)(2,1)S(1)}, bf16[128,512]{1,0:T(8,128)(2,1)S(1)}, u32[]{:S(2)}, u32[]{:S(2)}) collective-permute-start(bf16[128,512]{1,0:T(8,128)(2,1)S(1)} %pad_maximum_fusion), channel_id=1, source_target_pairs={{0,64},{64,128},{128,192},{192,256},{256,320},{320,384},{384,448},... | collective-permute-start | bytes 393224 | tf_op jit(solution)/shard_map/ppermute | solution.py:322
  63.4 0.0 copy-start.4
  63.4 1.0 shard_map.126
  64.4 0.9 collective-permute-done.tail
  65.3 0.0 copy-done.4
  65.3 1.8 %shard_map.127.rest_0_ = bf16[256,256]{1,0:T(8,128)(2,1)} custom-call(s32[1]{0:T(128)} %bitcast.place, s32[1,2]{1,0:T(1,128)} %offsets_in.1, bf16[256,256]{1,0:T(8,128)(2,1)S(1)} %bitcast.25, bf16[256,256]{1,0:T(8,128)(2,1)S(1)} %bitcast.23, bf16[256,256]{1,0:T(8,128)(2,1)S(1)} %bitcast.24, bf16[128,512]{1,0:T(8,128)(2,1)S(1)} %collective-permute-done.tail, ...), custom_call_target="tpu_custom_call" | custom-call | flops 67108864 | tf_op jit(solution)/shard_map/pallas_call | solution.py:30
  67.1 3.9 %all-to-all-done.2.got = bf16[4,64,256]{2,1,0:T(8,128)(2,1)S(1)} async-done(((bf16[4,64,256]{2,1,0:T(8,128)(2,1)}), bf16[4,64,256]{2,1,0:T(8,128)(2,1)S(1)}, u32[]{:S(2)}, u32[]{:S(2)}) %all-to-all-start.2) | async-done | bytes 131104 | tf_op jit(solution)/shard_map/all_to_all | solution.py:349
  71.1 8.1 %all_to_all.32.both = bf16[4,64,256]{2,1,0:T(8,128)(2,1)S(1)} all-to-all(bf16[4,64,256]{2,1,0:T(8,128)(2,1)S(1)} %shard_map.129), channel_id=1, replica_groups={{0,4,8,12},{16,20,24,28},{32,36,40,44},{48,52,56,60},{1,5,9,13},{17,21,..., dimensions={0} | all-to-all | bytes 262144 | tf_op jit(solution)/shard_map/all_to_all | solution.py:350
  79.1 0.2 shard_map.130
  79.4 19.1 %all_to_all.33.got = bf16[64,2,256]{2,1,0:T(2,128)(2,1)S(1)} all-to-all(bf16[64,2,256]{2,1,0:T(2,128)(2,1)S(1)} %shard_map.130), channel_id=1, replica_groups=mesh['tm'=16,'space'=16,'dp'=4] {'tm','dp'}, dimensions={0} | all-to-all | bytes 131072 | tf_op jit(solution)/shard_map/all_to_all | solution.py:339
  98.4 0.1 shard_map.131
  98.6 13.9 %all_to_all.34.got = bf16[64,2,256]{2,1,0:T(2,128)(2,1)S(1)} all-to-all(bf16[64,2,256]{2,1,0:T(2,128)(2,1)S(1)} %shard_map.131), channel_id=1, replica_groups=mesh['tm'=16,'space'=16,'dp'=4] {'tm','dp'}, dimensions={0} | all-to-all | bytes 131072 | tf_op jit(solution)/shard_map/all_to_all | solution.py:340
  112.4 0.7 shard_map.132
  (3 shorter events, 0.0 us)
Async XLA Ops:
  0.6 18.7 %copy-start = (bf16[1,256,256]{2,1,0:T(8,128)(2,1)S(1)}, bf16[1,256,256]{2,1,0:T(8,128)(2,1)}, u32[]{:S(2)}) copy-start(bf16[1,256,256]{2,1,0:T(8,128)(2,1)} %param.13) | copy-start | bytes 393220
  0.6 18.7 %copy-start.1 = (bf16[1,256,256]{2,1,0:T(8,128)(2,1)S(1)}, bf16[1,256,256]{2,1,0:T(8,128)(2,1)}, u32[]{:S(2)}) copy-start(bf16[1,256,256]{2,1,0:T(8,128)(2,1)} %param.18) | copy-start | bytes 393220
  3.3 17.0 %collective-permute-start.1 = (bf16[520,128]{1,0:T(8,128)(2,1)S(1)}, bf16[520,128]{1,0:T(8,128)(2,1)S(1)}, u32[]{:S(2)}, u32[]{:S(2)}) collective-permute-start(bf16[520,128]{1,0:T(8,128)(2,1)S(1)} %get-tuple-element.29), channel_id=1, source_target_pairs={{0,64},{64,0},{128,192},{192,128},{256,320},{320,256},{384,448},{4... | collective-permute-start | bytes 399368 | tf_op jit(solution)/shard_map/ppermute | solution.py:326
  35.6 3.3 %collective-permute-start.2 = (bf16[256,128]{1,0:T(8,128)(2,1)S(1)}, bf16[256,128]{1,0:T(8,128)(2,1)S(1)}, u32[]{:S(2)}, u32[]{:S(2)}) collective-permute-start(bf16[256,128]{1,0:T(8,128)(2,1)S(1)} %get-tuple-element.35), channel_id=1, source_target_pairs={{0,64},{64,0},{128,192},{192,128},{256,320},{320,256},{384,448},{4... | collective-permute-start | bytes 196616 | tf_op jit(solution)/shard_map/ppermute | solution.py:326
  47.2 11.7 %copy-start.2 = (bf16[1,256,256]{2,1,0:T(8,128)(2,1)S(1)}, bf16[1,256,256]{2,1,0:T(8,128)(2,1)}, u32[]{:S(2)}) copy-start(bf16[1,256,256]{2,1,0:T(8,128)(2,1)} %param.16) | copy-start | bytes 393220
  47.2 11.7 %copy-start.3 = (bf16[1,256,256]{2,1,0:T(8,128)(2,1)S(1)}, bf16[1,256,256]{2,1,0:T(8,128)(2,1)}, u32[]{:S(2)}) copy-start(bf16[1,256,256]{2,1,0:T(8,128)(2,1)} %param.17) | copy-start | bytes 393220
  47.2 23.9 %all-to-all-start.2 = ((bf16[4,64,256]{2,1,0:T(8,128)(2,1)}), bf16[4,64,256]{2,1,0:T(8,128)(2,1)S(1)}, u32[]{:S(2)}, u32[]{:S(2)}) async-start(bf16[4,64,256]{2,1,0:T(8,128)(2,1)} %shard_map.128), calls=%async_computation.2 | async-start | bytes 262144 | tf_op jit(solution)/shard_map/all_to_all | solution.py:349
  59.0 6.4 %collective-permute-start = (bf16[128,512]{1,0:T(8,128)(2,1)S(1)}, bf16[128,512]{1,0:T(8,128)(2,1)S(1)}, u32[]{:S(2)}, u32[]{:S(2)}) collective-permute-start(bf16[128,512]{1,0:T(8,128)(2,1)S(1)} %pad_maximum_fusion), channel_id=1, source_target_pairs={{0,64},{64,128},{128,192},{192,256},{256,320},{320,384},{384,448},... | collective-permute-start | bytes 393224 | tf_op jit(solution)/shard_map/ppermute | solution.py:322
  63.4 1.9 %copy-start.4 = (bf16[1,256,256]{2,1,0:T(8,128)(2,1)S(1)}, bf16[1,256,256]{2,1,0:T(8,128)(2,1)}, u32[]{:S(2)}) copy-start(bf16[1,256,256]{2,1,0:T(8,128)(2,1)} %param.15) | copy-start | bytes 393220

commit v7 on v6

--- a/solution.py
+++ b/solution.py
@@ -56,9 +56,10 @@
     send[at : at + EXTRA, :] = extra.astype(BF16)
 
 
-def pre_body(heads, place, lat_in, wb_in, wc_in, x_in, cot_in, ld_in, b_out, c_out, cumc_out, cumr_out,
+def pre_body(heads, share, place, lat_in, wb_in, wc_in, x_in, cot_in, ld_in, b_out, c_out, cumc_out, cumr_out,
              fresh_out, back_out, table_out, send, mine_out, lat, w, x, cot, ld, sems):
     n = wb_in.shape[1]
+    width = lat.shape[1]
     chunks = CHUNKS
     deep = lat.shape[1] // chunks
     pairs = [(ld_in, ld), (x_in, x), (cot_in, cot)]
@@ -116,8 +117,11 @@
         send[cols + h * hd : cols + (h + 1) * hd, :] = back.astype(BF16)
     b_out[...] = b
     c_out[...] = c
-    share = mine_out.shape[1]
-    mine_out[...] = lat[:, pl.ds(pl.multiple_of(place[0] * share, share), share)]
+    far = mine_out.shape[1] // share
+    near = width // mine_out.shape[1]
+    for g in range(far):
+        start = pl.multiple_of((near * g + place[0] % near) * share, share)
+        mine_out[:, g * share : (g + 1) * share] = lat[:, pl.ds(start, share)]
 
 
 def totals_of(got, at):
@@ -268,11 +272,10 @@
         rise = jnp.exp(cum) * scale
         gb = gb + tail * dot(x[:, at], grad, 1, 0)
         gc = gc + rise * dot(cot[:, at], state, 1, 0)
-    piece = out.shape[1]
     gb, gc = gb.astype(BF16), gc.astype(BF16)
     for i in range(out.shape[0]):
-        out[i, :, :n] = gb[i * piece : (i + 1) * piece, :]
-        out[i, :, n:] = gc[i * piece : (i + 1) * piece, :]
+        out[i, :, :n] = gb
+        out[i, :, n:] = gc
 
 
 def finish_body(heads, b, c, cumc, inner, gx, enter, leave, normed_out, input_grad):
@@ -292,22 +295,36 @@
         input_grad[:, at] = g.astype(BF16)
 
 
-def gather_body(scale, got, *rest):
-    out = rest[-1]
+def added(got):
     total = got[0].astype(F32)
     for i in range(1, got.shape[0]):
         total = total + got[i].astype(F32)
-    total = (total * scale).astype(BF16)
+    return total
+
+
+def project_body(share, mine, got, out):
+    term = dot(mine[...], added(got).astype(BF16), 0, 0)
+    far = term.shape[0] // share
+    piece = out.shape[1] // far
+    for k in range(out.shape[0]):
+        for g in range(far):
+            rows = slice(g * share + k * piece, g * share + (k + 1) * piece)
+            out[k, g * piece : (g + 1) * piece, :] = term[rows, :].astype(BF16)
+
+
+def spread_body(far, got, out):
+    total = added(got).astype(BF16).astype(F32)
+    piece = out.shape[1]
+    clips = out.shape[0] // far
+    for i in range(out.shape[0]):
+        g = i // clips
+        out[i] = total[g * piece : (g + 1) * piece, :].astype(BF16)
+
+
+def gather_body(scale, got, _, out):
+    total = (added(got) * scale).astype(BF16)
     for i in range(out.shape[0]):
         out[i] = total
-
-
-def project_body(mine, both, out):
-    size, rows, cols = both.shape
-    term = dot(mine[...], both[...].reshape(size * rows, cols), 0, 0)
-    piece = out.shape[1]
-    for i in range(out.shape[0]):
-        out[i] = term[i * piece : (i + 1) * piece, :].astype(BF16)
 
 
 def unpack_body(got, out):
@@ -324,30 +341,6 @@
 
 def swapped(block, axis, distance):
     return lax.ppermute(block, axis, [(i, i ^ distance) for i in range(lax.axis_size(axis))])
-
-
-def gathered(scale, got, copies, beside=()):
-    return call(
-        functools.partial(gather_body, scale),
-        [((copies, *got.shape[1:]), BF16)],
-        (got, *beside),
-        [VMEM] + [HBM] * len(beside),
-    )[0]
-
-
-def summed(pieces, axes, scale):
-    got = lax.all_to_all(pieces, axes, 0, 0)
-    return lax.all_to_all(gathered(scale, got, pieces.shape[0]), axes, 0, 0)
-
-
-def summed_in_groups(pieces, axis, beside):
-    near = pieces.shape[0]
-    far = lax.axis_size(axis) // near
-    inside = [[near * g + i for i in range(near)] for g in range(far)]
-    across = [[i + near * g for g in range(far)] for i in range(near)]
-    got = lax.all_to_all(pieces, axis, 0, 0, axis_index_groups=inside)
-    got = lax.all_to_all(gathered(1.0, got, far), axis, 0, 0, axis_index_groups=across)
-    return lax.all_to_all(gathered(1.0, got, near, beside), axis, 0, 0, axis_index_groups=inside)
 
 
 def on_device(latents, proj_input, proj_output, scan_input, log_decay, att_queries, att_keys,
@@ -359,6 +352,8 @@
     n = proj_input.shape[1]
     share = width // lax.axis_size("space")
     assert heads == 2
+    near = math.gcd(lax.axis_size("space"), 4)
+    far = lax.axis_size("space") // near
     tm = lax.axis_size("tm")
     me = lax.axis_index("tm")
     lat, x, ld = latents[0], scan_input[0], log_decay[0].T
@@ -368,13 +363,12 @@
         pltpu.with_memory_space_constraint(a, pltpu.HBM)
         for a in (lat, proj_input, proj_output, x, cot, ld)
     ]
-    tails = shifted(jnp.concatenate([k[rows - W :], v[rows - W :]], axis=1), "tm", 1)
     state = ((cols, n), F32)
     wire = ((2 * cols + EXTRA, n), BF16)
     b, c, cumc, cumr, fwd, bwd, table, send, mine = call(
-        functools.partial(pre_body, heads),
+        functools.partial(pre_body, heads, share),
         [((rows, n), BF16), ((rows, n), BF16), ((rows, heads), F32), ((heads, rows), F32), state, state,
-         ((24, n), F32), wire, ((rows, share), BF16)],
+         ((24, n), F32), wire, ((rows, share * far), BF16)],
         (lax.axis_index("space")[None], *inputs),
         [SMEM] + [HBM] * 6,
         [
@@ -410,10 +404,9 @@
         [SMEM] + [VMEM] * 5,
     )
     got = swapped(send, "tm", 1)
-    near = math.gcd(lax.axis_size("space"), 4)
     both, enter, leave = call(
         functools.partial(grads_body, heads),
-        [((near, rows // near, 2 * n), BF16), ((cols, n), BF16), ((cols, n), BF16)],
+        [((near, rows, 2 * n), BF16), ((cols, n), BF16), ((cols, n), BF16)],
         (me[None], keep, got, x, cot, cumc, both),
         [SMEM] + [VMEM] * 6,
         flops=4 * rows * cols * n,
@@ -424,6 +417,23 @@
         (b, c, cumc, inner, gx, enter, leave),
         flops=4 * rows * cols * n,
     )
+    clips = lax.axis_size("dp")
+    inside = [[near * g + i for i in range(near)] for g in range(far)]
+    across = [
+        [(near * g + i) * clips + clip for g in range(far) for clip in range(clips)] for i in range(near)
+    ]
+    piece = share // tm
+    got = lax.all_to_all(both, "space", 0, 0, axis_index_groups=inside)
+    term = call(
+        functools.partial(project_body, share),
+        [((tm, far * piece, 2 * n), BF16)],
+        (mine, got),
+        flops=2 * rows * share * far * 2 * n,
+    )[0]
+    got = lax.all_to_all(term, "tm", 0, 0)
+    term = call(functools.partial(spread_body, far), [((far * clips, piece, 2 * n), BF16)], (got,))[0]
+    last_k, last_v, term = lax.optimization_barrier((k, v, term))
+    tails = shifted(jnp.concatenate([last_k[rows - W :], last_v[rows - W :]], axis=1), "tm", 1)
     layer_out = call(
         functools.partial(attend_body, heads, QB),
         [((rows, cols), BF16)],
@@ -434,16 +444,15 @@
         transcendentals=rows * 2 * W * heads,
     )[0]
     done = pltpu.with_memory_space_constraint(layer_out, pltpu.HBM)
-    both = summed_in_groups(both, "space", (done,))
-    others = tm * lax.axis_size("dp")
+    got = lax.all_to_all(term, ("space", "dp"), 0, 0, axis_index_groups=across)
     term = call(
-        project_body,
-        [((others, share // others, 2 * n), BF16)],
-        (mine, both),
-        flops=2 * rows * share * 2 * n,
+        functools.partial(gather_body, 1.0 / math.sqrt(rows * tm * clips)),
+        [((tm, piece, 2 * n), BF16)],
+        (got, done),
+        [VMEM, HBM],
     )[0]
-    term = summed(term, ("tm", "dp"), 1.0 / math.sqrt(rows * others))
-    proj_grad = call(unpack_body, [((share, 2 * n), F32)], (term,))[0]
+    got = lax.all_to_all(term, "tm", 0, 0)
+    proj_grad = call(unpack_body, [((share, 2 * n), F32)], (got,))[0]
     return layer_out[None], input_grad[None], proj_grad
 
 

time: 114 us -> 113 us (level)
  blocking collectives: 63.3 us -> 58.5 us
  waiting for transfers between devices: 5.85 us -> 10.4 us
    all_to_all x4 -> x3, blocking collectives: 48.3 us -> 43.4 us  [the longest x2 26.8 us: on_device(): got = lax.all_to_all(term, 'tm', 0, 0)]
    all_to_all x1, waiting for transfers between devices: 3.94 us -> 8.5 us  [on_device(): got = lax.all_to_all(term, ('space', 'dp'), 0, 0, axis_index_groups=across)]
    all_to_all x1, starting transfers between devices: 11.7 us -> 14.4 us  [on_device(): got = lax.all_to_all(term, ('space', 'dp'), 0, 0, axis_index_groups=across)]
    ppermute x1, starting transfers between devices: 4.44 us -> 1.92 us  [shifted(): return lax.ppermute(block, axis, route)]
    pallas_call x12 -> x11, Pallas kernels: 8.43 us -> 8.44 us  [call(): pl.pallas_call(body, out_shape=[jax.ShapeDtypeStruct(s, t) for s, t in ou...]
where the time goes in v7:
time: 113 us
  blocking collectives  58.5 us (52%)
  starting transfers between devices  34.8 us (31%)
  waiting for transfers between devices  10.4 us (9%)
  Pallas kernels  8.44 us (7%)
    all_to_all x2, blocking collectives, on_device(): got = lax.all_to_all(term, 'tm', 0, 0)  26.8 us
    ppermute x2, starting transfers between devices, swapped(): lax.ppermute(block, axis, [(i, i ^ distance) for i in range(lax.axis_size...  18.5 us
    all_to_all x1, blocking collectives, on_device(): got = lax.all_to_all(both, 'space', 0, 0, axis_index_groups=inside)  16.7 us
    all_to_all x1, blocking collectives, on_device(): got = lax.all_to_all(spread, 'tm', 0, 0, axis_index_groups=same_core)  15.1 us
    all_to_all x1, starting transfers between devices, on_device(): got = lax.all_to_all(term, ('space', 'dp'), 0, 0, axis_index_groups=across)  14.4 us
    all_to_all x1, waiting for transfers between devices, on_device(): got = lax.all_to_all(term, ('space', 'dp'), 0, 0, axis_index_groups=across)  8.5 us
    pallas_call x11, Pallas kernels, call(): pl.pallas_call(body, out_shape=[jax.ShapeDtypeStruct(s, t) for s, t in ou...  8.44 us
  transfers between devices with their start and end apart: 4, of which 4 were waited for; matrix products, arithmetic and copies ran while one was open for 0% of the time, Pallas kernels for 3%

profile of v7, /device:TPU:1, one launch (start us, length us, event | category | flops | bytes accessed | tf_op | source)
XLA Modules:
  0.0 113.0 jit_solution(12110706303400569885)
XLA Ops:
  0.6 0.0 copy-start
  0.6 0.0 copy-start.1
  0.7 2.7 %shard_map.121 = (bf16[256,128]{1,0:T(8,128)(2,1)S(1)}, bf16[256,128]{1,0:T(8,128)(2,1)S(1)}, f32[256,2]{1,0:T(8,128)S(1)}, f32[2,256]{1,0:T(2,128)S(1)}, f32[25...) custom-call(s32[1]{0:T(128)} %bitcast.4.place, ...), custom_call_target="tpu_custom_call" | custom-call | flops 301989888 | tf_op jit(solution)/shard_map/pallas_call | solution.py:30
  3.3 16.1 %collective-permute-start = (bf16[520,128]{1,0:T(8,128)(2,1)S(1)}, bf16[520,128]{1,0:T(8,128)(2,1)S(1)}, u32[]{:S(2)}, u32[]{:S(2)}) collective-permute-start(bf16[520,128]{1,0:T(8,128)(2,1)S(1)} %get-tuple-element.27), channel_id=1, source_target_pairs={{0,64},{64,0},{128,192},{192,128},{256,320},{320,256},{384,448},{4... | collective-permute-start | bytes 399368 | tf_op jit(solution)/shard_map/ppermute | solution.py:343
  19.4 0.0 copy-done
  19.4 0.0 copy-done.1
  19.4 0.8 shard_map.122
  20.2 0.1 collective-permute-done.got.pair
  20.4 0.1 shard_map.123
  20.5 15.1 %all_to_all.25.got = bf16[8,136,128]{2,1,0:T(8,128)(2,1)S(1)} all-to-all(bf16[8,136,128]{2,1,0:T(8,128)(2,1)S(1)} %shard_map.123), channel_id=1, replica_groups={{0,128,256,384,512,640,768,896},{64,192,320,448,576,704,832,960},{1,129..., dimensions={0} | all-to-all | bytes 557056 | tf_op jit(solution)/shard_map/all_to_all | solution.py:399
  35.5 0.2 shard_map.124
  35.7 2.4 %collective-permute-start.1 = (bf16[256,128]{1,0:T(8,128)(2,1)S(1)}, bf16[256,128]{1,0:T(8,128)(2,1)S(1)}, u32[]{:S(2)}, u32[]{:S(2)}) collective-permute-start(bf16[256,128]{1,0:T(8,128)(2,1)S(1)} %get-tuple-element.37), channel_id=1, source_target_pairs={{0,64},{64,0},{128,192},{192,128},{256,320},{320,256},{384,448},{4... | collective-permute-start | bytes 196616 | tf_op jit(solution)/shard_map/ppermute | solution.py:343
  38.1 0.9 collective-permute-done.1.got
  39.0 0.3 shard_map.125
  39.3 16.7 %all_to_all.26.got = bf16[4,256,256]{2,1,0:T(8,128)(2,1)S(1)} all-to-all(bf16[4,256,256]{2,1,0:T(8,128)(2,1)S(1)} %get-tuple-element.39), channel_id=1, replica_groups={{0,4,8,12},{16,20,24,28},{32,36,40,44},{48,52,56,60},{1,5,9,13},{17,21,..., dimensions={0} | all-to-all | bytes 1048576 | tf_op jit(solution)/shard_map/all_to_all | solution.py:426
  56.0 0.3 shard_map.126
  56.3 15.5 %all_to_all.27.got = bf16[16,32,256]{2,1,0:T(8,128)(2,1)S(1)} all-to-all(bf16[16,32,256]{2,1,0:T(8,128)(2,1)S(1)} %shard_map.126), channel_id=1, replica_groups=mesh['tm'=16,'space'=16,'dp'=4] {'tm'}, dimensions={0} | all-to-all | bytes 524288 | tf_op jit(solution)/shard_map/all_to_all | solution.py:433
  71.7 0.7 shard_map.127
  72.4 0.0 copy-start.2
  72.4 0.0 copy-start.3
  72.4 14.4 %all-to-all-start.3 = ((bf16[16,8,256]{2,1,0:T(8,128)(2,1)}), bf16[16,8,256]{2,1,0:T(8,128)(2,1)S(1)}, u32[]{:S(2)}, u32[]{:S(2)}) async-start(bf16[16,8,256]{2,1,0:T(8,128)(2,1)} %shard_map.127), calls=%async_computation.3 | async-start | bytes 131072 | tf_op jit(solution)/shard_map/all_to_all | solution.py:447
  86.8 0.0 copy-done.2
  86.8 0.0 copy-done.3
  86.9 1.9 %collective-permute-start.2 = (bf16[128,512]{1,0:T(8,128)(2,1)S(1)}, bf16[128,512]{1,0:T(8,128)(2,1)S(1)}, u32[]{:S(2)}, u32[]{:S(2)}) collective-permute-start(bf16[128,512]{1,0:T(8,128)(2,1)S(1)} %pad_maximum_fusion), channel_id=1, source_target_pairs={{0,64},{64,128},{128,192},{192,256},{256,320},{320,384},{384,448},... | collective-permute-start | bytes 393224 | tf_op jit(solution)/shard_map/ppermute | solution.py:339
  88.8 0.0 copy-start.4
  88.8 1.0 shard_map.128
  89.8 0.9 collective-permute-done.2.tail
  90.7 0.0 copy-done.4
  90.7 1.8 %shard_map.129._ = bf16[256,256]{1,0:T(8,128)(2,1)} custom-call(s32[1]{0:T(128)} %bitcast.place, s32[1,2]{1,0:T(1,128)} %offsets_in.1, bf16[256,256]{1,0:T(8,128)(2,1)S(1)} %bitcast.23, bf16[256,256]{1,0:T(8,128)(2,1)S(1)} %bitcast.20, bf16[256,256]{1,0:T(8,128)(2,1)S(1)} %bitcast.22, bf16[128,512]{1,0:T(8,128)(2,1)S(1)} %collective-permute-done.2.tail, ...), custom_call_target="tpu_custom_call" | custom-call | flops 67108864 | tf_op jit(solution)/shard_map/pallas_call | solution.py:30
  92.5 8.5 %all-to-all-done.3.got = bf16[16,8,256]{2,1,0:T(8,128)(2,1)S(1)} async-done(((bf16[16,8,256]{2,1,0:T(8,128)(2,1)}), bf16[16,8,256]{2,1,0:T(8,128)(2,1)S(1)}, u32[]{:S(2)}, u32[]{:S(2)}) %all-to-all-start.3) | async-done | bytes 65568 | tf_op jit(solution)/shard_map/all_to_all | solution.py:447
  101.0 11.3 %all_to_all.28.got = bf16[16,8,256]{2,1,0:T(8,128)(2,1)S(1)} all-to-all(bf16[16,8,256]{2,1,0:T(8,128)(2,1)S(1)} %shard_map.130), channel_id=1, replica_groups=mesh['tm'=16,'space'=16,'dp'=4] {'tm'}, dimensions={0} | all-to-all | bytes 131072 | tf_op jit(solution)/shard_map/all_to_all | solution.py:454
  112.4 0.7 shard_map.131
  (4 shorter events, 0.0 us)
Async XLA Ops:
  0.6 18.8 %copy-start = (bf16[1,256,256]{2,1,0:T(8,128)(2,1)S(1)}, bf16[1,256,256]{2,1,0:T(8,128)(2,1)}, u32[]{:S(2)}) copy-start(bf16[1,256,256]{2,1,0:T(8,128)(2,1)} %param.13) | copy-start | bytes 393220
  0.6 18.8 %copy-start.1 = (bf16[1,256,256]{2,1,0:T(8,128)(2,1)S(1)}, bf16[1,256,256]{2,1,0:T(8,128)(2,1)}, u32[]{:S(2)}) copy-start(bf16[1,256,256]{2,1,0:T(8,128)(2,1)} %param.18) | copy-start | bytes 393220
  3.3 17.0 %collective-permute-start = (bf16[520,128]{1,0:T(8,128)(2,1)S(1)}, bf16[520,128]{1,0:T(8,128)(2,1)S(1)}, u32[]{:S(2)}, u32[]{:S(2)}) collective-permute-start(bf16[520,128]{1,0:T(8,128)(2,1)S(1)} %get-tuple-element.27), channel_id=1, source_target_pairs={{0,64},{64,0},{128,192},{192,128},{256,320},{320,256},{384,448},{4... | collective-permute-start | bytes 399368 | tf_op jit(solution)/shard_map/ppermute | solution.py:343
  35.7 3.3 %collective-permute-start.1 = (bf16[256,128]{1,0:T(8,128)(2,1)S(1)}, bf16[256,128]{1,0:T(8,128)(2,1)S(1)}, u32[]{:S(2)}, u32[]{:S(2)}) collective-permute-start(bf16[256,128]{1,0:T(8,128)(2,1)S(1)} %get-tuple-element.37), channel_id=1, source_target_pairs={{0,64},{64,0},{128,192},{192,128},{256,320},{320,256},{384,448},{4... | collective-permute-start | bytes 196616 | tf_op jit(solution)/shard_map/ppermute | solution.py:343
  72.4 14.4 %copy-start.2 = (bf16[1,256,256]{2,1,0:T(8,128)(2,1)S(1)}, bf16[1,256,256]{2,1,0:T(8,128)(2,1)}, u32[]{:S(2)}) copy-start(bf16[1,256,256]{2,1,0:T(8,128)(2,1)} %param.16) | copy-start | bytes 393220
  72.4 14.4 %copy-start.3 = (bf16[1,256,256]{2,1,0:T(8,128)(2,1)S(1)}, bf16[1,256,256]{2,1,0:T(8,128)(2,1)}, u32[]{:S(2)}) copy-start(bf16[1,256,256]{2,1,0:T(8,128)(2,1)} %param.17) | copy-start | bytes 393220
  72.4 28.6 %all-to-all-start.3 = ((bf16[16,8,256]{2,1,0:T(8,128)(2,1)}), bf16[16,8,256]{2,1,0:T(8,128)(2,1)S(1)}, u32[]{:S(2)}, u32[]{:S(2)}) async-start(bf16[16,8,256]{2,1,0:T(8,128)(2,1)} %shard_map.127), calls=%async_computation.3 | async-start | bytes 131072 | tf_op jit(solution)/shard_map/all_to_all | solution.py:447
  86.9 3.9 %collective-permute-start.2 = (bf16[128,512]{1,0:T(8,128)(2,1)S(1)}, bf16[128,512]{1,0:T(8,128)(2,1)S(1)}, u32[]{:S(2)}, u32[]{:S(2)}) collective-permute-start(bf16[128,512]{1,0:T(8,128)(2,1)S(1)} %pad_maximum_fusion), channel_id=1, source_target_pairs={{0,64},{64,128},{128,192},{192,256},{256,320},{320,384},{384,448},... | collective-permute-start | bytes 393224 | tf_op jit(solution)/shard_map/ppermute | solution.py:339
  88.8 1.9 %copy-start.4 = (bf16[1,256,256]{2,1,0:T(8,128)(2,1)S(1)}, bf16[1,256,256]{2,1,0:T(8,128)(2,1)}, u32[]{:S(2)}) copy-start(bf16[1,256,256]{2,1,0:T(8,128)(2,1)} %param.15) | copy-start | bytes 393220

commit v8 on v7

--- a/solution.py
+++ b/solution.py
@@ -273,9 +273,8 @@
         gb = gb + tail * dot(x[:, at], grad, 1, 0)
         gc = gc + rise * dot(cot[:, at], state, 1, 0)
     gb, gc = gb.astype(BF16), gc.astype(BF16)
-    for i in range(out.shape[0]):
-        out[i, :, :n] = gb
-        out[i, :, n:] = gc
+    out[:, :n] = gb
+    out[:, n:] = gc
 
 
 def finish_body(heads, b, c, cumc, inner, gx, enter, leave, normed_out, input_grad):
@@ -302,8 +301,13 @@
     return total
 
 
-def project_body(share, mine, got, out):
-    term = dot(mine[...], added(got).astype(BF16), 0, 0)
+def pass_on_body(own, got, out):
+    out[...] = (own[...].astype(F32) + got[...].astype(F32)).astype(BF16)
+
+
+def project_body(share, mine, own, got, _, out):
+    heads_sum = (own[...].astype(F32) + got[...].astype(F32)).astype(BF16)
+    term = dot(mine[...], heads_sum, 0, 0)
     far = term.shape[0] // share
     piece = out.shape[1] // far
     for k in range(out.shape[0]):
@@ -321,7 +325,7 @@
         out[i] = total[g * piece : (g + 1) * piece, :].astype(BF16)
 
 
-def gather_body(scale, got, _, out):
+def gather_body(scale, got, out):
     total = (added(got) * scale).astype(BF16)
     for i in range(out.shape[0]):
         out[i] = total
@@ -406,7 +410,7 @@
     got = swapped(send, "tm", 1)
     both, enter, leave = call(
         functools.partial(grads_body, heads),
-        [((near, rows, 2 * n), BF16), ((cols, n), BF16), ((cols, n), BF16)],
+        [((rows, 2 * n), BF16), ((cols, n), BF16), ((cols, n), BF16)],
         (me[None], keep, got, x, cot, cumc, both),
         [SMEM] + [VMEM] * 6,
         flops=4 * rows * cols * n,
@@ -418,22 +422,17 @@
         flops=4 * rows * cols * n,
     )
     clips = lax.axis_size("dp")
-    inside = [[near * g + i for i in range(near)] for g in range(far)]
     across = [
         [(near * g + i) * clips + clip for g in range(far) for clip in range(clips)] for i in range(near)
     ]
     piece = share // tm
-    got = lax.all_to_all(both, "space", 0, 0, axis_index_groups=inside)
-    term = call(
-        functools.partial(project_body, share),
-        [((tm, far * piece, 2 * n), BF16)],
-        (mine, got),
-        flops=2 * rows * share * far * 2 * n,
-    )[0]
-    got = lax.all_to_all(term, "tm", 0, 0)
-    term = call(functools.partial(spread_body, far), [((far * clips, piece, 2 * n), BF16)], (got,))[0]
-    last_k, last_v, term = lax.optimization_barrier((k, v, term))
-    tails = shifted(jnp.concatenate([last_k[rows - W :], last_v[rows - W :]], axis=1), "tm", 1)
+    distance = 1
+    got = swapped(both, "space", distance)
+    while 2 * distance < near:
+        both = call(pass_on_body, [((rows, 2 * n), BF16)], (both, got))[0]
+        distance *= 2
+        got = swapped(both, "space", distance)
+    tails = shifted(jnp.concatenate([k[rows - W :], v[rows - W :]], axis=1), "tm", 1)
     layer_out = call(
         functools.partial(attend_body, heads, QB),
         [((rows, cols), BF16)],
@@ -444,12 +443,20 @@
         transcendentals=rows * 2 * W * heads,
     )[0]
     done = pltpu.with_memory_space_constraint(layer_out, pltpu.HBM)
+    term = call(
+        functools.partial(project_body, share),
+        [((tm, far * piece, 2 * n), BF16)],
+        (mine, both, got, done),
+        [VMEM] * 3 + [HBM],
+        flops=2 * rows * share * far * 2 * n,
+    )[0]
+    got = lax.all_to_all(term, "tm", 0, 0)
+    term = call(functools.partial(spread_body, far), [((far * clips, piece, 2 * n), BF16)], (got,))[0]
     got = lax.all_to_all(term, ("space", "dp"), 0, 0, axis_index_groups=across)
     term = call(
         functools.partial(gather_body, 1.0 / math.sqrt(rows * tm * clips)),
         [((tm, piece, 2 * n), BF16)],
-        (got, done),
-        [VMEM, HBM],
+        (got,),
     )[0]
     got = lax.all_to_all(term, "tm", 0, 0)
     proj_grad = call(unpack_body, [((share, 2 * n), F32)], (got,))[0]

time: 113 us -> 111 us (0.982)
  starting transfers between devices: 34.8 us -> 24.8 us
  blocking collectives: 58.5 us -> 67.9 us
    all_to_all x1 -> x0, starting transfers between devices: 14.4 us -> none  [on_device(): got = lax.all_to_all(term, ('space', 'dp'), 0, 0, axis_index_groups=across)]
    all_to_all x1, blocking collectives: 16.7 us -> 26.7 us  [on_device(): got = lax.all_to_all(term, ('space', 'dp'), 0, 0, axis_index_groups=across)]
    all_to_all x1 -> x0, waiting for transfers between devices: 8.5 us -> none  [on_device(): got = lax.all_to_all(term, ('space', 'dp'), 0, 0, axis_index_groups=across)]
    ppermute x2 -> x4, waiting for transfers between devices: 1.02 us -> 9.42 us  [swapped(): lax.ppermute(block, axis, [(i, i ^ distance) for i in range(lax.axis_size...]
    ppermute x2 -> x4, starting transfers between devices: 18.5 us -> 22.4 us  [swapped(): lax.ppermute(block, axis, [(i, i ^ distance) for i in range(lax.axis_size...]
    pallas_call x11 -> x12, Pallas kernels: 8.44 us -> 7.81 us  [call(): pl.pallas_call(body, out_shape=[jax.ShapeDtypeStruct(s, t) for s, t in ou...]
  transfers between devices with their start and end apart: 4 -> 5, of which waited for: 4 -> 4; matrix products, arithmetic and copies ran while one was open for 0% -> 0% of each run, Pallas kernels for 3% -> 3%
where the time goes in v8:
time: 111 us
  blocking collectives  67.9 us (61%)
  starting transfers between devices  24.8 us (22%)
  waiting for transfers between devices  9.42 us (8%)
  Pallas kernels  7.81 us (7%)
    all_to_all x1, blocking collectives, on_device(): got = lax.all_to_all(term, ('space', 'dp'), 0, 0, axis_index_groups=across)  26.7 us
    all_to_all x2, blocking collectives, on_device(): got = lax.all_to_all(term, 'tm', 0, 0)  26.2 us
    ppermute x4, starting transfers between devices, swapped(): lax.ppermute(block, axis, [(i, i ^ distance) for i in range(lax.axis_size...  22.4 us
    all_to_all x1, blocking collectives, on_device(): got = lax.all_to_all(spread, 'tm', 0, 0, axis_index_groups=same_core)  15.1 us
    ppermute x4, waiting for transfers between devices, swapped(): lax.ppermute(block, axis, [(i, i ^ distance) for i in range(lax.axis_size...  9.42 us
    pallas_call x12, Pallas kernels, call(): pl.pallas_call(body, out_shape=[jax.ShapeDtypeStruct(s, t) for s, t in ou...  7.81 us
    ppermute x1, starting transfers between devices, shifted(): return lax.ppermute(block, axis, route)  2.44 us
  transfers between devices with their start and end apart: 5, of which 4 were waited for; matrix products, arithmetic and copies ran while one was open for 0% of the time, Pallas kernels for 3%

profile of v8, /device:TPU:1, one launch (start us, length us, event | category | flops | bytes accessed | tf_op | source)
XLA Modules:
  0.0 110.8 jit_solution(15010684478584552927)
XLA Ops:
  0.6 0.0 copy-start
  0.6 0.0 copy-start.1
  0.7 2.7 %shard_map.121 = (bf16[256,128]{1,0:T(8,128)(2,1)S(1)}, bf16[256,128]{1,0:T(8,128)(2,1)S(1)}, f32[256,2]{1,0:T(8,128)S(1)}, f32[2,256]{1,0:T(2,128)S(1)}, f32[25...) custom-call(s32[1]{0:T(128)} %bitcast.6.place, ...), custom_call_target="tpu_custom_call" | custom-call | flops 301989888 | tf_op jit(solution)/shard_map/pallas_call | solution.py:30
  3.3 16.1 %collective-permute-start.1 = (bf16[520,128]{1,0:T(8,128)(2,1)S(1)}, bf16[520,128]{1,0:T(8,128)(2,1)S(1)}, u32[]{:S(2)}, u32[]{:S(2)}) collective-permute-start(bf16[520,128]{1,0:T(8,128)(2,1)S(1)} %get-tuple-element.29), channel_id=1, source_target_pairs={{0,64},{64,0},{128,192},{192,128},{256,320},{320,256},{384,448},{4... | collective-permute-start | bytes 399368 | tf_op jit(solution)/shard_map/ppermute | solution.py:347
  19.4 0.0 copy-done
  19.4 0.0 copy-done.1
  19.4 0.8 shard_map.122
  20.2 0.1 collective-permute-done.1.got.pair
  20.4 0.1 shard_map.123
  20.5 15.1 %all_to_all.20.got = bf16[8,136,128]{2,1,0:T(8,128)(2,1)S(1)} all-to-all(bf16[8,136,128]{2,1,0:T(8,128)(2,1)S(1)} %shard_map.123), channel_id=1, replica_groups={{0,128,256,384,512,640,768,896},{64,192,320,448,576,704,832,960},{1,129..., dimensions={0} | all-to-all | bytes 557056 | tf_op jit(solution)/shard_map/all_to_all | solution.py:403
  35.5 0.2 shard_map.124
  35.7 2.4 %collective-permute-start.2 = (bf16[256,128]{1,0:T(8,128)(2,1)S(1)}, bf16[256,128]{1,0:T(8,128)(2,1)S(1)}, u32[]{:S(2)}, u32[]{:S(2)}) collective-permute-start(bf16[256,128]{1,0:T(8,128)(2,1)S(1)} %get-tuple-element.35), channel_id=1, source_target_pairs={{0,64},{64,0},{128,192},{192,128},{256,320},{320,256},{384,448},{4... | collective-permute-start | bytes 196616 | tf_op jit(solution)/shard_map/ppermute | solution.py:347
  38.1 0.9 collective-permute-done.2.got
  39.0 0.0 copy-start.2
  39.0 0.0 copy-start.3
  39.0 0.2 shard_map.125
  39.3 1.9 %collective-permute-start.3 = (bf16[256,256]{1,0:T(8,128)(2,1)S(1)}, bf16[256,256]{1,0:T(8,128)(2,1)S(1)}, u32[]{:S(2)}, u32[]{:S(2)}) collective-permute-start(bf16[256,256]{1,0:T(8,128)(2,1)S(1)} %get-tuple-element.42.own), channel_id=1, source_target_pairs={{0,4},{4,0},{8,12},{12,8},{16,20},{20,16},{24,28},{28,24},{32,36},... | collective-permute-start | bytes 393224 | tf_op jit(solution)/shard_map/ppermute | solution.py:347
  41.2 0.0 copy-done.2
  41.2 0.0 copy-done.3
  41.3 2.4 %collective-permute-start = (bf16[128,512]{1,0:T(8,128)(2,1)S(1)}, bf16[128,512]{1,0:T(8,128)(2,1)S(1)}, u32[]{:S(2)}, u32[]{:S(2)}) collective-permute-start(bf16[128,512]{1,0:T(8,128)(2,1)S(1)} %pad_maximum_fusion), channel_id=1, source_target_pairs={{0,64},{64,128},{128,192},{192,256},{256,320},{320,384},{384,448},... | collective-permute-start | bytes 393224 | tf_op jit(solution)/shard_map/ppermute | solution.py:343
  43.7 2.2 %collective-permute-done.3.got = bf16[256,256]{1,0:T(8,128)(2,1)S(1)} collective-permute-done((bf16[256,256]{1,0:T(8,128)(2,1)S(1)}, bf16[256,256]{1,0:T(8,128)(2,1)S(1)}, u32[]{:S(2)}, u32[]{:S(2)}) %collective-permute-start.3) | collective-permute-done | bytes 131104 | tf_op jit(solution)/shard_map/ppermute | solution.py:347
  45.9 1.9 %collective-permute-start.4 = (bf16[256,256]{1,0:T(8,128)(2,1)S(1)}, bf16[256,256]{1,0:T(8,128)(2,1)S(1)}, u32[]{:S(2)}, u32[]{:S(2)}) collective-permute-start(bf16[256,256]{1,0:T(8,128)(2,1)S(1)} %shard_map.128.own), channel_id=1, source_target_pairs={{0,8},{4,12},{8,0},{12,4},{16,24},{20,28},{24,16},{28,20},{32,40},... | collective-permute-start | bytes 393224 | tf_op jit(solution)/shard_map/ppermute | solution.py:347
  47.9 0.0 copy-start.4
  47.9 1.0 shard_map.126
  48.9 0.0 collective-permute-done.tail
  48.9 0.0 copy-done.4
  48.9 1.8 %shard_map.127._ = bf16[256,256]{1,0:T(8,128)(2,1)} custom-call(s32[1]{0:T(128)} %bitcast.place, s32[1,2]{1,0:T(1,128)} %offsets_in.1, bf16[256,256]{1,0:T(8,128)(2,1)S(1)} %bitcast.25, bf16[256,256]{1,0:T(8,128)(2,1)S(1)} %bitcast.23, bf16[256,256]{1,0:T(8,128)(2,1)S(1)} %bitcast.24, bf16[128,512]{1,0:T(8,128)(2,1)S(1)} %collective-permute-done.tail, ...), custom_call_target="tpu_custom_call" | custom-call | flops 67108864 | tf_op jit(solution)/shard_map/pallas_call | solution.py:30
  50.7 6.2 %collective-permute-done.4.got = bf16[256,256]{1,0:T(8,128)(2,1)S(1)} collective-permute-done((bf16[256,256]{1,0:T(8,128)(2,1)S(1)}, bf16[256,256]{1,0:T(8,128)(2,1)S(1)}, u32[]{:S(2)}, u32[]{:S(2)}) %collective-permute-start.4) | collective-permute-done | bytes 131104 | tf_op jit(solution)/shard_map/ppermute | solution.py:347
  56.9 0.3 shard_map.129
  57.2 14.8 %all_to_all.21.got = bf16[16,32,256]{2,1,0:T(8,128)(2,1)S(1)} all-to-all(bf16[16,32,256]{2,1,0:T(8,128)(2,1)S(1)} %shard_map.129), channel_id=1, replica_groups=mesh['tm'=16,'space'=16,'dp'=4] {'tm'}, dimensions={0} | all-to-all | bytes 524288 | tf_op jit(solution)/shard_map/all_to_all | solution.py:453
  72.0 26.7 %all_to_all.22.got = bf16[16,8,256]{2,1,0:T(8,128)(2,1)S(1)} all-to-all(bf16[16,8,256]{2,1,0:T(8,128)(2,1)S(1)} %shard_map.130), channel_id=1, replica_groups={{0,1,2,3,16,17,18,19,32,33,34,35,48,49,50,51},{4,5,6,7,20,21,22,23,36,3..., dimensions={0} | all-to-all | bytes 131072 | tf_op jit(solution)/shard_map/all_to_all | solution.py:455
  98.7 11.4 %all_to_all.23.got = bf16[16,8,256]{2,1,0:T(8,128)(2,1)S(1)} all-to-all(bf16[16,8,256]{2,1,0:T(8,128)(2,1)S(1)} %shard_map.131), channel_id=1, replica_groups=mesh['tm'=16,'space'=16,'dp'=4] {'tm'}, dimensions={0} | all-to-all | bytes 131072 | tf_op jit(solution)/shard_map/all_to_all | solution.py:461
  110.1 0.7 shard_map.132
  (5 shorter events, 0.1 us)
Async XLA Ops:
  0.6 18.8 %copy-start = (bf16[1,256,256]{2,1,0:T(8,128)(2,1)S(1)}, bf16[1,256,256]{2,1,0:T(8,128)(2,1)}, u32[]{:S(2)}) copy-start(bf16[1,256,256]{2,1,0:T(8,128)(2,1)} %param.13) | copy-start | bytes 393220
  0.6 18.8 %copy-start.1 = (bf16[1,256,256]{2,1,0:T(8,128)(2,1)S(1)}, bf16[1,256,256]{2,1,0:T(8,128)(2,1)}, u32[]{:S(2)}) copy-start(bf16[1,256,256]{2,1,0:T(8,128)(2,1)} %param.18) | copy-start | bytes 393220
  3.3 17.0 %collective-permute-start.1 = (bf16[520,128]{1,0:T(8,128)(2,1)S(1)}, bf16[520,128]{1,0:T(8,128)(2,1)S(1)}, u32[]{:S(2)}, u32[]{:S(2)}) collective-permute-start(bf16[520,128]{1,0:T(8,128)(2,1)S(1)} %get-tuple-element.29), channel_id=1, source_target_pairs={{0,64},{64,0},{128,192},{192,128},{256,320},{320,256},{384,448},{4... | collective-permute-start | bytes 399368 | tf_op jit(solution)/shard_map/ppermute | solution.py:347
  35.7 3.3 %collective-permute-start.2 = (bf16[256,128]{1,0:T(8,128)(2,1)S(1)}, bf16[256,128]{1,0:T(8,128)(2,1)S(1)}, u32[]{:S(2)}, u32[]{:S(2)}) collective-permute-start(bf16[256,128]{1,0:T(8,128)(2,1)S(1)} %get-tuple-element.35), channel_id=1, source_target_pairs={{0,64},{64,0},{128,192},{192,128},{256,320},{320,256},{384,448},{4... | collective-permute-start | bytes 196616 | tf_op jit(solution)/shard_map/ppermute | solution.py:347
  39.0 2.2 %copy-start.2 = (bf16[1,256,256]{2,1,0:T(8,128)(2,1)S(1)}, bf16[1,256,256]{2,1,0:T(8,128)(2,1)}, u32[]{:S(2)}) copy-start(bf16[1,256,256]{2,1,0:T(8,128)(2,1)} %param.16) | copy-start | bytes 393220
  39.0 2.2 %copy-start.3 = (bf16[1,256,256]{2,1,0:T(8,128)(2,1)S(1)}, bf16[1,256,256]{2,1,0:T(8,128)(2,1)}, u32[]{:S(2)}) copy-start(bf16[1,256,256]{2,1,0:T(8,128)(2,1)} %param.17) | copy-start | bytes 393220
  39.3 6.6 %collective-permute-start.3 = (bf16[256,256]{1,0:T(8,128)(2,1)S(1)}, bf16[256,256]{1,0:T(8,128)(2,1)S(1)}, u32[]{:S(2)}, u32[]{:S(2)}) collective-permute-start(bf16[256,256]{1,0:T(8,128)(2,1)S(1)} %get-tuple-element.42.own), channel_id=1, source_target_pairs={{0,4},{4,0},{8,12},{12,8},{16,20},{20,16},{24,28},{28,24},{32,36},... | collective-permute-start | bytes 393224 | tf_op jit(solution)/shard_map/ppermute | solution.py:347
  41.3 7.6 %collective-permute-start = (bf16[128,512]{1,0:T(8,128)(2,1)S(1)}, bf16[128,512]{1,0:T(8,128)(2,1)S(1)}, u32[]{:S(2)}, u32[]{:S(2)}) collective-permute-start(bf16[128,512]{1,0:T(8,128)(2,1)S(1)} %pad_maximum_fusion), channel_id=1, source_target_pairs={{0,64},{64,128},{128,192},{192,256},{256,320},{320,384},{384,448},... | collective-permute-start | bytes 393224 | tf_op jit(solution)/shard_map/ppermute | solution.py:343
  45.9 11.0 %collective-permute-start.4 = (bf16[256,256]{1,0:T(8,128)(2,1)S(1)}, bf16[256,256]{1,0:T(8,128)(2,1)S(1)}, u32[]{:S(2)}, u32[]{:S(2)}) collective-permute-start(bf16[256,256]{1,0:T(8,128)(2,1)S(1)} %shard_map.128.own), channel_id=1, source_target_pairs={{0,8},{4,12},{8,0},{12,4},{16,24},{20,28},{24,16},{28,20},{32,40},... | collective-permute-start | bytes 393224 | tf_op jit(solution)/shard_map/ppermute | solution.py:347
  47.9 1.0 copy-start.4

commit v9 on v8

--- a/solution.py
+++ b/solution.py
@@ -305,15 +305,20 @@
     out[...] = (own[...].astype(F32) + got[...].astype(F32)).astype(BF16)
 
 
-def project_body(share, mine, own, got, _, out):
+def project_body(share, place, mine, own, got, _, keep, send):
     heads_sum = (own[...].astype(F32) + got[...].astype(F32)).astype(BF16)
     term = dot(mine[...], heads_sum, 0, 0)
     far = term.shape[0] // share
-    piece = out.shape[1] // far
-    for k in range(out.shape[0]):
+    piece = keep.shape[1] // far
+    late = place[0] % 2 == 1
+    for k in range(keep.shape[0]):
         for g in range(far):
-            rows = slice(g * share + k * piece, g * share + (k + 1) * piece)
-            out[k, g * piece : (g + 1) * piece, :] = term[rows, :].astype(BF16)
+            start = g * share + 2 * k * piece
+            first = term[start : start + piece, :]
+            second = term[start + piece : start + 2 * piece, :]
+            at = slice(g * piece, (g + 1) * piece)
+            keep[k, at, :] = jnp.where(late, second, first).astype(BF16)
+            send[k, at, :] = jnp.where(late, first, second).astype(BF16)
 
 
 def spread_body(far, got, out):
@@ -443,14 +448,16 @@
         transcendentals=rows * 2 * W * heads,
     )[0]
     done = pltpu.with_memory_space_constraint(layer_out, pltpu.HBM)
-    term = call(
+    half = ((tm // 2, far * piece, 2 * n), BF16)
+    term, send = call(
         functools.partial(project_body, share),
-        [((tm, far * piece, 2 * n), BF16)],
-        (mine, both, got, done),
-        [VMEM] * 3 + [HBM],
+        [half, half],
+        (me[None], mine, both, got, done),
+        [SMEM] + [VMEM] * 3 + [HBM],
         flops=2 * rows * share * far * 2 * n,
-    )[0]
-    got = lax.all_to_all(term, "tm", 0, 0)
+    )
+    term = call(pass_on_body, [half], (term, swapped(send, "tm", 1)))[0]
+    got = lax.all_to_all(term, "tm", 0, 0, axis_index_groups=same_core)
     term = call(functools.partial(spread_body, far), [((far * clips, piece, 2 * n), BF16)], (got,))[0]
     got = lax.all_to_all(term, ("space", "dp"), 0, 0, axis_index_groups=across)
     term = call(

time: 111 us -> 112 us (level)
  blocking collectives: 67.9 us -> 65.4 us
  starting transfers between devices: 24.8 us -> 27.2 us
    all_to_all x2 -> x1, blocking collectives: 26.2 us -> 13.2 us  [on_device(): got = lax.all_to_all(term, 'tm', 0, 0)]
    all_to_all x0 -> x1, blocking collectives: none -> 10.8 us  [on_device(): got = lax.all_to_all(term, 'tm', 0, 0, axis_index_groups=same_core)]
    ppermute x4 -> x5, starting transfers between devices: 22.4 us -> 24.8 us  [swapped(): lax.ppermute(block, axis, [(i, i ^ distance) for i in range(lax.axis_size...]
    ppermute x4 -> x5, waiting for transfers between devices: 9.42 us -> 10.4 us  [swapped(): lax.ppermute(block, axis, [(i, i ^ distance) for i in range(lax.axis_size...]
    pallas_call x12 -> x13, Pallas kernels: 7.81 us -> 7.82 us  [call(): pl.pallas_call(body, out_shape=[jax.ShapeDtypeStruct(s, t) for s, t in ou...]
  transfers between devices with their start and end apart: 5 -> 6, of which waited for: 4 -> 5; matrix products, arithmetic and copies ran while one was open for 0% -> 0% of each run, Pallas kernels for 3% -> 3%
where the time goes in v9:
time: 112 us
  blocking collectives  65.4 us (58%)
  starting transfers between devices  27.2 us (24%)
  waiting for transfers between devices  10.4 us (9%)
  Pallas kernels  7.82 us (7%)
    all_to_all x1, blocking collectives, on_device(): got = lax.all_to_all(term, ('space', 'dp'), 0, 0, axis_index_groups=across)  26.3 us
    ppermute x5, starting transfers between devices, swapped(): lax.ppermute(block, axis, [(i, i ^ distance) for i in range(lax.axis_size...  24.8 us
    all_to_all x1, blocking collectives, on_device(): got = lax.all_to_all(spread, 'tm', 0, 0, axis_index_groups=same_core)  15.1 us
    all_to_all x1, blocking collectives, on_device(): got = lax.all_to_all(term, 'tm', 0, 0)  13.2 us
    all_to_all x1, blocking collectives, on_device(): got = lax.all_to_all(term, 'tm', 0, 0, axis_index_groups=same_core)  10.8 us
    ppermute x5, waiting for transfers between devices, swapped(): lax.ppermute(block, axis, [(i, i ^ distance) for i in range(lax.axis_size...  10.4 us
    pallas_call x13, Pallas kernels, call(): pl.pallas_call(body, out_shape=[jax.ShapeDtypeStruct(s, t) for s, t in ou...  7.82 us
    ppermute x1, starting transfers between devices, shifted(): return lax.ppermute(block, axis, route)  2.44 us
  transfers between devices with their start and end apart: 6, of which 5 were waited for; matrix products, arithmetic and copies ran while one was open for 0% of the time, Pallas kernels for 3%

profile of v9, /device:TPU:1, one launch (start us, length us, event | category | flops | bytes accessed | tf_op | source)
XLA Modules:
  0.0 111.7 jit_solution(16667142291992674144)
XLA Ops:
  0.6 0.0 copy-start
  0.6 0.0 copy-start.1
  0.7 2.7 %shard_map.121 = (bf16[256,128]{1,0:T(8,128)(2,1)S(1)}, bf16[256,128]{1,0:T(8,128)(2,1)S(1)}, f32[256,2]{1,0:T(8,128)S(1)}, f32[2,256]{1,0:T(2,128)S(1)}, f32[25...) custom-call(s32[1]{0:T(128)} %bitcast.6.place, ...), custom_call_target="tpu_custom_call" | custom-call | flops 301989888 | tf_op jit(solution)/shard_map/pallas_call | solution.py:30
  3.3 16.1 %collective-permute-start.1 = (bf16[520,128]{1,0:T(8,128)(2,1)S(1)}, bf16[520,128]{1,0:T(8,128)(2,1)S(1)}, u32[]{:S(2)}, u32[]{:S(2)}) collective-permute-start(bf16[520,128]{1,0:T(8,128)(2,1)S(1)} %get-tuple-element.31), channel_id=1, source_target_pairs={{0,64},{64,0},{128,192},{192,128},{256,320},{320,256},{384,448},{4... | collective-permute-start | bytes 399368 | tf_op jit(solution)/shard_map/ppermute | solution.py:352
  19.4 0.0 copy-done
  19.4 0.0 copy-done.1
  19.4 0.8 shard_map.122
  20.2 0.1 collective-permute-done.1.got.pair
  20.4 0.1 shard_map.123
  20.5 15.1 %all_to_all.20.got = bf16[8,136,128]{2,1,0:T(8,128)(2,1)S(1)} all-to-all(bf16[8,136,128]{2,1,0:T(8,128)(2,1)S(1)} %shard_map.123), channel_id=1, replica_groups={{0,128,256,384,512,640,768,896},{64,192,320,448,576,704,832,960},{1,129..., dimensions={0} | all-to-all | bytes 557056 | tf_op jit(solution)/shard_map/all_to_all | solution.py:408
  35.5 0.2 shard_map.124
  35.7 2.4 %collective-permute-start.2 = (bf16[256,128]{1,0:T(8,128)(2,1)S(1)}, bf16[256,128]{1,0:T(8,128)(2,1)S(1)}, u32[]{:S(2)}, u32[]{:S(2)}) collective-permute-start(bf16[256,128]{1,0:T(8,128)(2,1)S(1)} %get-tuple-element.37), channel_id=1, source_target_pairs={{0,64},{64,0},{128,192},{192,128},{256,320},{320,256},{384,448},{4... | collective-permute-start | bytes 196616 | tf_op jit(solution)/shard_map/ppermute | solution.py:352
  38.1 0.9 collective-permute-done.2.got
  39.0 0.0 copy-start.2
  39.0 0.0 copy-start.3
  39.0 0.2 shard_map.125
  39.3 1.9 %collective-permute-start.3 = (bf16[256,256]{1,0:T(8,128)(2,1)S(1)}, bf16[256,256]{1,0:T(8,128)(2,1)S(1)}, u32[]{:S(2)}, u32[]{:S(2)}) collective-permute-start(bf16[256,256]{1,0:T(8,128)(2,1)S(1)} %get-tuple-element.44.own), channel_id=1, source_target_pairs={{0,4},{4,0},{8,12},{12,8},{16,20},{20,16},{24,28},{28,24},{32,36},... | collective-permute-start | bytes 393224 | tf_op jit(solution)/shard_map/ppermute | solution.py:352
  41.2 0.0 copy-done.2
  41.2 0.0 copy-done.3
  41.3 2.4 %collective-permute-start = (bf16[128,512]{1,0:T(8,128)(2,1)S(1)}, bf16[128,512]{1,0:T(8,128)(2,1)S(1)}, u32[]{:S(2)}, u32[]{:S(2)}) collective-permute-start(bf16[128,512]{1,0:T(8,128)(2,1)S(1)} %pad_maximum_fusion), channel_id=1, source_target_pairs={{0,64},{64,128},{128,192},{192,256},{256,320},{320,384},{384,448},... | collective-permute-start | bytes 393224 | tf_op jit(solution)/shard_map/ppermute | solution.py:348
  43.7 2.2 %collective-permute-done.3.got = bf16[256,256]{1,0:T(8,128)(2,1)S(1)} collective-permute-done((bf16[256,256]{1,0:T(8,128)(2,1)S(1)}, bf16[256,256]{1,0:T(8,128)(2,1)S(1)}, u32[]{:S(2)}, u32[]{:S(2)}) %collective-permute-start.3) | collective-permute-done | bytes 131104 | tf_op jit(solution)/shard_map/ppermute | solution.py:352
  45.9 1.9 %collective-permute-start.4 = (bf16[256,256]{1,0:T(8,128)(2,1)S(1)}, bf16[256,256]{1,0:T(8,128)(2,1)S(1)}, u32[]{:S(2)}, u32[]{:S(2)}) collective-permute-start(bf16[256,256]{1,0:T(8,128)(2,1)S(1)} %shard_map.128.own), channel_id=1, source_target_pairs={{0,8},{4,12},{8,0},{12,4},{16,24},{20,28},{24,16},{28,20},{32,40},... | collective-permute-start | bytes 393224 | tf_op jit(solution)/shard_map/ppermute | solution.py:352
  47.9 0.0 copy-start.4
  47.9 1.0 shard_map.126
  48.9 0.0 collective-permute-done.tail
  48.9 0.0 copy-done.4
  48.9 1.8 %shard_map.127._ = bf16[256,256]{1,0:T(8,128)(2,1)} custom-call(s32[1]{0:T(128)} %bitcast.place, s32[1,2]{1,0:T(1,128)} %offsets_in.1, bf16[256,256]{1,0:T(8,128)(2,1)S(1)} %bitcast.25, bf16[256,256]{1,0:T(8,128)(2,1)S(1)} %bitcast.23, bf16[256,256]{1,0:T(8,128)(2,1)S(1)} %bitcast.24, bf16[128,512]{1,0:T(8,128)(2,1)S(1)} %collective-permute-done.tail, ...), custom_call_target="tpu_custom_call" | custom-call | flops 67108864 | tf_op jit(solution)/shard_map/pallas_call | solution.py:30
  50.7 6.2 %collective-permute-done.4.got = bf16[256,256]{1,0:T(8,128)(2,1)S(1)} collective-permute-done((bf16[256,256]{1,0:T(8,128)(2,1)S(1)}, bf16[256,256]{1,0:T(8,128)(2,1)S(1)}, u32[]{:S(2)}, u32[]{:S(2)}) %collective-permute-start.4) | collective-permute-done | bytes 131104 | tf_op jit(solution)/shard_map/ppermute | solution.py:352
  56.9 0.3 shard_map.129
  57.2 2.5 %collective-permute-start.5 = (bf16[8,32,256]{2,1,0:T(8,128)(2,1)S(1)}, bf16[8,32,256]{2,1,0:T(8,128)(2,1)S(1)}, u32[]{:S(2)}, u32[]{:S(2)}) collective-permute-start(bf16[8,32,256]{2,1,0:T(8,128)(2,1)S(1)} %get-tuple-element.46), channel_id=1, source_target_pairs={{0,64},{64,0},{128,192},{192,128},{256,320},{320,256},{384,448},{4... | collective-permute-start | bytes 393224 | tf_op jit(solution)/shard_map/ppermute | solution.py:352
  59.7 1.0 collective-permute-done.5.got
  60.7 10.8 %all_to_all.21.got = bf16[8,32,256]{2,1,0:T(8,128)(2,1)S(1)} all-to-all(bf16[8,32,256]{2,1,0:T(8,128)(2,1)S(1)} %shard_map.130), channel_id=1, replica_groups={{0,128,256,384,512,640,768,896},{64,192,320,448,576,704,832,960},{1,129..., dimensions={0} | all-to-all | bytes 262144 | tf_op jit(solution)/shard_map/all_to_all | solution.py:460
  71.5 26.3 %all_to_all.22.got = bf16[16,8,256]{2,1,0:T(8,128)(2,1)S(1)} all-to-all(bf16[16,8,256]{2,1,0:T(8,128)(2,1)S(1)} %shard_map.131), channel_id=1, replica_groups={{0,1,2,3,16,17,18,19,32,33,34,35,48,49,50,51},{4,5,6,7,20,21,22,23,36,3..., dimensions={0} | all-to-all | bytes 131072 | tf_op jit(solution)/shard_map/all_to_all | solution.py:462
  97.8 13.2 %all_to_all.23.got = bf16[16,8,256]{2,1,0:T(8,128)(2,1)S(1)} all-to-all(bf16[16,8,256]{2,1,0:T(8,128)(2,1)S(1)} %shard_map.132), channel_id=1, replica_groups=mesh['tm'=16,'space'=16,'dp'=4] {'tm'}, dimensions={0} | all-to-all | bytes 131072 | tf_op jit(solution)/shard_map/all_to_all | solution.py:468
  111.0 0.7 shard_map.133
  (6 shorter events, 0.1 us)
Async XLA Ops:
  0.6 18.8 %copy-start = (bf16[1,256,256]{2,1,0:T(8,128)(2,1)S(1)}, bf16[1,256,256]{2,1,0:T(8,128)(2,1)}, u32[]{:S(2)}) copy-start(bf16[1,256,256]{2,1,0:T(8,128)(2,1)} %param.13) | copy-start | bytes 393220
  0.6 18.8 %copy-start.1 = (bf16[1,256,256]{2,1,0:T(8,128)(2,1)S(1)}, bf16[1,256,256]{2,1,0:T(8,128)(2,1)}, u32[]{:S(2)}) copy-start(bf16[1,256,256]{2,1,0:T(8,128)(2,1)} %param.18) | copy-start | bytes 393220
  3.3 17.0 %collective-permute-start.1 = (bf16[520,128]{1,0:T(8,128)(2,1)S(1)}, bf16[520,128]{1,0:T(8,128)(2,1)S(1)}, u32[]{:S(2)}, u32[]{:S(2)}) collective-permute-start(bf16[520,128]{1,0:T(8,128)(2,1)S(1)} %get-tuple-element.31), channel_id=1, source_target_pairs={{0,64},{64,0},{128,192},{192,128},{256,320},{320,256},{384,448},{4... | collective-permute-start | bytes 399368 | tf_op jit(solution)/shard_map/ppermute | solution.py:352
  35.7 3.3 %collective-permute-start.2 = (bf16[256,128]{1,0:T(8,128)(2,1)S(1)}, bf16[256,128]{1,0:T(8,128)(2,1)S(1)}, u32[]{:S(2)}, u32[]{:S(2)}) collective-permute-start(bf16[256,128]{1,0:T(8,128)(2,1)S(1)} %get-tuple-element.37), channel_id=1, source_target_pairs={{0,64},{64,0},{128,192},{192,128},{256,320},{320,256},{384,448},{4... | collective-permute-start | bytes 196616 | tf_op jit(solution)/shard_map/ppermute | solution.py:352
  39.0 2.2 %copy-start.2 = (bf16[1,256,256]{2,1,0:T(8,128)(2,1)S(1)}, bf16[1,256,256]{2,1,0:T(8,128)(2,1)}, u32[]{:S(2)}) copy-start(bf16[1,256,256]{2,1,0:T(8,128)(2,1)} %param.16) | copy-start | bytes 393220
  39.0 2.2 %copy-start.3 = (bf16[1,256,256]{2,1,0:T(8,128)(2,1)S(1)}, bf16[1,256,256]{2,1,0:T(8,128)(2,1)}, u32[]{:S(2)}) copy-start(bf16[1,256,256]{2,1,0:T(8,128)(2,1)} %param.17) | copy-start | bytes 393220
  39.3 6.6 %collective-permute-start.3 = (bf16[256,256]{1,0:T(8,128)(2,1)S(1)}, bf16[256,256]{1,0:T(8,128)(2,1)S(1)}, u32[]{:S(2)}, u32[]{:S(2)}) collective-permute-start(bf16[256,256]{1,0:T(8,128)(2,1)S(1)} %get-tuple-element.44.own), channel_id=1, source_target_pairs={{0,4},{4,0},{8,12},{12,8},{16,20},{20,16},{24,28},{28,24},{32,36},... | collective-permute-start | bytes 393224 | tf_op jit(solution)/shard_map/ppermute | solution.py:352
  41.3 7.6 %collective-permute-start = (bf16[128,512]{1,0:T(8,128)(2,1)S(1)}, bf16[128,512]{1,0:T(8,128)(2,1)S(1)}, u32[]{:S(2)}, u32[]{:S(2)}) collective-permute-start(bf16[128,512]{1,0:T(8,128)(2,1)S(1)} %pad_maximum_fusion), channel_id=1, source_target_pairs={{0,64},{64,128},{128,192},{192,256},{256,320},{320,384},{384,448},... | collective-permute-start | bytes 393224 | tf_op jit(solution)/shard_map/ppermute | solution.py:348
  45.9 11.0 %collective-permute-start.4 = (bf16[256,256]{1,0:T(8,128)(2,1)S(1)}, bf16[256,256]{1,0:T(8,128)(2,1)S(1)}, u32[]{:S(2)}, u32[]{:S(2)}) collective-permute-start(bf16[256,256]{1,0:T(8,128)(2,1)S(1)} %shard_map.128.own), channel_id=1, source_target_pairs={{0,8},{4,12},{8,0},{12,4},{16,24},{20,28},{24,16},{28,20},{32,40},... | collective-permute-start | bytes 393224 | tf_op jit(solution)/shard_map/ppermute | solution.py:352
  47.9 1.0 copy-start.4
  57.2 3.4 %collective-permute-start.5 = (bf16[8,32,256]{2,1,0:T(8,128)(2,1)S(1)}, bf16[8,32,256]{2,1,0:T(8,128)(2,1)S(1)}, u32[]{:S(2)}, u32[]{:S(2)}) collective-permute-start(bf16[8,32,256]{2,1,0:T(8,128)(2,1)S(1)} %get-tuple-element.46), channel_id=1, source_target_pairs={{0,64},{64,0},{128,192},{192,128},{256,320},{320,256},{384,448},{4... | collective-permute-start | bytes 393224 | tf_op jit(solution)/shard_map/ppermute | solution.py:352

commit v10 on v8

--- a/solution.py
+++ b/solution.py
@@ -57,7 +57,7 @@
 
 
 def pre_body(heads, share, place, lat_in, wb_in, wc_in, x_in, cot_in, ld_in, b_out, c_out, cumc_out, cumr_out,
-             fresh_out, back_out, table_out, send, mine_out, lat, w, x, cot, ld, sems):
+             fresh_out, back_out, table_out, send, mine_out, x, cot, lat, w, ld, sems):
     n = wb_in.shape[1]
     width = lat.shape[1]
     chunks = CHUNKS
@@ -331,12 +331,6 @@
         out[i] = total
 
 
-def unpack_body(got, out):
-    piece = got.shape[1]
-    for i in range(got.shape[0]):
-        out[i * piece : (i + 1) * piece, :] = got[i].astype(F32)
-
-
 def shifted(block, axis, distance):
     devices = range(lax.axis_size(axis))
     route = [(i - distance, i) for i in devices if i - distance in devices]
@@ -369,17 +363,15 @@
     ]
     state = ((cols, n), F32)
     wire = ((2 * cols + EXTRA, n), BF16)
-    b, c, cumc, cumr, fwd, bwd, table, send, mine = call(
+    b, c, cumc, cumr, fwd, bwd, table, send, mine, x, cot = call(
         functools.partial(pre_body, heads, share),
         [((rows, n), BF16), ((rows, n), BF16), ((rows, heads), F32), ((heads, rows), F32), state, state,
-         ((24, n), F32), wire, ((rows, share * far), BF16)],
+         ((24, n), F32), wire, ((rows, share * far), BF16), ((rows, cols), BF16), ((rows, cols), BF16)],
         (lax.axis_index("space")[None], *inputs),
         [SMEM] + [HBM] * 6,
         [
             pltpu.VMEM((rows, width), BF16),
             pltpu.VMEM((width, 2 * n), BF16),
-            pltpu.VMEM((rows, cols), BF16),
-            pltpu.VMEM((rows, cols), BF16),
             pltpu.VMEM((heads, rows), F32),
             pltpu.SemaphoreType.DMA((3 * CHUNKS + 3,)),
         ],
@@ -459,7 +451,7 @@
         (got,),
     )[0]
     got = lax.all_to_all(term, "tm", 0, 0)
-    proj_grad = call(unpack_body, [((share, 2 * n), F32)], (got,))[0]
+    proj_grad = got.reshape(share, 2 * n).astype(F32)
     return layer_out[None], input_grad[None], proj_grad
 
 

time: 111 us -> 111 us (level)
    pallas_call x12 -> x11, Pallas kernels: 7.81 us -> 7.12 us  [call(): pl.pallas_call(body, out_shape=[jax.ShapeDtypeStruct(s, t) for s, t in ou...]
where the time goes in v10:
time: 111 us
  blocking collectives  67.9 us (61%)
  starting transfers between devices  24.8 us (22%)
  waiting for transfers between devices  9.43 us (8%)
  Pallas kernels  7.12 us (6%)
    all_to_all x1, blocking collectives, on_device(): got = lax.all_to_all(term, ('space', 'dp'), 0, 0, axis_index_groups=across)  26.7 us
    all_to_all x2, blocking collectives, on_device(): got = lax.all_to_all(term, 'tm', 0, 0)  26.2 us
    ppermute x4, starting transfers between devices, swapped(): lax.ppermute(block, axis, [(i, i ^ distance) for i in range(lax.axis_size...  22.3 us
    all_to_all x1, blocking collectives, on_device(): got = lax.all_to_all(spread, 'tm', 0, 0, axis_index_groups=same_core)  15.1 us
    ppermute x4, waiting for transfers between devices, swapped(): lax.ppermute(block, axis, [(i, i ^ distance) for i in range(lax.axis_size...  9.43 us
    pallas_call x11, Pallas kernels, call(): pl.pallas_call(body, out_shape=[jax.ShapeDtypeStruct(s, t) for s, t in ou...  7.12 us
    ppermute x1, starting transfers between devices, shifted(): return lax.ppermute(block, axis, route)  2.43 us
  transfers between devices with their start and end apart: 5, of which 4 were waited for; matrix products, arithmetic and copies ran while one was open for 0% of the time, Pallas kernels for 3%

profile of v10, /device:TPU:1, one launch (start us, length us, event | category | flops | bytes accessed | tf_op | source)
XLA Modules:
  0.0 110.7 jit_solution(14423133938703349364)
XLA Ops:
  0.6 2.7 %shard_map.121 = (bf16[256,128]{1,0:T(8,128)(2,1)S(1)}, bf16[256,128]{1,0:T(8,128)(2,1)S(1)}, f32[256,2]{1,0:T(8,128)S(1)}, f32[2,256]{1,0:T(2,128)S(1)}, f32[25...) custom-call(s32[1]{0:T(128)} %bitcast.6.place, ...), custom_call_target="tpu_custom_call" | custom-call | flops 301989888 | tf_op jit(solution)/shard_map/pallas_call | solution.py:30
  3.3 16.1 %collective-permute-start.1 = (bf16[520,128]{1,0:T(8,128)(2,1)S(1)}, bf16[520,128]{1,0:T(8,128)(2,1)S(1)}, u32[]{:S(2)}, u32[]{:S(2)}) collective-permute-start(bf16[520,128]{1,0:T(8,128)(2,1)S(1)} %get-tuple-element.33), channel_id=1, source_target_pairs={{0,64},{64,0},{128,192},{192,128},{256,320},{320,256},{384,448},{4... | collective-permute-start | bytes 399368 | tf_op jit(solution)/shard_map/ppermute | solution.py:341
  19.4 0.8 shard_map.122
  20.2 0.2 collective-permute-done.1.got.pair
  20.3 0.1 shard_map.123
  20.4 15.1 %all_to_all.20.got = bf16[8,136,128]{2,1,0:T(8,128)(2,1)S(1)} all-to-all(bf16[8,136,128]{2,1,0:T(8,128)(2,1)S(1)} %shard_map.123), channel_id=1, replica_groups={{0,128,256,384,512,640,768,896},{64,192,320,448,576,704,832,960},{1,129..., dimensions={0} | all-to-all | bytes 557056 | tf_op jit(solution)/shard_map/all_to_all | solution.py:395
  35.5 0.2 shard_map.124
  35.6 2.4 %collective-permute-start.2 = (bf16[256,128]{1,0:T(8,128)(2,1)S(1)}, bf16[256,128]{1,0:T(8,128)(2,1)S(1)}, u32[]{:S(2)}, u32[]{:S(2)}) collective-permute-start(bf16[256,128]{1,0:T(8,128)(2,1)S(1)} %get-tuple-element.39), channel_id=1, source_target_pairs={{0,64},{64,0},{128,192},{192,128},{256,320},{320,256},{384,448},{4... | collective-permute-start | bytes 196616 | tf_op jit(solution)/shard_map/ppermute | solution.py:341
  38.1 0.9 collective-permute-done.2.got
  39.0 0.0 copy-start
  39.0 0.0 copy-start.1
  39.0 0.2 shard_map.125
  39.2 1.9 %collective-permute-start.3 = (bf16[256,256]{1,0:T(8,128)(2,1)S(1)}, bf16[256,256]{1,0:T(8,128)(2,1)S(1)}, u32[]{:S(2)}, u32[]{:S(2)}) collective-permute-start(bf16[256,256]{1,0:T(8,128)(2,1)S(1)} %get-tuple-element.46.own), channel_id=1, source_target_pairs={{0,4},{4,0},{8,12},{12,8},{16,20},{20,16},{24,28},{28,24},{32,36},... | collective-permute-start | bytes 393224 | tf_op jit(solution)/shard_map/ppermute | solution.py:341
  41.2 0.0 copy-done
  41.2 0.0 copy-done.1
  41.2 2.4 %collective-permute-start = (bf16[128,512]{1,0:T(8,128)(2,1)S(1)}, bf16[128,512]{1,0:T(8,128)(2,1)S(1)}, u32[]{:S(2)}, u32[]{:S(2)}) collective-permute-start(bf16[128,512]{1,0:T(8,128)(2,1)S(1)} %pad_maximum_fusion), channel_id=1, source_target_pairs={{0,64},{64,128},{128,192},{192,256},{256,320},{320,384},{384,448},... | collective-permute-start | bytes 393224 | tf_op jit(solution)/shard_map/ppermute | solution.py:337
  43.7 2.2 %collective-permute-done.3.got = bf16[256,256]{1,0:T(8,128)(2,1)S(1)} collective-permute-done((bf16[256,256]{1,0:T(8,128)(2,1)S(1)}, bf16[256,256]{1,0:T(8,128)(2,1)S(1)}, u32[]{:S(2)}, u32[]{:S(2)}) %collective-permute-start.3) | collective-permute-done | bytes 131104 | tf_op jit(solution)/shard_map/ppermute | solution.py:341
  45.9 1.9 %collective-permute-start.4 = (bf16[256,256]{1,0:T(8,128)(2,1)S(1)}, bf16[256,256]{1,0:T(8,128)(2,1)S(1)}, u32[]{:S(2)}, u32[]{:S(2)}) collective-permute-start(bf16[256,256]{1,0:T(8,128)(2,1)S(1)} %shard_map.128.own), channel_id=1, source_target_pairs={{0,8},{4,12},{8,0},{12,4},{16,24},{20,28},{24,16},{28,20},{32,40},... | collective-permute-start | bytes 393224 | tf_op jit(solution)/shard_map/ppermute | solution.py:341
  47.8 0.0 copy-start.2
  47.8 1.0 shard_map.126
  48.8 0.0 collective-permute-done.tail
  48.8 0.0 copy-done.2
  48.9 1.8 %shard_map.127._ = bf16[256,256]{1,0:T(8,128)(2,1)} custom-call(s32[1]{0:T(128)} %bitcast.place, s32[1,2]{1,0:T(1,128)} %offsets_in.1, bf16[256,256]{1,0:T(8,128)(2,1)S(1)} %bitcast.22, bf16[256,256]{1,0:T(8,128)(2,1)S(1)} %bitcast.20, bf16[256,256]{1,0:T(8,128)(2,1)S(1)} %bitcast.21, bf16[128,512]{1,0:T(8,128)(2,1)S(1)} %collective-permute-done.tail, ...), custom_call_target="tpu_custom_call" | custom-call | flops 67108864 | tf_op jit(solution)/shard_map/pallas_call | solution.py:30
  50.7 6.2 %collective-permute-done.4.got = bf16[256,256]{1,0:T(8,128)(2,1)S(1)} collective-permute-done((bf16[256,256]{1,0:T(8,128)(2,1)S(1)}, bf16[256,256]{1,0:T(8,128)(2,1)S(1)}, u32[]{:S(2)}, u32[]{:S(2)}) %collective-permute-start.4) | collective-permute-done | bytes 131104 | tf_op jit(solution)/shard_map/ppermute | solution.py:341
  56.9 0.3 shard_map.129
  57.1 14.8 %all_to_all.21.got = bf16[16,32,256]{2,1,0:T(8,128)(2,1)S(1)} all-to-all(bf16[16,32,256]{2,1,0:T(8,128)(2,1)S(1)} %shard_map.129), channel_id=1, replica_groups=mesh['tm'=16,'space'=16,'dp'=4] {'tm'}, dimensions={0} | all-to-all | bytes 524288 | tf_op jit(solution)/shard_map/all_to_all | solution.py:445
  72.0 26.7 %all_to_all.22.got = bf16[16,8,256]{2,1,0:T(8,128)(2,1)S(1)} all-to-all(bf16[16,8,256]{2,1,0:T(8,128)(2,1)S(1)} %shard_map.130), channel_id=1, replica_groups={{0,1,2,3,16,17,18,19,32,33,34,35,48,49,50,51},{4,5,6,7,20,21,22,23,36,3..., dimensions={0} | all-to-all | bytes 131072 | tf_op jit(solution)/shard_map/all_to_all | solution.py:447
  98.7 11.4 %all_to_all.23 = bf16[16,8,256]{2,1,0:T(8,128)(2,1)S(1)} all-to-all(bf16[16,8,256]{2,1,0:T(8,128)(2,1)S(1)} %shard_map.131), channel_id=1, replica_groups=mesh['tm'=16,'space'=16,'dp'=4] {'tm'}, dimensions={0} | all-to-all | bytes 131072 | tf_op jit(solution)/shard_map/all_to_all | solution.py:453
  110.1 0.7 bitcast_convert_fusion
  (5 shorter events, 0.1 us)
Async XLA Ops:
  3.3 17.0 %collective-permute-start.1 = (bf16[520,128]{1,0:T(8,128)(2,1)S(1)}, bf16[520,128]{1,0:T(8,128)(2,1)S(1)}, u32[]{:S(2)}, u32[]{:S(2)}) collective-permute-start(bf16[520,128]{1,0:T(8,128)(2,1)S(1)} %get-tuple-element.33), channel_id=1, source_target_pairs={{0,64},{64,0},{128,192},{192,128},{256,320},{320,256},{384,448},{4... | collective-permute-start | bytes 399368 | tf_op jit(solution)/shard_map/ppermute | solution.py:341
  35.6 3.3 %collective-permute-start.2 = (bf16[256,128]{1,0:T(8,128)(2,1)S(1)}, bf16[256,128]{1,0:T(8,128)(2,1)S(1)}, u32[]{:S(2)}, u32[]{:S(2)}) collective-permute-start(bf16[256,128]{1,0:T(8,128)(2,1)S(1)} %get-tuple-element.39), channel_id=1, source_target_pairs={{0,64},{64,0},{128,192},{192,128},{256,320},{320,256},{384,448},{4... | collective-permute-start | bytes 196616 | tf_op jit(solution)/shard_map/ppermute | solution.py:341
  39.0 2.2 %copy-start = (bf16[1,256,256]{2,1,0:T(8,128)(2,1)S(1)}, bf16[1,256,256]{2,1,0:T(8,128)(2,1)}, u32[]{:S(2)}) copy-start(bf16[1,256,256]{2,1,0:T(8,128)(2,1)} %param.16) | copy-start | bytes 393220
  39.0 2.2 %copy-start.1 = (bf16[1,256,256]{2,1,0:T(8,128)(2,1)S(1)}, bf16[1,256,256]{2,1,0:T(8,128)(2,1)}, u32[]{:S(2)}) copy-start(bf16[1,256,256]{2,1,0:T(8,128)(2,1)} %param.17) | copy-start | bytes 393220
  39.2 6.6 %collective-permute-start.3 = (bf16[256,256]{1,0:T(8,128)(2,1)S(1)}, bf16[256,256]{1,0:T(8,128)(2,1)S(1)}, u32[]{:S(2)}, u32[]{:S(2)}) collective-permute-start(bf16[256,256]{1,0:T(8,128)(2,1)S(1)} %get-tuple-element.46.own), channel_id=1, source_target_pairs={{0,4},{4,0},{8,12},{12,8},{16,20},{20,16},{24,28},{28,24},{32,36},... | collective-permute-start | bytes 393224 | tf_op jit(solution)/shard_map/ppermute | solution.py:341
  41.2 7.6 %collective-permute-start = (bf16[128,512]{1,0:T(8,128)(2,1)S(1)}, bf16[128,512]{1,0:T(8,128)(2,1)S(1)}, u32[]{:S(2)}, u32[]{:S(2)}) collective-permute-start(bf16[128,512]{1,0:T(8,128)(2,1)S(1)} %pad_maximum_fusion), channel_id=1, source_target_pairs={{0,64},{64,128},{128,192},{192,256},{256,320},{320,384},{384,448},... | collective-permute-start | bytes 393224 | tf_op jit(solution)/shard_map/ppermute | solution.py:337
  45.9 11.0 %collective-permute-start.4 = (bf16[256,256]{1,0:T(8,128)(2,1)S(1)}, bf16[256,256]{1,0:T(8,128)(2,1)S(1)}, u32[]{:S(2)}, u32[]{:S(2)}) collective-permute-start(bf16[256,256]{1,0:T(8,128)(2,1)S(1)} %shard_map.128.own), channel_id=1, source_target_pairs={{0,8},{4,12},{8,0},{12,4},{16,24},{20,28},{24,16},{28,20},{32,40},... | collective-permute-start | bytes 393224 | tf_op jit(solution)/shard_map/ppermute | solution.py:341
  47.8 1.0 copy-start.2
